TPU v7x, 512 devices: a whole 4x4x16 slice. The times are simulated.
512 devices in a mesh: lon: 128 (over y, x_lo, z), lat: 4 (over x_hi, core).
Axes of the slice: x: 4 (x_hi: 2, x_lo: 2; x = x_hi * 2 + x_lo), y: 4, z: 16, core: 2. Of those that a mesh axis runs over, the one named last changes fastest.
Arguments:
- fields: float32 [64, 2560, 6, 128], P('lat', 'lon'), may hold values from -6 to 6
- day_mask: int32 [2, 64, 2560], P(None, 'lat', 'lon'), may hold values from 0 to 1, as said below
- w_in: bfloat16 [2, 1024, 768], P(None, 'lon'), may hold values from -0.21875 to 0.21875
- w_mid: bfloat16 [2, 1024, 1024], P(None, 'lon'), may hold values from -0.1875 to 0.1875
- w_out: bfloat16 [2, 1024, 768], P(None, 'lon'), may hold values from -0.1875 to 0.1875
Outputs:
- final_fields: float32 [64, 2560, 6, 128], P('lat', 'lon')
Inputs may be any that keep to these rules, and one draw needn't show every extreme that they name: day_mask is equal on latitude rows 2 j and 2 j + 1; at longitude index b + 1280 it equals 1 minus its value at longitude b.
All inputs are finite; a program needn't handle non-finite values.
Results may differ from a plain program's by a relative error of at most 0.0075.
Values may be sent and summed in bfloat16 or wider, within the bound.
No kernel may reach another device: no remote copies, remote signals or barrier semaphores. Data moves between devices by JAX's collectives and lax.ppermute only.
A program may use at most 128 MiB of HBM per device.

v0:
```python
import jax
import jax.numpy as jnp
from jax import lax
from jax.sharding import PartitionSpec as P

STEPS = 2


COURANT = 0.25
DIFFUSE = 0.1
EPSILON = 1e-06


def with_halo(cells, sides, width, closed):
    for axis, dim in sides:
        count = lax.axis_size(axis)
        ends = count if closed else count - 1
        head = lax.slice_in_dim(cells, 0, width, axis=dim)
        tail = lax.slice_in_dim(cells, cells.shape[dim] - width, cells.shape[dim], axis=dim)
        cells = jnp.concatenate(
            [
                lax.ppermute(tail, axis, [(i, (i + 1) % count) for i in range(ends)]),
                cells,
                lax.ppermute(head, axis, [((i + 1) % count, i) for i in range(ends)]),
            ],
            axis=dim,
        )
    return cells


def sent_together(arrays, axis, dim, along):
    ends, at = ([], 0)
    for a in arrays[:-1]:
        at += a.shape[along]
        ends.append(at)
    both = jnp.concatenate(arrays, axis=along)
    return tuple(jnp.split(lax.all_gather(both, axis, axis=dim, tiled=True), ends, axis=along))


def transport(fields_now):
    lon_padded = with_halo(fields_now.astype(jnp.bfloat16), (("lon", 1),), 1, True).astype(
        fields_now.dtype
    )
    lat_padded = with_halo(fields_now.astype(jnp.bfloat16), (("lat", 0),), 1, False).astype(
        fields_now.dtype
    )
    east_side = lon_padded[:, 2:]
    west_side = lon_padded[:, :-2]
    north_side = lat_padded[2:]
    south_side = lat_padded[:-2]
    wind_east = fields_now[:, :, 0:1]
    wind_north = fields_now[:, :, 1:2]
    advected = wind_east * (east_side - west_side) + wind_north * (north_side - south_side)
    smoothed = east_side + west_side + north_side + south_side - 4.0 * fields_now
    return fields_now - COURANT * advected + DIFFUSE * smoothed


def normalize(columns):
    mean_square = jnp.mean(columns * columns, axis=-1, keepdims=True)
    return (columns * lax.rsqrt(mean_square + EPSILON)).astype(jnp.bfloat16)


def network(inputs, first_layer, middle_layer, last_layer):
    before = lax.dot_general(
        inputs, first_layer, (((1,), (1,)), ((), ())), preferred_element_type=jnp.float32
    )
    first = jax.nn.silu(before).astype(jnp.bfloat16)
    second = jax.nn.silu(jnp.dot(first, middle_layer, preferred_element_type=jnp.float32)).astype(
        jnp.bfloat16
    )
    return jnp.dot(second, last_layer, preferred_element_type=jnp.float32)


def shards(fields, day_mask, w_in, w_mid, w_out):
    gathered = sent_together((w_in, w_mid, w_out), "lon", 1, 2)
    layer_first, layer_middle, layer_last = gathered

    def apply_net(inputs, which):
        return network(inputs, layer_first[which], layer_middle[which], layer_last[which])

    lat_rows = fields.shape[0]
    lon_cols = fields.shape[1]
    column_width = fields.shape[2] * fields.shape[3]
    fields_now = fields
    for step_index in range(STEPS):
        moved = transport(fields_now)
        inputs = normalize(moved.reshape(lat_rows, lon_cols, column_width))
        sunlit = day_mask[step_index] == 1
        flat_inputs = inputs.reshape(lat_rows * lon_cols, column_width)
        day_output = apply_net(flat_inputs, 0)
        night_output = apply_net(flat_inputs, 1)
        tendency = jnp.where(sunlit.reshape(-1, 1), day_output, night_output)
        fields_now = moved + tendency.reshape(moved.shape)
    return fields_now


def solution(mesh):
    in_specs = (
        P("lat", "lon", None, None),
        P(None, "lat", "lon"),
        P(None, "lon", None),
        P(None, "lon", None),
        P(None, "lon", None),
    )
    out_specs = P("lat", "lon", None, None)
    return jax.shard_map(shards, mesh=mesh, in_specs=in_specs, out_specs=out_specs, check_vma=False)
```

profile of v0, /device:TPU:1, one launch (start us, length us, event | category | flops | bytes accessed | tf_op | source)
XLA Modules:
  0.0 680.2 jit_solution(8691543623730091749)
XLA Ops:
  6.5 0.0 all-gather.2.cloned.1.call-start
  6.5 1.5 pad_maximum_fusion
  8.0 0.0 all-gather.2.cloned.1.call-update
  8.1 0.0 copy-start.1
  8.1 1.5 copy.61
  9.6 4.4 collective-permute-start
  14.0 12.9 %collective-permute-start.1 = (bf16[16,1,6,128]{3,2,1,0:T(8,128)(2,1)S(1)}, bf16[16,1,6,128]{3,2,1,0:T(8,128)(2,1)S(1)}, u32[]{:S(2)}, u32[]{:S(2)}) collective-permute-start(bf16[16,1,6,128]{3,2,1,0:T(8,128)(2,1)S(1)} %get-tuple-element.20), channel_id=1, source_target_pairs={{4,0},{8,4},{12,8},{16,12},{20,16},{24,20},{28,24},{32,28},{36,32}... | collective-permute-start | bytes 73736 | tf_op jit(solution)/shard_map/ppermute | solution.py:24
  26.9 5.2 collective-permute-start.2
  32.1 1.9 collective-permute-start.3
  34.1 0.1 eq.23
  34.2 0.1 eq.21
  34.3 0.1 copy.14
  34.4 0.1 copy.16
  34.4 0.0 collective-permute-done
  34.4 0.0 collective-permute-done.1
  34.5 0.2 maximum_convert_fusion.2
  34.7 0.0 collective-permute-done.2
  34.7 4.8 collective-permute-done.3
  39.5 0.2 maximum_convert_fusion
  39.8 1.4 multiply_reduce_fusion.1
  41.2 0.4 multiply_convert_fusion.9
  41.6 487.3 %all-gather.2.cloned.1.call-done = bf16[2,1024,2560]{2,1,0:T(8,128)(2,1)} async-done(((bf16[2,8,2560]{2,1,0:T(8,128)(2,1)}), bf16[2,1024,2560]{2,1,0:T(8,128)(2,1)}) %all-gather.2.cloned.1.call-update) | async-done | bytes 10485776 | tf_op jit(solution)/shard_map/all_gather | solution.py:37
  528.9 3.6 multiply_convert_fusion.5
  532.5 3.6 multiply_convert_fusion.7
  536.1 2.1 fusion.7
  538.2 3.0 fusion.12
  541.3 1.4 reshape.72
  542.6 0.2 fusion.41
  542.9 1.9 collective-permute-start.4
  544.9 7.6 %collective-permute-start.5 = (bf16[16,1,6,128]{3,2,1,0:T(8,128)(2,1)S(1)}, bf16[16,1,6,128]{3,2,1,0:T(8,128)(2,1)S(1)}, u32[]{:S(2)}, u32[]{:S(2)}) collective-permute-start(bf16[16,1,6,128]{3,2,1,0:T(8,128)(2,1)S(1)} %get-tuple-element.16), channel_id=1, source_target_pairs={{4,0},{8,4},{12,8},{16,12},{20,16},{24,20},{28,24},{32,28},{36,32}... | collective-permute-start | bytes 73736 | tf_op jit(solution)/shard_map/ppermute | solution.py:24
  552.4 96.7 %collective-permute-start.6 = (bf16[1,20,6,128]{3,2,1,0:T(8,128)(2,1)S(1)}, bf16[1,20,6,128]{3,2,1,0:T(8,128)(2,1)S(1)}, u32[]{:S(2)}, u32[]{:S(2)}) collective-permute-start(bf16[1,20,6,128]{3,2,1,0:T(8,128)(2,1)S(1)} %get-tuple-element.17), channel_id=1, source_target_pairs={{0,1},{1,2},{2,3},{4,5},{5,6},{6,7},{8,9},{9,10},{10,11},{12,13},{... | collective-permute-start | bytes 92168 | tf_op jit(solution)/shard_map/ppermute | solution.py:22
  649.2 2.1 collective-permute-start.7
  651.3 0.3 fusion.43
  651.6 0.0 collective-permute-done.4
  651.6 0.0 collective-permute-done.5
  651.6 0.2 maximum_convert_fusion.3
  651.8 0.0 collective-permute-done.6
  651.8 4.2 collective-permute-done.7
  656.0 0.2 maximum_convert_fusion.1
  656.2 1.3 multiply_reduce_fusion
  657.5 0.4 multiply_convert_fusion.4
  657.9 3.6 multiply_convert_fusion
  661.6 3.6 multiply_convert_fusion.2
  665.2 2.1 fusion.6
  667.3 3.0 fusion.13
  670.3 1.4 reshape.73
  671.7 0.2 add.98
  671.9 1.5 copy.23
  (12 shorter events, 0.1 us)
Async XLA Ops:
  6.5 27.5 %copy-start = (f32[16,20,6,128]{3,0,2,1:T(8,128)S(1)}, f32[16,20,6,128]{3,0,2,1:T(8,128)}, u32[]{:S(2)}) copy-start(f32[16,20,6,128]{3,0,2,1:T(8,128)} %param.5) | copy-start | bytes 2949124
  6.5 522.4 %all-gather.2.cloned.1.call-start = ((), (), s32[]{:S(2)}) async-start(), calls=%async_computation | async-start | bytes 10567680 | tf_op jit(solution)/shard_map/all_gather | solution.py:37
  8.1 26.0 %copy-start.1 = (s32[2,16,20]{2,1,0:T(8,128)S(1)}, s32[2,16,20]{2,1,0:T(8,128)}, u32[]{:S(2)}) copy-start(s32[2,16,20]{2,1,0:T(8,128)} %param.6) | copy-start | bytes 7684
  9.6 24.8 %collective-permute-start = (bf16[16,1,6,128]{3,2,1,0:T(8,128)(2,1)S(1)}, bf16[16,1,6,128]{3,2,1,0:T(8,128)(2,1)S(1)}, u32[]{:S(2)}, u32[]{:S(2)}) collective-permute-start(bf16[16,1,6,128]{3,2,1,0:T(8,128)(2,1)S(1)} %get-tuple-element.19), channel_id=1, source_target_pairs={{0,4},{4,8},{8,12},{12,16},{16,20},{20,24},{24,28},{28,32},{32,36}... | collective-permute-start | bytes 73736 | tf_op jit(solution)/shard_map/ppermute | solution.py:22
  14.0 20.4 %collective-permute-start.1 = (bf16[16,1,6,128]{3,2,1,0:T(8,128)(2,1)S(1)}, bf16[16,1,6,128]{3,2,1,0:T(8,128)(2,1)S(1)}, u32[]{:S(2)}, u32[]{:S(2)}) collective-permute-start(bf16[16,1,6,128]{3,2,1,0:T(8,128)(2,1)S(1)} %get-tuple-element.20), channel_id=1, source_target_pairs={{4,0},{8,4},{12,8},{16,12},{20,16},{24,20},{28,24},{32,28},{36,32}... | collective-permute-start | bytes 73736 | tf_op jit(solution)/shard_map/ppermute | solution.py:24
  26.9 7.8 %collective-permute-start.2 = (bf16[1,20,6,128]{3,2,1,0:T(8,128)(2,1)S(1)}, bf16[1,20,6,128]{3,2,1,0:T(8,128)(2,1)S(1)}, u32[]{:S(2)}, u32[]{:S(2)}) collective-permute-start(bf16[1,20,6,128]{3,2,1,0:T(8,128)(2,1)S(1)} %get-tuple-element.21), channel_id=1, source_target_pairs={{0,1},{1,2},{2,3},{4,5},{5,6},{6,7},{8,9},{9,10},{10,11},{12,13},{... | collective-permute-start | bytes 92168 | tf_op jit(solution)/shard_map/ppermute | solution.py:22
  32.1 7.4 %collective-permute-start.3 = (bf16[1,20,6,128]{3,2,1,0:T(8,128)(2,1)S(1)}, bf16[1,20,6,128]{3,2,1,0:T(8,128)(2,1)S(1)}, u32[]{:S(2)}, u32[]{:S(2)}) collective-permute-start(bf16[1,20,6,128]{3,2,1,0:T(8,128)(2,1)S(1)} %get-tuple-element.22), channel_id=1, source_target_pairs={{1,0},{2,1},{3,2},{5,4},{6,5},{7,6},{9,8},{10,9},{11,10},{13,12},{... | collective-permute-start | bytes 92168 | tf_op jit(solution)/shard_map/ppermute | solution.py:24
  542.9 108.7 %collective-permute-start.4 = (bf16[16,1,6,128]{3,2,1,0:T(8,128)(2,1)S(1)}, bf16[16,1,6,128]{3,2,1,0:T(8,128)(2,1)S(1)}, u32[]{:S(2)}, u32[]{:S(2)}) collective-permute-start(bf16[16,1,6,128]{3,2,1,0:T(8,128)(2,1)S(1)} %get-tuple-element.15), channel_id=1, source_target_pairs={{0,4},{4,8},{8,12},{12,16},{16,20},{20,24},{24,28},{28,32},{32,36}... | collective-permute-start | bytes 73736 | tf_op jit(solution)/shard_map/ppermute | solution.py:22
  544.9 106.7 %collective-permute-start.5 = (bf16[16,1,6,128]{3,2,1,0:T(8,128)(2,1)S(1)}, bf16[16,1,6,128]{3,2,1,0:T(8,128)(2,1)S(1)}, u32[]{:S(2)}, u32[]{:S(2)}) collective-permute-start(bf16[16,1,6,128]{3,2,1,0:T(8,128)(2,1)S(1)} %get-tuple-element.16), channel_id=1, source_target_pairs={{4,0},{8,4},{12,8},{16,12},{20,16},{24,20},{28,24},{32,28},{36,32}... | collective-permute-start | bytes 73736 | tf_op jit(solution)/shard_map/ppermute | solution.py:24
  552.4 99.4 %collective-permute-start.6 = (bf16[1,20,6,128]{3,2,1,0:T(8,128)(2,1)S(1)}, bf16[1,20,6,128]{3,2,1,0:T(8,128)(2,1)S(1)}, u32[]{:S(2)}, u32[]{:S(2)}) collective-permute-start(bf16[1,20,6,128]{3,2,1,0:T(8,128)(2,1)S(1)} %get-tuple-element.17), channel_id=1, source_target_pairs={{0,1},{1,2},{2,3},{4,5},{5,6},{6,7},{8,9},{9,10},{10,11},{12,13},{... | collective-permute-start | bytes 92168 | tf_op jit(solution)/shard_map/ppermute | solution.py:22
  649.2 6.8 %collective-permute-start.7 = (bf16[1,20,6,128]{3,2,1,0:T(8,128)(2,1)S(1)}, bf16[1,20,6,128]{3,2,1,0:T(8,128)(2,1)S(1)}, u32[]{:S(2)}, u32[]{:S(2)}) collective-permute-start(bf16[1,20,6,128]{3,2,1,0:T(8,128)(2,1)S(1)} %get-tuple-element.18), channel_id=1, source_target_pairs={{1,0},{2,1},{3,2},{5,4},{6,5},{7,6},{9,8},{10,9},{11,10},{13,12},{... | collective-permute-start | bytes 92168 | tf_op jit(solution)/shard_map/ppermute | solution.py:24
Sparse Core Ops, SparseCore 0:
  9.4 519.4 all-gather.1
where the time goes:
time: 681 us; the launch traced here: 680 us
  waiting for transfers between devices  496 us (73%)
  starting transfers between devices  133 us (20%)
  matrix products  24.7 us (4%)
  between operations  13.7 us (2%)
    all_gather x1, waiting for transfers between devices, sent_together(): lax.all_gather(both, axis, axis=dim, tiled=True)  487 us
    ppermute x4, starting transfers between devices, with_halo(): lax.ppermute(tail, axis, [(i, (i + 1) % count) for i in range(ends)])  108 us
    ppermute x4, starting transfers between devices, with_halo(): lax.ppermute(head, axis, [((i + 1) % count, i) for i in range(ends)])  24.5 us
    dot_general x4, matrix products, network(): jnp.dot(first, middle_layer, preferred_element_type=jnp.float32)  14.4 us
  transfers between devices with their start and end apart: 9, of which 3 were waited for; matrix products, arithmetic and copies ran while one was open for 1% of the time, Pallas kernels for 0%

commit v1 on v0

v1 whole, which is shorter than its diff:
```python
import functools

import jax
import jax.numpy as jnp
from jax import lax
from jax.experimental import pallas as pl
from jax.experimental.pallas import tpu as pltpu
from jax.sharding import Mesh
from jax.sharding import PartitionSpec as P

COURANT = 0.25
DIFFUSE = 0.1
EPSILON = 1e-06
AXES = ("y", "xl", "z", "xh", "core")
LON = ("y", "xl", "z")
LAT = ("xh", "core")
F, L = 6, 128
C, R = 20, 16
WIDE = C + 2
MAIN = WIDE * R
ROWS = MAIN + 2 * C + 8
IN = F * L
HID = 1024
HALF = 1280
TILE = 256


def ring_partner(i, kind):
    if kind == 0:
        return i ^ 1
    return (i + 1) % 4 if i % 2 else (i - 1) % 4


def x_exchange(a, rnd):
    pairs = []
    for x in range(4):
        for c in range(2):
            p = ring_partner(x, c if rnd == 0 else 1 - c)
            pairs.append(((x % 2) * 4 + (x // 2) * 2 + c, (p % 2) * 4 + (p // 2) * 2 + c))
    return lax.ppermute(a, ("xl", "xh", "core"), pairs)


def y_exchange(a, rnd):
    pairs = []
    for y in range(4):
        for c in range(2):
            p = ring_partner(y, c if rnd == 0 else 1 - c)
            pairs.append((y * 2 + c, p * 2 + c))
    return lax.ppermute(a, ("y", "core"), pairs)


def core_swap(a):
    return lax.ppermute(a, "core", [(0, 1), (1, 0)])


def gather_weights(block):
    z = lax.all_gather(block, "z", axis=0)
    a, b = z[:8], z[8:]
    a1, b1 = x_exchange(a, 0), y_exchange(b, 0)
    a2, b2 = jnp.stack([a, a1]), jnp.stack([b, b1])
    a3, b3 = x_exchange(a2, 1), y_exchange(b2, 1)
    a4, b4 = jnp.concatenate([a2, a3]), jnp.concatenate([b2, b3])
    a5, b5 = y_exchange(a4, 0), x_exchange(b4, 0)
    a6, b6 = jnp.stack([a4, a5]), jnp.stack([b4, b5])
    a7, b7 = y_exchange(a6, 1), x_exchange(b6, 1)
    ca6, cb6 = core_swap(a6), core_swap(b6)
    ca7, cb7 = core_swap(a7), core_swap(b7)
    return [p.reshape(8 * 64, HALF) for p in (a6, a7, b6, b7, ca6, ca7, cb6, cb7)]


def moved_of(cen, east, west, u, v):
    north = pltpu.roll(cen, cen.shape[0] - 1, 0)
    south = pltpu.roll(cen, 1, 0)
    advected = u * (east - west) + v * (north - south)
    smoothed = east + west + north + south - 4.0 * cen
    return cen - COURANT * advected + DIFFUSE * smoothed


def column_moved(ext, c):
    cen = [ext[c, f] for f in range(F)]
    return [moved_of(cen[f], ext[c + 1, f], ext[c - 1, f], cen[0], cen[1]) for f in range(F)]


def rs_of(parts):
    ss = parts[0] * parts[0]
    for p in parts[1:]:
        ss = ss + p * p
    return lax.rsqrt(jnp.sum(ss, axis=-1, keepdims=True) * (1.0 / IN) + EPSILON)


def lanes(f):
    return slice(f * L, (f + 1) * L)


def prepare_kernel(ft, mask, lon_w, lon_e, lat_s, lat_n, moved, normed, mk, ext, edge):
    moved[MAIN:, :] = jnp.zeros((ROWS - MAIN, IN), jnp.float32)
    mk[MAIN:, :] = jnp.zeros((ROWS - MAIN, L), jnp.float32)

    def own(c, carry):
        for f in range(F):
            ext[c + 2, f, 8 : 8 + R, :] = ft[c, f]
        row = pl.multiple_of((c + 1) * R, R)
        mk[pl.ds(row, R), :] = mask[c]
        return carry

    lax.fori_loop(0, C, own, 0)
    for c in range(2):
        for f in range(F):
            ext[c, f, 8 : 8 + R, :] = lon_w[c, f].astype(jnp.float32)
            ext[C + 2 + c, f, 8 : 8 + R, :] = lon_e[c, f].astype(jnp.float32)
    mk[0:R, :] = lon_w[1, F].astype(jnp.float32)
    mk[MAIN - R : MAIN, :] = lon_e[0, F].astype(jnp.float32)

    def sides(c, carry):
        for f in range(F):
            ext[c + 1, f, 6:8, :] = lat_s[c, f].astype(jnp.float32)
            ext[c + 1, f, 8 + R : 10 + R, :] = lat_n[c, f].astype(jnp.float32)
        return carry

    lax.fori_loop(0, WIDE, sides, 0)

    def step(c, carry):
        parts = column_moved(ext, c + 1)
        rs = rs_of(parts)
        row = pl.multiple_of(c * R, R)
        for f in range(F):
            moved[pl.ds(row, R), lanes(f)] = parts[f][8 : 8 + R]
            normed[pl.ds(row, R), lanes(f)] = (parts[f] * rs)[8 : 8 + R].astype(jnp.bfloat16)

        for f in range(F):
            edge[c, f, 0:1, :] = parts[f][7:8]
            edge[c, f, 1:2, :] = parts[f][8 + R : 9 + R]
        return carry

    lax.fori_loop(0, WIDE, step, 0)
    for c in range(C):
        for k, side in enumerate((lat_s, lat_n)):
            row = MAIN + k * C + c
            for f in range(F):
                moved[row : row + 1, lanes(f)] = edge[c + 1, f, k : k + 1, :]
            mk[row : row + 1, :] = side[c + 1, F].astype(jnp.float32)[1 - k : 2 - k]
    tail = [moved[MAIN:, lanes(f)] for f in range(F)]
    rs = rs_of(tail)
    for f in range(F):
        normed[MAIN:, lanes(f)] = (tail[f] * rs).astype(jnp.bfloat16)


def silu(t):
    half = 0.5 * t
    return (half + half * jnp.tanh(half)).astype(jnp.bfloat16)


def networks(x, mask_ref, weights, h1, h2, out, rows):
    def net(n, carry):
        want = (1 - n).astype(jnp.float32)
        for t in range(HID // TILE):
            w = weights[n, t * TILE : (t + 1) * TILE, 0:IN]
            d = lax.dot_general(x[...], w, (((1,), (1,)), ((), ())), preferred_element_type=jnp.float32)
            h1[0:rows, t * TILE : (t + 1) * TILE] = silu(d)
        for t in range(HID // TILE):
            w = weights[n, :, IN + t * TILE : IN + (t + 1) * TILE]
            d = jnp.dot(h1[0:rows, :], w, preferred_element_type=jnp.float32)
            h2[0:rows, t * TILE : (t + 1) * TILE] = silu(d)
        pick = mask_ref[...] == want
        pick = jnp.concatenate([pick, pick], axis=1)
        for t in range(IN // TILE):
            cols = slice(t * TILE, (t + 1) * TILE)
            w = weights[n, :, IN + HID + t * TILE : IN + HID + (t + 1) * TILE]
            d = jnp.dot(h2[0:rows, :], w, preferred_element_type=jnp.float32)
            out[0:rows, cols] = jnp.where(pick, d, out[0:rows, cols])
        return carry

    lax.fori_loop(0, 2, net, 0)


def step_kernel(table, x1, moved1, mask0, mask1, *rest):
    pieces = rest[:8]
    result = rest[8]
    weights, h1, h2, out, ext, x2, moved2, sems = rest[9:]
    core = table[16]
    copies = []
    for k in range(8):
        net = core if k < 4 else 1 - core
        colour = (k // 2) % 2
        late = (k % 2) * 2
        for p in range(2):
            for q in range(4):
                j, i = (late + p, q) if colour == 0 else (q, late + p)
                x = table[net * 8 + i]
                y = table[net * 8 + 4 + j]
                row = pl.multiple_of(y * 256 + (x % 2) * 128 + colour * 64, 64)
                col = pl.multiple_of((x // 2) * HALF, 128)
                src = pieces[k].at[pl.ds((p * 4 + q) * 64, 64), :]
                dst = weights.at[net, pl.ds(row, 64), pl.ds(col, HALF)]
                copies.append(pltpu.make_async_copy(src, dst, sems.at[len(copies)]))
    for c in copies:
        c.start()
    for c in copies:
        c.wait()

    networks(x1, mask0, weights, h1, h2, out, ROWS)

    def spread(c, carry):
        row = pl.multiple_of(c * R, R)
        for f in range(F):
            ext[c, f, 8 : 8 + R, :] = moved1[pl.ds(row, R), lanes(f)] + out[pl.ds(row, R), lanes(f)]
        return carry

    lax.fori_loop(0, WIDE, spread, 0)

    for c in range(C):
        for k, (at, flag) in enumerate(((7, 17), (8 + R, 18))):
            row = MAIN + k * C + c
            value = moved1[row : row + 1, :] + out[row : row + 1, :]
            value = jnp.where(table[flag] == 1, value, jnp.zeros_like(value))
            for f in range(F):
                ext[c + 1, f, at : at + 1, :] = value[:, lanes(f)]

    def second(c, carry):
        parts = column_moved(ext, c + 1)
        rs = rs_of(parts)
        row = pl.multiple_of(c * R, R)
        for f in range(F):
            moved2[pl.ds(row, R), lanes(f)] = parts[f][8 : 8 + R]
            x2[pl.ds(row, R), lanes(f)] = (parts[f] * rs)[8 : 8 + R].astype(jnp.bfloat16)
        return carry

    lax.fori_loop(0, C, second, 0)
    networks(x2, mask1, weights, h1, h2, out, C * R)

    def finish(c, carry):
        row = pl.multiple_of(c * R, R)
        for f in range(F):
            result[c, f] = moved2[pl.ds(row, R), lanes(f)] + out[pl.ds(row, R), lanes(f)]
        return carry

    lax.fori_loop(0, C, finish, 0)


def vmem(n):
    return [pl.BlockSpec(memory_space=pltpu.VMEM)] * n


def shards(fields, day_mask, w_in, w_mid, w_out):
    y, xl, xh, core = (lax.axis_index(a) for a in ("y", "xl", "xh", "core"))
    lat = xh * 2 + core

    joined = jnp.concatenate([w_in, w_mid, w_out], axis=2)
    block = lax.dynamic_slice(joined, (core, 0, xh * HALF), (1, 8, HALF))[0]
    pieces = gather_weights(block)

    ft = fields.transpose(1, 2, 0, 3)
    masks = jnp.broadcast_to(
        day_mask.transpose(0, 2, 1)[..., None].astype(jnp.float32), (2, C, R, L)
    )
    both = jnp.concatenate([ft.astype(jnp.bfloat16), masks[0][:, None].astype(jnp.bfloat16)], axis=1)
    lon_n = 128
    lon_w = lax.ppermute(both[C - 2 :], LON, [(i, (i + 1) % lon_n) for i in range(lon_n)])
    lon_e = lax.ppermute(both[:2], LON, [((i + 1) % lon_n, i) for i in range(lon_n)])
    wide = jnp.concatenate([lon_w[1:], both, lon_e[:1]], axis=0)
    lat_s = lax.ppermute(wide[:, :, R - 2 :], LAT, [(i, i + 1) for i in range(3)])
    lat_n = lax.ppermute(wide[:, :, :2], LAT, [(i + 1, i) for i in range(3)])

    moved1, x1, mask0 = pl.pallas_call(
        prepare_kernel,
        out_shape=(
            jax.ShapeDtypeStruct((ROWS, IN), jnp.float32),
            jax.ShapeDtypeStruct((ROWS, IN), jnp.bfloat16),
            jax.ShapeDtypeStruct((ROWS, L), jnp.float32),
        ),
        in_specs=vmem(6),
        out_specs=vmem(3),
        scratch_shapes=[
            pltpu.VMEM((C + 4, F, 32, L), jnp.float32),
            pltpu.VMEM((WIDE, F, 8, L), jnp.float32),
        ],
        compiler_params=pltpu.CompilerParams(vmem_limit_bytes=12 << 20),
        name="prepare",
    )(ft, masks[0], lon_w, lon_e, lat_s, lat_n)

    x = xh * 2 + xl

    def partners(i):
        return i ^ 1, jnp.where(i % 2 == 1, (i + 1) % 4, (i + 3) % 4)

    def order(i, net):
        p, n = partners(i)[net], partners(i)[1 - net]
        return [i, p, n, partners(n)[net]]

    entries = [*order(x, 0), *order(y, 0), *order(x, 1), *order(y, 1)]
    entries += [core, (lat > 0).astype(jnp.int32), (lat < 3).astype(jnp.int32)]
    table = jnp.stack([e.astype(jnp.int32) for e in entries])

    result = pl.pallas_call(
        step_kernel,
        out_shape=jax.ShapeDtypeStruct((C, F, R, L), jnp.float32),
        in_specs=[pl.BlockSpec(memory_space=pltpu.SMEM)]
        + vmem(4)
        + [pl.BlockSpec(memory_space=pl.ANY)] * 8,
        out_specs=pl.BlockSpec(memory_space=pltpu.VMEM),
        scratch_shapes=[
            pltpu.VMEM((2, HID, 2 * HALF), jnp.bfloat16),
            pltpu.VMEM((ROWS, HID), jnp.bfloat16),
            pltpu.VMEM((ROWS, HID), jnp.bfloat16),
            pltpu.VMEM((ROWS, IN), jnp.float32),
            pltpu.VMEM((WIDE, F, 32, L), jnp.float32),
            pltpu.VMEM((C * R, IN), jnp.bfloat16),
            pltpu.VMEM((C * R, IN), jnp.float32),
            pltpu.SemaphoreType.DMA((64,)),
        ],
        compiler_params=pltpu.CompilerParams(vmem_limit_bytes=36 << 20),
        name="steps",
    )(table, x1, moved1, mask0, masks[1].reshape(C * R, L), *pieces)
    return result.transpose(2, 0, 1, 3)


def solution(mesh):
    grid = Mesh(mesh.devices.reshape(4, 2, 16, 2, 2), AXES)
    in_specs = (
        P(LAT, LON, None, None),
        P(None, LAT, LON),
        P(None, LON, None),
        P(None, LON, None),
        P(None, LON, None),
    )
    return jax.shard_map(
        shards, mesh=grid, in_specs=in_specs, out_specs=P(LAT, LON, None, None), check_vma=False
    )
```

time: 681 us -> 158 us (0.23)
  waiting for transfers between devices: 496 us -> 27.5 us
  starting transfers between devices: 133 us -> 72.9 us
  blocking collectives: 0 us -> 30.8 us
  matrix products: 24.7 us -> 0 us
  Pallas kernels: 0 us -> 21.1 us
  between operations: 13.7 us -> 0.52 us
    all_gather x1 -> x0, waiting for transfers between devices: 487 us -> none  [sent_together(): lax.all_gather(both, axis, axis=dim, tiled=True)]
    ppermute x8 -> x16, starting transfers between devices: 133 us -> 72.9 us  [the longest x4 37.3 us: core_swap(): return lax.ppermute(a, 'core', [(0, 1), (1, 0)])]
    all_gather x0 -> x1, blocking collectives: none -> 30.8 us  [gather_weights(): z = lax.all_gather(block, 'z', axis=0)]
    dot_general x8 -> x0, matrix products: 24.7 us -> none  [the longest x4 14.4 us: network(): jnp.dot(first, middle_layer, preferred_element_type=jnp.float32)]
    pallas_call x0 -> x2, Pallas kernels: none -> 21.1 us  [the longest x1 17.9 us: shards(): pl.pallas_call(step_kernel, out_shape=jax.ShapeDtypeStruct((C, F, R, L),...]
    ppermute x8 -> x16, waiting for transfers between devices: 9.03 us -> 27.5 us  [the longest x4 8.5 us: y_exchange(): return lax.ppermute(a, ('y', 'core'), pairs)]
  transfers between devices with their start and end apart: 9 -> 16, of which waited for: 3 -> 7; matrix products, arithmetic and copies ran while one was open for 1% -> 2% of each run, Pallas kernels for 0% -> 2%
where the time goes in v1:
time: 158 us; the launch traced here: 157 us
  starting transfers between devices  72.9 us (46%)
  blocking collectives  30.8 us (19%)
  waiting for transfers between devices  27.5 us (17%)
  Pallas kernels  21.1 us (13%)
  other arithmetic  2.65 us (2%)
  local copies, waits for them, and re-layouts  2 us (1%)
    ppermute x4, starting transfers between devices, core_swap(): return lax.ppermute(a, 'core', [(0, 1), (1, 0)])  37.3 us
    all_gather x1, blocking collectives, gather_weights(): z = lax.all_gather(block, 'z', axis=0)  30.8 us
    pallas_call x1, Pallas kernels, shards(): pl.pallas_call(step_kernel, out_shape=jax.ShapeDtypeStruct((C, F, R, L),...  17.9 us
    ppermute x4, starting transfers between devices, x_exchange(): return lax.ppermute(a, ('xl', 'xh', 'core'), pairs)  13.3 us
    ppermute x4, starting transfers between devices, y_exchange(): return lax.ppermute(a, ('y', 'core'), pairs)  12.3 us
    ppermute x4, waiting for transfers between devices, y_exchange(): return lax.ppermute(a, ('y', 'core'), pairs)  8.5 us
    ppermute x1, waiting for transfers between devices, shards(): lax.ppermute(both[C - 2:], LON, [(i, (i + 1) % lon_n) for i in range(lon_...  7.2 us
    ppermute x4, waiting for transfers between devices, x_exchange(): return lax.ppermute(a, ('xl', 'xh', 'core'), pairs)  4.59 us
  transfers between devices with their start and end apart: 16, of which 7 were waited for; matrix products, arithmetic and copies ran while one was open for 2% of the time, Pallas kernels for 2%

profile of v1, /device:TPU:1, one launch (start us, length us, event | category | flops | bytes accessed | tf_op | source)
XLA Modules:
  0.0 157.5 jit_solution(1366379371951500456)
XLA Ops:
  0.0 0.7 fusion.1
  0.7 30.8 %all_gather.3 = bf16[16,8,1280]{2,1,0:T(8,128)(2,1)S(1)} all-gather(bf16[1,8,1280]{2,1,0:T(8,128)(2,1)S(1)} %fusion.1), channel_id=1, replica_groups=mesh['y'=4,'xl'=2,'z'=16,'xh'=2,'core'=2] {'z'}, dimensions={0}, use_global_device_ids=true | all-gather | bytes 348160 | tf_op jit(solution)/shard_map/all_gather | solution.py:57
  31.6 4.4 %collective-permute-start.4 = (bf16[8,8,1280]{2,1,0:T(8,128)(2,1)S(1)}, bf16[8,8,1280]{2,1,0:T(8,128)(2,1)S(1)}, u32[]{:S(2)}, u32[]{:S(2)}) collective-permute-start(bf16[8,8,1280]{2,1,0:T(8,128)(2,1)S(1)} %get-tuple-element.22), channel_id=1, source_target_pairs={{0,64},{1,67},{64,0},{65,3},{2,66},{3,65},{66,2},{67,1},{4,68},{5,... | collective-permute-start | bytes 491528 | tf_op jit(solution)/shard_map/ppermute | solution.py:40
  36.0 4.6 %collective-permute-start.8 = (bf16[8,8,1280]{2,1,0:T(8,128)(2,1)S(1)}, bf16[8,8,1280]{2,1,0:T(8,128)(2,1)S(1)}, u32[]{:S(2)}, u32[]{:S(2)}) collective-permute-start(bf16[8,8,1280]{2,1,0:T(8,128)(2,1)S(1)} %get-tuple-element.21), channel_id=1, source_target_pairs={{0,128},{1,385},{128,0},{129,257},{256,384},{257,129},{384,256},{3... | collective-permute-start | bytes 491528 | tf_op jit(solution)/shard_map/ppermute | solution.py:49
  40.6 0.0 collective-permute-done.4
  40.7 1.9 %collective-permute-start.5 = (bf16[2,8,8,1280]{3,2,1,0:T(8,128)(2,1)S(1)}, bf16[2,8,8,1280]{3,2,1,0:T(8,128)(2,1)S(1)}, u32[]{:S(2)}, u32[]{:S(2)}) collective-permute-start(bf16[2,8,8,1280]{3,2,1,0:T(8,128)(2,1)S(1)} %pad_maximum_fusion.4), channel_id=1, source_target_pairs={{0,66},{1,65},{64,2},{65,1},{2,64},{3,67},{66,0},{67,3},{4,70},{5,... | collective-permute-start | bytes 983048 | tf_op jit(solution)/shard_map/ppermute | solution.py:40
  42.6 0.7 collective-permute-done.8
  43.3 1.9 %collective-permute-start.9 = (bf16[2,8,8,1280]{3,2,1,0:T(8,128)(2,1)S(1)}, bf16[2,8,8,1280]{3,2,1,0:T(8,128)(2,1)S(1)}, u32[]{:S(2)}, u32[]{:S(2)}) collective-permute-start(bf16[2,8,8,1280]{3,2,1,0:T(8,128)(2,1)S(1)} %pad_maximum_fusion.5), channel_id=1, source_target_pairs={{0,384},{1,129},{128,256},{129,1},{256,128},{257,385},{384,0},{385... | collective-permute-start | bytes 983048 | tf_op jit(solution)/shard_map/ppermute | solution.py:49
  45.3 4.6 %collective-permute-done.5 = bf16[2,8,8,1280]{3,2,1,0:T(8,128)(2,1)S(1)} collective-permute-done((bf16[2,8,8,1280]{3,2,1,0:T(8,128)(2,1)S(1)}, bf16[2,8,8,1280]{3,2,1,0:T(8,128)(2,1)S(1)}, u32[]{:S(2)}, u32[]{:S(2)}) %collective-permute-start.5) | collective-permute-done | bytes 327712 | tf_op jit(solution)/shard_map/ppermute | solution.py:40
  49.9 0.1 fusion.4
  50.0 3.8 %collective-permute-start.6 = (bf16[4,8,8,1280]{3,2,1,0:T(8,128)(2,1)S(1)}, bf16[4,8,8,1280]{3,2,1,0:T(8,128)(2,1)S(1)}, u32[]{:S(2)}, u32[]{:S(2)}) collective-permute-start(bf16[4,8,8,1280]{3,2,1,0:T(8,128)(2,1)S(1)} %get-tuple-element.14), channel_id=1, source_target_pairs={{0,128},{1,385},{128,0},{129,257},{256,384},{257,129},{384,256},{3... | collective-permute-start | bytes 1966088 | tf_op jit(solution)/shard_map/ppermute | solution.py:49
  53.7 0.0 collective-permute-done.9
  53.7 0.1 fusion.3
  53.9 4.4 %collective-permute-start.10 = (bf16[4,8,8,1280]{3,2,1,0:T(8,128)(2,1)S(1)}, bf16[4,8,8,1280]{3,2,1,0:T(8,128)(2,1)S(1)}, u32[]{:S(2)}, u32[]{:S(2)}) collective-permute-start(bf16[4,8,8,1280]{3,2,1,0:T(8,128)(2,1)S(1)} %get-tuple-element.12), channel_id=1, source_target_pairs={{0,64},{1,67},{64,0},{65,3},{2,66},{3,65},{66,2},{67,1},{4,68},{5,... | collective-permute-start | bytes 1966088 | tf_op jit(solution)/shard_map/ppermute | solution.py:40
  58.3 7.8 %collective-permute-done.6 = bf16[4,8,8,1280]{3,2,1,0:T(8,128)(2,1)S(1)} collective-permute-done((bf16[4,8,8,1280]{3,2,1,0:T(8,128)(2,1)S(1)}, bf16[4,8,8,1280]{3,2,1,0:T(8,128)(2,1)S(1)}, u32[]{:S(2)}, u32[]{:S(2)}) %collective-permute-start.6) | collective-permute-done | bytes 655392 | tf_op jit(solution)/shard_map/ppermute | solution.py:49
  66.0 0.1 pad_maximum_fusion
  66.2 1.9 %collective-permute-start.7 = (bf16[2,4,8,8,1280]{4,3,2,1,0:T(8,128)(2,1)S(1)}, bf16[2,4,8,8,1280]{4,3,2,1,0:T(8,128)(2,1)}, u32[]{:S(2)}, u32[]{:S(2)}) collective-permute-start(bf16[2,4,8,8,1280]{4,3,2,1,0:T(8,128)(2,1)S(1)} %pad_maximum_fusion), channel_id=1, source_target_pairs={{0,384},{1,129},{128,256},{129,1},{256,128},{257,385},{384,0},{385... | collective-permute-start | bytes 3932168 | tf_op jit(solution)/shard_map/ppermute | solution.py:49
  68.1 0.0 collective-permute-done.10
  68.1 0.0 copy-start.1
  68.1 0.1 pad_maximum_fusion.1
  68.2 2.6 %collective-permute-start.11 = (bf16[2,4,8,8,1280]{4,3,2,1,0:T(8,128)(2,1)S(1)}, bf16[2,4,8,8,1280]{4,3,2,1,0:T(8,128)(2,1)}, u32[]{:S(2)}, u32[]{:S(2)}) collective-permute-start(bf16[2,4,8,8,1280]{4,3,2,1,0:T(8,128)(2,1)S(1)} %pad_maximum_fusion.1), channel_id=1, source_target_pairs={{0,66},{1,65},{64,2},{65,1},{2,64},{3,67},{66,0},{67,3},{4,70},{5,... | collective-permute-start | bytes 3932168 | tf_op jit(solution)/shard_map/ppermute | solution.py:40
  70.8 18.4 %collective-permute-start.12 = (bf16[2,4,8,8,1280]{4,3,2,1,0:T(8,128)(2,1)S(1)}, bf16[2,4,8,8,1280]{4,3,2,1,0:T(8,128)(2,1)}, u32[]{:S(2)}, u32[]{:S(2)}) collective-permute-start(bf16[2,4,8,8,1280]{4,3,2,1,0:T(8,128)(2,1)S(1)} %pad_maximum_fusion), channel_id=1, source_target_pairs={{0,1},{1,0},{2,3},{3,2},{4,5},{5,4},{6,7},{7,6},{8,9},{9,8},{10,11... | collective-permute-start | bytes 3932168 | tf_op jit(solution)/shard_map/ppermute | solution.py:53
  89.3 1.9 %collective-permute-start.14 = (bf16[2,4,8,8,1280]{4,3,2,1,0:T(8,128)(2,1)S(1)}, bf16[2,4,8,8,1280]{4,3,2,1,0:T(8,128)(2,1)}, u32[]{:S(2)}, u32[]{:S(2)}) collective-permute-start(bf16[2,4,8,8,1280]{4,3,2,1,0:T(8,128)(2,1)S(1)} %pad_maximum_fusion.1), channel_id=1, source_target_pairs={{0,1},{1,0},{2,3},{3,2},{4,5},{5,4},{6,7},{7,6},{8,9},{9,8},{10,11... | collective-permute-start | bytes 3932168 | tf_op jit(solution)/shard_map/ppermute | solution.py:53
  91.2 5.4 %collective-permute-start.13 = (bf16[2,4,8,8,1280]{4,3,2,1,0:T(8,128)(2,1)}, bf16[2,4,8,8,1280]{4,3,2,1,0:T(8,128)(2,1)}, u32[]{:S(2)}, u32[]{:S(2)}) collective-permute-start(bf16[2,4,8,8,1280]{4,3,2,1,0:T(8,128)(2,1)} %collective-permute-done.7), channel_id=1, source_target_pairs={{0,1},{1,0},{2,3},{3,2},{4,5},{5,4},{6,7},{7,6},{8,9},{9,8},{10,11... | collective-permute-start | bytes 3932168 | tf_op jit(solution)/shard_map/ppermute | solution.py:53
  96.7 11.5 %collective-permute-start.15 = (bf16[2,4,8,8,1280]{4,3,2,1,0:T(8,128)(2,1)}, bf16[2,4,8,8,1280]{4,3,2,1,0:T(8,128)(2,1)}, u32[]{:S(2)}, u32[]{:S(2)}) collective-permute-start(bf16[2,4,8,8,1280]{4,3,2,1,0:T(8,128)(2,1)} %collective-permute-done.11), channel_id=1, source_target_pairs={{0,1},{1,0},{2,3},{3,2},{4,5},{5,4},{6,7},{7,6},{8,9},{9,8},{10,11... | collective-permute-start | bytes 3932168 | tf_op jit(solution)/shard_map/ppermute | solution.py:53
  108.2 0.1 copy.12
  108.3 1.3 bitcast_convert_fusion
  109.6 0.1 broadcast_in_dim_squeeze.3
  109.7 2.4 %collective-permute-start.1 = (bf16[2,7,16,128]{3,2,1,0:T(8,128)(2,1)S(1)}, bf16[2,7,16,128]{3,2,1,0:T(8,128)(2,1)S(1)}, u32[]{:S(2)}, u32[]{:S(2)}) collective-permute-start(bf16[2,7,16,128]{3,2,1,0:T(8,128)(2,1)S(1)} %get-tuple-element.17), channel_id=1, source_target_pairs={{4,0},{8,4},{12,8},{16,12},{20,16},{24,20},{28,24},{32,28},{36,32}... | collective-permute-start | bytes 172040 | tf_op jit(solution)/shard_map/ppermute | solution.py:259
  112.1 3.0 %collective-permute-done.1.lon_e = bf16[2,7,16,128]{3,2,1,0:T(8,128)(2,1)S(1)} collective-permute-done((bf16[2,7,16,128]{3,2,1,0:T(8,128)(2,1)S(1)}, bf16[2,7,16,128]{3,2,1,0:T(8,128)(2,1)S(1)}, u32[]{:S(2)}, u32[]{:S(2)}) %collective-permute-start.1) | collective-permute-done | bytes 57376 | tf_op jit(solution)/shard_map/ppermute | solution.py:259
  115.0 1.9 %collective-permute-start = (bf16[2,7,16,128]{3,2,1,0:T(8,128)(2,1)S(1)}, bf16[2,7,16,128]{3,2,1,0:T(8,128)(2,1)S(1)}, u32[]{:S(2)}, u32[]{:S(2)}) collective-permute-start(bf16[2,7,16,128]{3,2,1,0:T(8,128)(2,1)S(1)} %get-tuple-element.18), channel_id=1, source_target_pairs={{0,4},{4,8},{8,12},{12,16},{16,20},{20,24},{24,28},{28,32},{32,36}... | collective-permute-start | bytes 172040 | tf_op jit(solution)/shard_map/ppermute | solution.py:258
  117.0 7.2 %collective-permute-done.lon_w = bf16[2,7,16,128]{3,2,1,0:T(8,128)(2,1)S(1)} collective-permute-done((bf16[2,7,16,128]{3,2,1,0:T(8,128)(2,1)S(1)}, bf16[2,7,16,128]{3,2,1,0:T(8,128)(2,1)S(1)}, u32[]{:S(2)}, u32[]{:S(2)}) %collective-permute-start) | collective-permute-done | bytes 57376 | tf_op jit(solution)/shard_map/ppermute | solution.py:258
  124.2 0.1 pad_maximum_fusion.6
  124.3 3.9 %collective-permute-start.3 = (bf16[22,7,2,128]{3,2,1,0:T(2,128)(2,1)S(1)}, bf16[22,7,2,128]{3,2,1,0:T(2,128)(2,1)S(1)}, u32[]{:S(2)}, u32[]{:S(2)}) collective-permute-start(bf16[22,7,2,128]{3,2,1,0:T(2,128)(2,1)S(1)} %get-tuple-element.15), channel_id=1, source_target_pairs={{1,0},{2,1},{3,2},{5,4},{6,5},{7,6},{9,8},{10,9},{11,10},{13,12},{... | collective-permute-start | bytes 236552 | tf_op jit(solution)/shard_map/ppermute | solution.py:262
  128.2 3.3 %collective-permute-done.3.lat_n = bf16[22,7,2,128]{3,2,1,0:T(2,128)(2,1)S(1)} collective-permute-done((bf16[22,7,2,128]{3,2,1,0:T(2,128)(2,1)S(1)}, bf16[22,7,2,128]{3,2,1,0:T(2,128)(2,1)S(1)}, u32[]{:S(2)}, u32[]{:S(2)}) %collective-permute-start.3) | collective-permute-done | bytes 78880 | tf_op jit(solution)/shard_map/ppermute | solution.py:262
  131.5 1.9 %collective-permute-start.2 = (bf16[22,7,2,128]{3,2,1,0:T(2,128)(2,1)S(1)}, bf16[22,7,2,128]{3,2,1,0:T(2,128)(2,1)S(1)}, u32[]{:S(2)}, u32[]{:S(2)}) collective-permute-start(bf16[22,7,2,128]{3,2,1,0:T(2,128)(2,1)S(1)} %get-tuple-element.16), channel_id=1, source_target_pairs={{0,1},{1,2},{2,3},{4,5},{5,6},{6,7},{8,9},{9,10},{10,11},{12,13},{... | collective-permute-start | bytes 236552 | tf_op jit(solution)/shard_map/ppermute | solution.py:261
  133.6 0.1 copy.13
  133.7 0.1 broadcast_in_dim.11
  133.8 0.1 copy.11
  133.9 0.1 stack.105.table
  134.0 0.9 collective-permute-done.2.lat_s
  134.9 0.1 broadcast_in_dim.10.mask
  135.0 0.0 copy-start
  135.0 1.2 copy-done
  136.2 3.2 %prepare.1 = (f32[400,768]{1,0:T(8,128)S(1)}, bf16[400,768]{1,0:T(8,128)(2,1)S(1)}, f32[400,128]{1,0:T(8,128)S(1)}) custom-call(f32[20,6,16,128]{3,2,1,0:T(8,128)S(1)} %bitcast.44, f32[20,16,128]{2,1,0:T(8,128)S(1)} %broadcast_in_dim.10.mask, bf16[2,7,16,128]{3,2,1,0:T(8,128)(2,1)S(1)} %collective-permute-done.lon_w, ...), custom_call_target="tpu_custom_call" | custom-call | tf_op jit(solution)/shard_map/prepare/pallas_call | solution.py:264
  139.5 0.0 collective-permute-done.14
  139.5 0.1 broadcast_in_dim.12.mask1
  139.6 17.9 %steps.1 = f32[20,6,16,128]{3,2,1,0:T(8,128)} custom-call(s32[19]{0:T(128)S(1)} %stack.105.table, bf16[400,768]{1,0:T(8,128)(2,1)S(1)} %get-tuple-element.8.x1, f32[400,768]{1,0:T(8,128)S(1)} %get-tuple-element.9.moved1, f32[400,128]{1,0:T(8,128)S(1)} %get-tuple-element.10.mask0, f32[320,128]{1,0:T(8,128)S(1)} %broadcast_in_dim.12.mask1, ...), custom_call_target="tpu_custom_call" | custom-call | tf_op jit(solution)/shard_map/steps/pallas_call | solution.py:294
  (15 shorter events, 0.2 us)
Async XLA Ops:
  31.6 9.1 %collective-permute-start.4 = (bf16[8,8,1280]{2,1,0:T(8,128)(2,1)S(1)}, bf16[8,8,1280]{2,1,0:T(8,128)(2,1)S(1)}, u32[]{:S(2)}, u32[]{:S(2)}) collective-permute-start(bf16[8,8,1280]{2,1,0:T(8,128)(2,1)S(1)} %get-tuple-element.22), channel_id=1, source_target_pairs={{0,64},{1,67},{64,0},{65,3},{2,66},{3,65},{66,2},{67,1},{4,68},{5,... | collective-permute-start | bytes 491528 | tf_op jit(solution)/shard_map/ppermute | solution.py:40
  36.0 7.3 %collective-permute-start.8 = (bf16[8,8,1280]{2,1,0:T(8,128)(2,1)S(1)}, bf16[8,8,1280]{2,1,0:T(8,128)(2,1)S(1)}, u32[]{:S(2)}, u32[]{:S(2)}) collective-permute-start(bf16[8,8,1280]{2,1,0:T(8,128)(2,1)S(1)} %get-tuple-element.21), channel_id=1, source_target_pairs={{0,128},{1,385},{128,0},{129,257},{256,384},{257,129},{384,256},{3... | collective-permute-start | bytes 491528 | tf_op jit(solution)/shard_map/ppermute | solution.py:49
  40.7 9.2 %collective-permute-start.5 = (bf16[2,8,8,1280]{3,2,1,0:T(8,128)(2,1)S(1)}, bf16[2,8,8,1280]{3,2,1,0:T(8,128)(2,1)S(1)}, u32[]{:S(2)}, u32[]{:S(2)}) collective-permute-start(bf16[2,8,8,1280]{3,2,1,0:T(8,128)(2,1)S(1)} %pad_maximum_fusion.4), channel_id=1, source_target_pairs={{0,66},{1,65},{64,2},{65,1},{2,64},{3,67},{66,0},{67,3},{4,70},{5,... | collective-permute-start | bytes 983048 | tf_op jit(solution)/shard_map/ppermute | solution.py:40
  43.3 10.4 %collective-permute-start.9 = (bf16[2,8,8,1280]{3,2,1,0:T(8,128)(2,1)S(1)}, bf16[2,8,8,1280]{3,2,1,0:T(8,128)(2,1)S(1)}, u32[]{:S(2)}, u32[]{:S(2)}) collective-permute-start(bf16[2,8,8,1280]{3,2,1,0:T(8,128)(2,1)S(1)} %pad_maximum_fusion.5), channel_id=1, source_target_pairs={{0,384},{1,129},{128,256},{129,1},{256,128},{257,385},{384,0},{385... | collective-permute-start | bytes 983048 | tf_op jit(solution)/shard_map/ppermute | solution.py:49
  50.0 16.1 %collective-permute-start.6 = (bf16[4,8,8,1280]{3,2,1,0:T(8,128)(2,1)S(1)}, bf16[4,8,8,1280]{3,2,1,0:T(8,128)(2,1)S(1)}, u32[]{:S(2)}, u32[]{:S(2)}) collective-permute-start(bf16[4,8,8,1280]{3,2,1,0:T(8,128)(2,1)S(1)} %get-tuple-element.14), channel_id=1, source_target_pairs={{0,128},{1,385},{128,0},{129,257},{256,384},{257,129},{384,256},{3... | collective-permute-start | bytes 1966088 | tf_op jit(solution)/shard_map/ppermute | solution.py:49
  53.9 14.2 %collective-permute-start.10 = (bf16[4,8,8,1280]{3,2,1,0:T(8,128)(2,1)S(1)}, bf16[4,8,8,1280]{3,2,1,0:T(8,128)(2,1)S(1)}, u32[]{:S(2)}, u32[]{:S(2)}) collective-permute-start(bf16[4,8,8,1280]{3,2,1,0:T(8,128)(2,1)S(1)} %get-tuple-element.12), channel_id=1, source_target_pairs={{0,64},{1,67},{64,0},{65,3},{2,66},{3,65},{66,2},{67,1},{4,68},{5,... | collective-permute-start | bytes 1966088 | tf_op jit(solution)/shard_map/ppermute | solution.py:40
  66.2 25.0 %collective-permute-start.7 = (bf16[2,4,8,8,1280]{4,3,2,1,0:T(8,128)(2,1)S(1)}, bf16[2,4,8,8,1280]{4,3,2,1,0:T(8,128)(2,1)}, u32[]{:S(2)}, u32[]{:S(2)}) collective-permute-start(bf16[2,4,8,8,1280]{4,3,2,1,0:T(8,128)(2,1)S(1)} %pad_maximum_fusion), channel_id=1, source_target_pairs={{0,384},{1,129},{128,256},{129,1},{256,128},{257,385},{384,0},{385... | collective-permute-start | bytes 3932168 | tf_op jit(solution)/shard_map/ppermute | solution.py:49
  68.1 40.1 %copy-start.1 = (s32[2,16,20]{2,1,0:T(8,128)S(1)}, s32[2,16,20]{2,1,0:T(8,128)}, u32[]{:S(2)}) copy-start(s32[2,16,20]{2,1,0:T(8,128)} %param.6) | copy-start | bytes 7684
  68.2 28.4 %collective-permute-start.11 = (bf16[2,4,8,8,1280]{4,3,2,1,0:T(8,128)(2,1)S(1)}, bf16[2,4,8,8,1280]{4,3,2,1,0:T(8,128)(2,1)}, u32[]{:S(2)}, u32[]{:S(2)}) collective-permute-start(bf16[2,4,8,8,1280]{4,3,2,1,0:T(8,128)(2,1)S(1)} %pad_maximum_fusion.1), channel_id=1, source_target_pairs={{0,66},{1,65},{64,2},{65,1},{2,64},{3,67},{66,0},{67,3},{4,70},{5,... | collective-permute-start | bytes 3932168 | tf_op jit(solution)/shard_map/ppermute | solution.py:40
  70.8 68.6 %collective-permute-start.12 = (bf16[2,4,8,8,1280]{4,3,2,1,0:T(8,128)(2,1)S(1)}, bf16[2,4,8,8,1280]{4,3,2,1,0:T(8,128)(2,1)}, u32[]{:S(2)}, u32[]{:S(2)}) collective-permute-start(bf16[2,4,8,8,1280]{4,3,2,1,0:T(8,128)(2,1)S(1)} %pad_maximum_fusion), channel_id=1, source_target_pairs={{0,1},{1,0},{2,3},{3,2},{4,5},{5,4},{6,7},{7,6},{8,9},{9,8},{10,11... | collective-permute-start | bytes 3932168 | tf_op jit(solution)/shard_map/ppermute | solution.py:53
  89.3 50.2 %collective-permute-start.14 = (bf16[2,4,8,8,1280]{4,3,2,1,0:T(8,128)(2,1)S(1)}, bf16[2,4,8,8,1280]{4,3,2,1,0:T(8,128)(2,1)}, u32[]{:S(2)}, u32[]{:S(2)}) collective-permute-start(bf16[2,4,8,8,1280]{4,3,2,1,0:T(8,128)(2,1)S(1)} %pad_maximum_fusion.1), channel_id=1, source_target_pairs={{0,1},{1,0},{2,3},{3,2},{4,5},{5,4},{6,7},{7,6},{8,9},{9,8},{10,11... | collective-permute-start | bytes 3932168 | tf_op jit(solution)/shard_map/ppermute | solution.py:53
  91.2 48.3 %collective-permute-start.13 = (bf16[2,4,8,8,1280]{4,3,2,1,0:T(8,128)(2,1)}, bf16[2,4,8,8,1280]{4,3,2,1,0:T(8,128)(2,1)}, u32[]{:S(2)}, u32[]{:S(2)}) collective-permute-start(bf16[2,4,8,8,1280]{4,3,2,1,0:T(8,128)(2,1)} %collective-permute-done.7), channel_id=1, source_target_pairs={{0,1},{1,0},{2,3},{3,2},{4,5},{5,4},{6,7},{7,6},{8,9},{9,8},{10,11... | collective-permute-start | bytes 3932168 | tf_op jit(solution)/shard_map/ppermute | solution.py:53
  96.7 42.8 %collective-permute-start.15 = (bf16[2,4,8,8,1280]{4,3,2,1,0:T(8,128)(2,1)}, bf16[2,4,8,8,1280]{4,3,2,1,0:T(8,128)(2,1)}, u32[]{:S(2)}, u32[]{:S(2)}) collective-permute-start(bf16[2,4,8,8,1280]{4,3,2,1,0:T(8,128)(2,1)} %collective-permute-done.11), channel_id=1, source_target_pairs={{0,1},{1,0},{2,3},{3,2},{4,5},{5,4},{6,7},{7,6},{8,9},{9,8},{10,11... | collective-permute-start | bytes 3932168 | tf_op jit(solution)/shard_map/ppermute | solution.py:53
  109.7 5.4 %collective-permute-start.1 = (bf16[2,7,16,128]{3,2,1,0:T(8,128)(2,1)S(1)}, bf16[2,7,16,128]{3,2,1,0:T(8,128)(2,1)S(1)}, u32[]{:S(2)}, u32[]{:S(2)}) collective-permute-start(bf16[2,7,16,128]{3,2,1,0:T(8,128)(2,1)S(1)} %get-tuple-element.17), channel_id=1, source_target_pairs={{4,0},{8,4},{12,8},{16,12},{20,16},{24,20},{28,24},{32,28},{36,32}... | collective-permute-start | bytes 172040 | tf_op jit(solution)/shard_map/ppermute | solution.py:259
  115.0 9.1 %collective-permute-start = (bf16[2,7,16,128]{3,2,1,0:T(8,128)(2,1)S(1)}, bf16[2,7,16,128]{3,2,1,0:T(8,128)(2,1)S(1)}, u32[]{:S(2)}, u32[]{:S(2)}) collective-permute-start(bf16[2,7,16,128]{3,2,1,0:T(8,128)(2,1)S(1)} %get-tuple-element.18), channel_id=1, source_target_pairs={{0,4},{4,8},{8,12},{12,16},{16,20},{20,24},{24,28},{28,32},{32,36}... | collective-permute-start | bytes 172040 | tf_op jit(solution)/shard_map/ppermute | solution.py:258
  124.3 7.2 %collective-permute-start.3 = (bf16[22,7,2,128]{3,2,1,0:T(2,128)(2,1)S(1)}, bf16[22,7,2,128]{3,2,1,0:T(2,128)(2,1)S(1)}, u32[]{:S(2)}, u32[]{:S(2)}) collective-permute-start(bf16[22,7,2,128]{3,2,1,0:T(2,128)(2,1)S(1)} %get-tuple-element.15), channel_id=1, source_target_pairs={{1,0},{2,1},{3,2},{5,4},{6,5},{7,6},{9,8},{10,9},{11,10},{13,12},{... | collective-permute-start | bytes 236552 | tf_op jit(solution)/shard_map/ppermute | solution.py:262
  131.5 3.4 %collective-permute-start.2 = (bf16[22,7,2,128]{3,2,1,0:T(2,128)(2,1)S(1)}, bf16[22,7,2,128]{3,2,1,0:T(2,128)(2,1)S(1)}, u32[]{:S(2)}, u32[]{:S(2)}) collective-permute-start(bf16[22,7,2,128]{3,2,1,0:T(2,128)(2,1)S(1)} %get-tuple-element.16), channel_id=1, source_target_pairs={{0,1},{1,2},{2,3},{4,5},{5,6},{6,7},{8,9},{9,10},{10,11},{12,13},{... | collective-permute-start | bytes 236552 | tf_op jit(solution)/shard_map/ppermute | solution.py:261
  135.0 1.2 copy-start

commit v2 on v1

--- a/solution.py
+++ b/solution.py
@@ -1,7 +1,6 @@
-import functools
-
 import jax
 import jax.numpy as jnp
+import numpy as np
 from jax import lax
 from jax.experimental import pallas as pl
 from jax.experimental.pallas import tpu as pltpu
@@ -150,13 +149,17 @@
     return (half + half * jnp.tanh(half)).astype(jnp.bfloat16)
 
 
-def networks(x, mask_ref, weights, h1, h2, out, rows):
+def networks(x, mask_ref, weights, h1, h2, out, rows, arrive):
     def net(n, carry):
+        if arrive:
+            arrive(n, 0)
         want = (1 - n).astype(jnp.float32)
         for t in range(HID // TILE):
             w = weights[n, t * TILE : (t + 1) * TILE, 0:IN]
             d = lax.dot_general(x[...], w, (((1,), (1,)), ((), ())), preferred_element_type=jnp.float32)
             h1[0:rows, t * TILE : (t + 1) * TILE] = silu(d)
+        if arrive:
+            arrive(n, 1)
         for t in range(HID // TILE):
             w = weights[n, :, IN + t * TILE : IN + (t + 1) * TILE]
             d = jnp.dot(h1[0:rows, :], w, preferred_element_type=jnp.float32)
@@ -178,7 +181,6 @@
     result = rest[8]
     weights, h1, h2, out, ext, x2, moved2, sems = rest[9:]
     core = table[16]
-    copies = []
     for k in range(8):
         net = core if k < 4 else 1 - core
         colour = (k // 2) % 2
@@ -192,13 +194,16 @@
                 col = pl.multiple_of((x // 2) * HALF, 128)
                 src = pieces[k].at[pl.ds((p * 4 + q) * 64, 64), :]
                 dst = weights.at[net, pl.ds(row, 64), pl.ds(col, HALF)]
-                copies.append(pltpu.make_async_copy(src, dst, sems.at[len(copies)]))
-    for c in copies:
-        c.start()
-    for c in copies:
-        c.wait()
-
-    networks(x1, mask0, weights, h1, h2, out, ROWS)
+                sem = (net * 2 + x // 2) * 16 + y * 4 + (x % 2) * 2 + colour
+                pltpu.make_async_copy(src, dst, sems.at[sem]).start()
+
+    def arrive(net, half):
+        for k in range(16):
+            src = pieces[0].at[pl.ds(0, 64), :]
+            dst = weights.at[net, pl.ds(k * 64, 64), pl.ds(half * HALF, HALF)]
+            pltpu.make_async_copy(src, dst, sems.at[(net * 2 + half) * 16 + k]).wait()
+
+    networks(x1, mask0, weights, h1, h2, out, ROWS, arrive)
 
     def spread(c, carry):
         row = pl.multiple_of(c * R, R)
@@ -226,7 +231,7 @@
         return carry
 
     lax.fori_loop(0, C, second, 0)
-    networks(x2, mask1, weights, h1, h2, out, C * R)
+    networks(x2, mask1, weights, h1, h2, out, C * R, None)
 
     def finish(c, carry):
         row = pl.multiple_of(c * R, R)
@@ -237,14 +242,27 @@
     lax.fori_loop(0, C, finish, 0)
 
 
+def position_table():
+    out = np.zeros((32, 32), np.int32)
+
+    def order(i, net):
+        p = ring_partner(i, net)
+        n = ring_partner(i, 1 - net)
+        return [i, p, n, ring_partner(n, net)]
+
+    for y, xl, xh, core in np.ndindex(4, 2, 2, 2):
+        x, lat = xh * 2 + xl, xh * 2 + core
+        row = order(x, 0) + order(y, 0) + order(x, 1) + order(y, 1) + [core, int(lat > 0), int(lat < 3)]
+        out[((y * 2 + xl) * 2 + xh) * 2 + core, : len(row)] = row
+    return out
+
+
 def vmem(n):
     return [pl.BlockSpec(memory_space=pltpu.VMEM)] * n
 
 
 def shards(fields, day_mask, w_in, w_mid, w_out):
     y, xl, xh, core = (lax.axis_index(a) for a in ("y", "xl", "xh", "core"))
-    lat = xh * 2 + core
-
     joined = jnp.concatenate([w_in, w_mid, w_out], axis=2)
     block = lax.dynamic_slice(joined, (core, 0, xh * HALF), (1, 8, HALF))[0]
     pieces = gather_weights(block)
@@ -253,15 +271,29 @@
     masks = jnp.broadcast_to(
         day_mask.transpose(0, 2, 1)[..., None].astype(jnp.float32), (2, C, R, L)
     )
-    both = jnp.concatenate([ft.astype(jnp.bfloat16), masks[0][:, None].astype(jnp.bfloat16)], axis=1)
-    lon_n = 128
-    lon_w = lax.ppermute(both[C - 2 :], LON, [(i, (i + 1) % lon_n) for i in range(lon_n)])
-    lon_e = lax.ppermute(both[:2], LON, [((i + 1) % lon_n, i) for i in range(lon_n)])
-    wide = jnp.concatenate([lon_w[1:], both, lon_e[:1]], axis=0)
-    lat_s = lax.ppermute(wide[:, :, R - 2 :], LAT, [(i, i + 1) for i in range(3)])
-    lat_n = lax.ppermute(wide[:, :, :2], LAT, [(i + 1, i) for i in range(3)])
-
-    moved1, x1, mask0 = pl.pallas_call(
+    lon_n, lat_n_blocks = 128, 4
+
+    def packed(cols, rows):
+        part = ft[cols, :, rows].astype(jnp.bfloat16)
+        return jnp.concatenate([part, masks[0][cols, None, rows].astype(jnp.bfloat16)], axis=1)
+
+    lon_w = lax.ppermute(
+        packed(slice(C - 2, C), slice(0, R)), LON, [(i, (i + 1) % lon_n) for i in range(lon_n)]
+    )
+    lon_e = lax.ppermute(
+        packed(slice(0, 2), slice(0, R)), LON, [((i + 1) % lon_n, i) for i in range(lon_n)]
+    )
+
+    def wide(rows):
+        return jnp.concatenate(
+            [lon_w[1:, :, rows], packed(slice(0, C), rows), lon_e[:1, :, rows]], axis=0
+        )
+
+    ends = range(lat_n_blocks - 1)
+    lat_s = lax.ppermute(wide(slice(R - 2, R)), LAT, [(i, i + 1) for i in ends])
+    lat_n = lax.ppermute(wide(slice(0, 2)), LAT, [(i + 1, i) for i in ends])
+
+    prepare = pl.pallas_call(
         prepare_kernel,
         out_shape=(
             jax.ShapeDtypeStruct((ROWS, IN), jnp.float32),
@@ -276,20 +308,11 @@
         ],
         compiler_params=pltpu.CompilerParams(vmem_limit_bytes=12 << 20),
         name="prepare",
-    )(ft, masks[0], lon_w, lon_e, lat_s, lat_n)
-
-    x = xh * 2 + xl
-
-    def partners(i):
-        return i ^ 1, jnp.where(i % 2 == 1, (i + 1) % 4, (i + 3) % 4)
-
-    def order(i, net):
-        p, n = partners(i)[net], partners(i)[1 - net]
-        return [i, p, n, partners(n)[net]]
-
-    entries = [*order(x, 0), *order(y, 0), *order(x, 1), *order(y, 1)]
-    entries += [core, (lat > 0).astype(jnp.int32), (lat < 3).astype(jnp.int32)]
-    table = jnp.stack([e.astype(jnp.int32) for e in entries])
+    )
+    moved1, x1, mask0 = prepare(ft, masks[0], lon_w, lon_e, lat_s, lat_n)
+
+    at = ((y * 2 + xl) * 2 + xh) * 2 + core
+    table = lax.dynamic_slice(jnp.asarray(position_table()), (at, 0), (1, 32))[0]
 
     result = pl.pallas_call(
         step_kernel,
@@ -323,6 +346,7 @@
         P(None, LON, None),
         P(None, LON, None),
     )
+
     return jax.shard_map(
         shards, mesh=grid, in_specs=in_specs, out_specs=P(LAT, LON, None, None), check_vma=False
     )

time: 158 us -> 151 us (0.956)
  starting transfers between devices: 72.9 us -> 68 us
  waiting for transfers between devices: 27.5 us -> 23 us
    ppermute x4, waiting for transfers between devices: 14.4 us -> 9.86 us  [the longest x1 5.25 us: shards(): lat_n = lax.ppermute(wide(slice(0, 2)), LAT, [(i + 1, i) for i in ends])]
    ppermute x4, starting transfers between devices: 37.3 us -> 34.1 us  [core_swap(): return lax.ppermute(a, 'core', [(0, 1), (1, 0)])]
    ppermute x4, starting transfers between devices: 10.1 us -> 8.29 us  [the longest x1 2.54 us: shards(): lat_s = lax.ppermute(wide(slice(R - 2, R)), LAT, [(i, i + 1) for i in ends])]
  transfers between devices with their start and end apart: 16 -> 16, of which waited for: 7 -> 6; matrix products, arithmetic and copies ran while one was open for 2% -> 3% of each run, Pallas kernels for 2% -> 2%
where the time goes in v2:
time: 151 us; the launch traced here: 150 us
  starting transfers between devices  68 us (45%)
  blocking collectives  30.8 us (20%)
  waiting for transfers between devices  23 us (15%)
  Pallas kernels  22 us (15%)
  local copies, waits for them, and re-layouts  3.33 us (2%)
  other arithmetic  2.79 us (2%)
    ppermute x4, starting transfers between devices, core_swap(): return lax.ppermute(a, 'core', [(0, 1), (1, 0)])  34.1 us
    all_gather x1, blocking collectives, gather_weights(): z = lax.all_gather(block, 'z', axis=0)  30.8 us
    pallas_call x1, Pallas kernels, shards(): pl.pallas_call(step_kernel, out_shape=jax.ShapeDtypeStruct((C, F, R, L),...  18.7 us
    ppermute x4, starting transfers between devices, x_exchange(): return lax.ppermute(a, ('xl', 'xh', 'core'), pairs)  13.3 us
    ppermute x4, starting transfers between devices, y_exchange(): return lax.ppermute(a, ('y', 'core'), pairs)  12.3 us
    ppermute x4, waiting for transfers between devices, y_exchange(): return lax.ppermute(a, ('y', 'core'), pairs)  8.5 us
    ppermute x1, waiting for transfers between devices, shards(): lat_n = lax.ppermute(wide(slice(0, 2)), LAT, [(i + 1, i) for i in ends])  5.25 us
    ppermute x4, waiting for transfers between devices, x_exchange(): return lax.ppermute(a, ('xl', 'xh', 'core'), pairs)  4.59 us
  transfers between devices with their start and end apart: 16, of which 6 were waited for; matrix products, arithmetic and copies ran while one was open for 3% of the time, Pallas kernels for 2%

profile of v2, /device:TPU:1, one launch (start us, length us, event | category | flops | bytes accessed | tf_op | source)
XLA Modules:
  0.0 150.2 jit_solution(3374307907838108677)
XLA Ops:
  0.0 0.7 fusion.1
  0.7 30.8 %all_gather.3 = bf16[16,8,1280]{2,1,0:T(8,128)(2,1)S(1)} all-gather(bf16[1,8,1280]{2,1,0:T(8,128)(2,1)S(1)} %fusion.1), channel_id=1, replica_groups=mesh['y'=4,'xl'=2,'z'=16,'xh'=2,'core'=2] {'z'}, dimensions={0}, use_global_device_ids=true | all-gather | bytes 348160 | tf_op jit(solution)/shard_map/all_gather | solution.py:56
  31.6 4.4 %collective-permute-start.4 = (bf16[8,8,1280]{2,1,0:T(8,128)(2,1)S(1)}, bf16[8,8,1280]{2,1,0:T(8,128)(2,1)S(1)}, u32[]{:S(2)}, u32[]{:S(2)}) collective-permute-start(bf16[8,8,1280]{2,1,0:T(8,128)(2,1)S(1)} %get-tuple-element.22), channel_id=1, source_target_pairs={{0,64},{1,67},{64,0},{65,3},{2,66},{3,65},{66,2},{67,1},{4,68},{5,... | collective-permute-start | bytes 491528 | tf_op jit(solution)/shard_map/ppermute | solution.py:39
  36.0 4.6 %collective-permute-start.8 = (bf16[8,8,1280]{2,1,0:T(8,128)(2,1)S(1)}, bf16[8,8,1280]{2,1,0:T(8,128)(2,1)S(1)}, u32[]{:S(2)}, u32[]{:S(2)}) collective-permute-start(bf16[8,8,1280]{2,1,0:T(8,128)(2,1)S(1)} %get-tuple-element.21), channel_id=1, source_target_pairs={{0,128},{1,385},{128,0},{129,257},{256,384},{257,129},{384,256},{3... | collective-permute-start | bytes 491528 | tf_op jit(solution)/shard_map/ppermute | solution.py:48
  40.7 1.9 %collective-permute-start.5 = (bf16[2,8,8,1280]{3,2,1,0:T(8,128)(2,1)S(1)}, bf16[2,8,8,1280]{3,2,1,0:T(8,128)(2,1)S(1)}, u32[]{:S(2)}, u32[]{:S(2)}) collective-permute-start(bf16[2,8,8,1280]{3,2,1,0:T(8,128)(2,1)S(1)} %pad_maximum_fusion.4), channel_id=1, source_target_pairs={{0,66},{1,65},{64,2},{65,1},{2,64},{3,67},{66,0},{67,3},{4,70},{5,... | collective-permute-start | bytes 983048 | tf_op jit(solution)/shard_map/ppermute | solution.py:39
  42.6 0.7 collective-permute-done.8
  43.3 1.9 %collective-permute-start.9 = (bf16[2,8,8,1280]{3,2,1,0:T(8,128)(2,1)S(1)}, bf16[2,8,8,1280]{3,2,1,0:T(8,128)(2,1)S(1)}, u32[]{:S(2)}, u32[]{:S(2)}) collective-permute-start(bf16[2,8,8,1280]{3,2,1,0:T(8,128)(2,1)S(1)} %pad_maximum_fusion.5), channel_id=1, source_target_pairs={{0,384},{1,129},{128,256},{129,1},{256,128},{257,385},{384,0},{385... | collective-permute-start | bytes 983048 | tf_op jit(solution)/shard_map/ppermute | solution.py:48
  45.3 4.6 %collective-permute-done.5 = bf16[2,8,8,1280]{3,2,1,0:T(8,128)(2,1)S(1)} collective-permute-done((bf16[2,8,8,1280]{3,2,1,0:T(8,128)(2,1)S(1)}, bf16[2,8,8,1280]{3,2,1,0:T(8,128)(2,1)S(1)}, u32[]{:S(2)}, u32[]{:S(2)}) %collective-permute-start.5) | collective-permute-done | bytes 327712 | tf_op jit(solution)/shard_map/ppermute | solution.py:39
  49.9 0.1 fusion.6
  50.0 3.8 %collective-permute-start.6 = (bf16[4,8,8,1280]{3,2,1,0:T(8,128)(2,1)S(1)}, bf16[4,8,8,1280]{3,2,1,0:T(8,128)(2,1)S(1)}, u32[]{:S(2)}, u32[]{:S(2)}) collective-permute-start(bf16[4,8,8,1280]{3,2,1,0:T(8,128)(2,1)S(1)} %get-tuple-element.14), channel_id=1, source_target_pairs={{0,128},{1,385},{128,0},{129,257},{256,384},{257,129},{384,256},{3... | collective-permute-start | bytes 1966088 | tf_op jit(solution)/shard_map/ppermute | solution.py:48
  53.7 0.1 fusion.5
  53.9 4.4 %collective-permute-start.10 = (bf16[4,8,8,1280]{3,2,1,0:T(8,128)(2,1)S(1)}, bf16[4,8,8,1280]{3,2,1,0:T(8,128)(2,1)S(1)}, u32[]{:S(2)}, u32[]{:S(2)}) collective-permute-start(bf16[4,8,8,1280]{3,2,1,0:T(8,128)(2,1)S(1)} %get-tuple-element.12), channel_id=1, source_target_pairs={{0,64},{1,67},{64,0},{65,3},{2,66},{3,65},{66,2},{67,1},{4,68},{5,... | collective-permute-start | bytes 1966088 | tf_op jit(solution)/shard_map/ppermute | solution.py:39
  58.3 7.8 %collective-permute-done.6 = bf16[4,8,8,1280]{3,2,1,0:T(8,128)(2,1)S(1)} collective-permute-done((bf16[4,8,8,1280]{3,2,1,0:T(8,128)(2,1)S(1)}, bf16[4,8,8,1280]{3,2,1,0:T(8,128)(2,1)S(1)}, u32[]{:S(2)}, u32[]{:S(2)}) %collective-permute-start.6) | collective-permute-done | bytes 655392 | tf_op jit(solution)/shard_map/ppermute | solution.py:48
  66.0 0.1 pad_maximum_fusion
  66.2 1.9 %collective-permute-start.7 = (bf16[2,4,8,8,1280]{4,3,2,1,0:T(8,128)(2,1)S(1)}, bf16[2,4,8,8,1280]{4,3,2,1,0:T(8,128)(2,1)}, u32[]{:S(2)}, u32[]{:S(2)}) collective-permute-start(bf16[2,4,8,8,1280]{4,3,2,1,0:T(8,128)(2,1)S(1)} %pad_maximum_fusion), channel_id=1, source_target_pairs={{0,384},{1,129},{128,256},{129,1},{256,128},{257,385},{384,0},{385... | collective-permute-start | bytes 3932168 | tf_op jit(solution)/shard_map/ppermute | solution.py:48
  68.1 0.1 pad_maximum_fusion.1
  68.2 2.6 %collective-permute-start.11 = (bf16[2,4,8,8,1280]{4,3,2,1,0:T(8,128)(2,1)S(1)}, bf16[2,4,8,8,1280]{4,3,2,1,0:T(8,128)(2,1)}, u32[]{:S(2)}, u32[]{:S(2)}) collective-permute-start(bf16[2,4,8,8,1280]{4,3,2,1,0:T(8,128)(2,1)S(1)} %pad_maximum_fusion.1), channel_id=1, source_target_pairs={{0,66},{1,65},{64,2},{65,1},{2,64},{3,67},{66,0},{67,3},{4,70},{5,... | collective-permute-start | bytes 3932168 | tf_op jit(solution)/shard_map/ppermute | solution.py:39
  70.8 0.1 fusion.12
  70.9 0.1 copy.19
  71.0 1.3 bitcast_convert_fusion
  72.4 1.9 %collective-permute-start = (bf16[2,7,16,128]{3,2,1,0:T(8,128)(2,1)S(1)}, bf16[2,7,16,128]{3,2,1,0:T(8,128)(2,1)S(1)}, u32[]{:S(2)}, u32[]{:S(2)}) collective-permute-start(bf16[2,7,16,128]{3,2,1,0:T(8,128)(2,1)S(1)} %pad_maximum_fusion.8), channel_id=1, source_target_pairs={{0,4},{4,8},{8,12},{12,16},{16,20},{20,24},{24,28},{28,32},{32,36}... | collective-permute-start | bytes 172040 | tf_op jit(solution)/shard_map/ppermute | solution.py:280
  74.3 0.1 copy.20
  74.4 0.1 copy.23
  74.5 0.1 broadcast_in_dim.24
  74.6 19.1 %collective-permute-start.12 = (bf16[2,4,8,8,1280]{4,3,2,1,0:T(8,128)(2,1)S(1)}, bf16[2,4,8,8,1280]{4,3,2,1,0:T(8,128)(2,1)}, u32[]{:S(2)}, u32[]{:S(2)}) collective-permute-start(bf16[2,4,8,8,1280]{4,3,2,1,0:T(8,128)(2,1)S(1)} %pad_maximum_fusion), channel_id=1, source_target_pairs={{0,1},{1,0},{2,3},{3,2},{4,5},{5,4},{6,7},{7,6},{8,9},{9,8},{10,11... | collective-permute-start | bytes 3932168 | tf_op jit(solution)/shard_map/ppermute | solution.py:52
  93.7 1.9 %collective-permute-start.14 = (bf16[2,4,8,8,1280]{4,3,2,1,0:T(8,128)(2,1)S(1)}, bf16[2,4,8,8,1280]{4,3,2,1,0:T(8,128)(2,1)}, u32[]{:S(2)}, u32[]{:S(2)}) collective-permute-start(bf16[2,4,8,8,1280]{4,3,2,1,0:T(8,128)(2,1)S(1)} %pad_maximum_fusion.1), channel_id=1, source_target_pairs={{0,1},{1,0},{2,3},{3,2},{4,5},{5,4},{6,7},{7,6},{8,9},{9,8},{10,11... | collective-permute-start | bytes 3932168 | tf_op jit(solution)/shard_map/ppermute | solution.py:52
  95.6 2.4 %collective-permute-start.13 = (bf16[2,4,8,8,1280]{4,3,2,1,0:T(8,128)(2,1)}, bf16[2,4,8,8,1280]{4,3,2,1,0:T(8,128)(2,1)}, u32[]{:S(2)}, u32[]{:S(2)}) collective-permute-start(bf16[2,4,8,8,1280]{4,3,2,1,0:T(8,128)(2,1)} %collective-permute-done.7), channel_id=1, source_target_pairs={{0,1},{1,0},{2,3},{3,2},{4,5},{5,4},{6,7},{7,6},{8,9},{9,8},{10,11... | collective-permute-start | bytes 3932168 | tf_op jit(solution)/shard_map/ppermute | solution.py:52
  98.0 10.7 %collective-permute-start.15 = (bf16[2,4,8,8,1280]{4,3,2,1,0:T(8,128)(2,1)}, bf16[2,4,8,8,1280]{4,3,2,1,0:T(8,128)(2,1)}, u32[]{:S(2)}, u32[]{:S(2)}) collective-permute-start(bf16[2,4,8,8,1280]{4,3,2,1,0:T(8,128)(2,1)} %collective-permute-done.11), channel_id=1, source_target_pairs={{0,1},{1,0},{2,3},{3,2},{4,5},{5,4},{6,7},{7,6},{8,9},{9,8},{10,11... | collective-permute-start | bytes 3932168 | tf_op jit(solution)/shard_map/ppermute | solution.py:52
  108.8 0.1 copy.22
  108.9 0.1 copy.21
  109.0 0.1 copy.18
  109.1 0.1 fusion.7
  109.3 1.9 %collective-permute-start.1 = (bf16[2,7,16,128]{3,2,1,0:T(8,128)(2,1)S(1)}, bf16[2,7,16,128]{3,2,1,0:T(8,128)(2,1)S(1)}, u32[]{:S(2)}, u32[]{:S(2)}) collective-permute-start(bf16[2,7,16,128]{3,2,1,0:T(8,128)(2,1)S(1)} %pad_maximum_fusion.9), channel_id=1, source_target_pairs={{4,0},{8,4},{12,8},{16,12},{20,16},{24,20},{28,24},{32,28},{36,32}... | collective-permute-start | bytes 172040 | tf_op jit(solution)/shard_map/ppermute | solution.py:283
  111.2 3.4 %collective-permute-done.1.lon_e = bf16[2,7,16,128]{3,2,1,0:T(8,128)(2,1)S(1)} collective-permute-done((bf16[2,7,16,128]{3,2,1,0:T(8,128)(2,1)S(1)}, bf16[2,7,16,128]{3,2,1,0:T(8,128)(2,1)S(1)}, u32[]{:S(2)}, u32[]{:S(2)}) %collective-permute-start.1) | collective-permute-done | bytes 57376 | tf_op jit(solution)/shard_map/ppermute | solution.py:283
  114.7 0.1 convert_element_type.39
  114.7 0.1 pad_maximum_fusion.6
  114.9 2.5 %collective-permute-start.2 = (bf16[22,7,2,128]{3,2,1,0:T(2,128)(2,1)S(1)}, bf16[22,7,2,128]{3,2,1,0:T(2,128)(2,1)S(1)}, u32[]{:S(2)}, u32[]{:S(2)}) collective-permute-start(bf16[22,7,2,128]{3,2,1,0:T(2,128)(2,1)S(1)} %pad_maximum_fusion.6), channel_id=1, source_target_pairs={{0,1},{1,2},{2,3},{4,5},{5,6},{6,7},{8,9},{9,10},{10,11},{12,13},{... | collective-permute-start | bytes 236552 | tf_op jit(solution)/shard_map/ppermute | solution.py:293
  117.4 0.1 convert_element_type.40
  117.5 0.1 pad_maximum_fusion.7
  117.7 1.2 collective-permute-done.2.lat_s
  118.9 1.9 %collective-permute-start.3 = (bf16[22,7,2,128]{3,2,1,0:T(2,128)(2,1)S(1)}, bf16[22,7,2,128]{3,2,1,0:T(2,128)(2,1)S(1)}, u32[]{:S(2)}, u32[]{:S(2)}) collective-permute-start(bf16[22,7,2,128]{3,2,1,0:T(2,128)(2,1)S(1)} %pad_maximum_fusion.7), channel_id=1, source_target_pairs={{1,0},{2,1},{3,2},{5,4},{6,5},{7,6},{9,8},{10,9},{11,10},{13,12},{... | collective-permute-start | bytes 236552 | tf_op jit(solution)/shard_map/ppermute | solution.py:294
  120.8 0.7 fusion.2.table
  121.5 5.2 %collective-permute-done.3.lat_n = bf16[22,7,2,128]{3,2,1,0:T(2,128)(2,1)S(1)} collective-permute-done((bf16[22,7,2,128]{3,2,1,0:T(2,128)(2,1)S(1)}, bf16[22,7,2,128]{3,2,1,0:T(2,128)(2,1)S(1)}, u32[]{:S(2)}, u32[]{:S(2)}) %collective-permute-start.3) | collective-permute-done | bytes 78880 | tf_op jit(solution)/shard_map/ppermute | solution.py:294
  126.7 0.1 broadcast_in_dim.21.mask
  126.8 1.2 copy-done
  128.0 3.2 %prepare.1 = (f32[400,768]{1,0:T(8,128)S(1)}, bf16[400,768]{1,0:T(8,128)(2,1)S(1)}, f32[400,128]{1,0:T(8,128)S(1)}) custom-call(f32[20,6,16,128]{3,2,1,0:T(8,128)S(1)} %bitcast.37, f32[20,16,128]{2,1,0:T(8,128)S(1)} %broadcast_in_dim.21.mask, bf16[2,7,16,128]{3,2,1,0:T(8,128)(2,1)S(1)} %collective-permute-done.lon_w, ...), custom_call_target="tpu_custom_call" | custom-call | tf_op jit(solution)/shard_map/prepare/pallas_call | solution.py:312
  131.3 0.1 broadcast_in_dim.25.mask1
  131.4 18.7 %steps.1 = f32[20,6,16,128]{3,2,1,0:T(8,128)} custom-call(s32[32]{0:T(128)S(1)} %fusion.2.table, bf16[400,768]{1,0:T(8,128)(2,1)S(1)} %get-tuple-element.8.x1, f32[400,768]{1,0:T(8,128)S(1)} %get-tuple-element.9.moved1, f32[400,128]{1,0:T(8,128)S(1)} %get-tuple-element.10.mask0, f32[320,128]{1,0:T(8,128)S(1)} %broadcast_in_dim.25.mask1, ...), custom_call_target="tpu_custom_call" | custom-call | tf_op jit(solution)/shard_map/steps/pallas_call | solution.py:317
  (27 shorter events, 0.4 us)
Async XLA Ops:
  31.6 9.1 %collective-permute-start.4 = (bf16[8,8,1280]{2,1,0:T(8,128)(2,1)S(1)}, bf16[8,8,1280]{2,1,0:T(8,128)(2,1)S(1)}, u32[]{:S(2)}, u32[]{:S(2)}) collective-permute-start(bf16[8,8,1280]{2,1,0:T(8,128)(2,1)S(1)} %get-tuple-element.22), channel_id=1, source_target_pairs={{0,64},{1,67},{64,0},{65,3},{2,66},{3,65},{66,2},{67,1},{4,68},{5,... | collective-permute-start | bytes 491528 | tf_op jit(solution)/shard_map/ppermute | solution.py:39
  36.0 7.3 %collective-permute-start.8 = (bf16[8,8,1280]{2,1,0:T(8,128)(2,1)S(1)}, bf16[8,8,1280]{2,1,0:T(8,128)(2,1)S(1)}, u32[]{:S(2)}, u32[]{:S(2)}) collective-permute-start(bf16[8,8,1280]{2,1,0:T(8,128)(2,1)S(1)} %get-tuple-element.21), channel_id=1, source_target_pairs={{0,128},{1,385},{128,0},{129,257},{256,384},{257,129},{384,256},{3... | collective-permute-start | bytes 491528 | tf_op jit(solution)/shard_map/ppermute | solution.py:48
  40.7 9.2 %collective-permute-start.5 = (bf16[2,8,8,1280]{3,2,1,0:T(8,128)(2,1)S(1)}, bf16[2,8,8,1280]{3,2,1,0:T(8,128)(2,1)S(1)}, u32[]{:S(2)}, u32[]{:S(2)}) collective-permute-start(bf16[2,8,8,1280]{3,2,1,0:T(8,128)(2,1)S(1)} %pad_maximum_fusion.4), channel_id=1, source_target_pairs={{0,66},{1,65},{64,2},{65,1},{2,64},{3,67},{66,0},{67,3},{4,70},{5,... | collective-permute-start | bytes 983048 | tf_op jit(solution)/shard_map/ppermute | solution.py:39
  43.3 10.4 %collective-permute-start.9 = (bf16[2,8,8,1280]{3,2,1,0:T(8,128)(2,1)S(1)}, bf16[2,8,8,1280]{3,2,1,0:T(8,128)(2,1)S(1)}, u32[]{:S(2)}, u32[]{:S(2)}) collective-permute-start(bf16[2,8,8,1280]{3,2,1,0:T(8,128)(2,1)S(1)} %pad_maximum_fusion.5), channel_id=1, source_target_pairs={{0,384},{1,129},{128,256},{129,1},{256,128},{257,385},{384,0},{385... | collective-permute-start | bytes 983048 | tf_op jit(solution)/shard_map/ppermute | solution.py:48
  50.0 16.1 %collective-permute-start.6 = (bf16[4,8,8,1280]{3,2,1,0:T(8,128)(2,1)S(1)}, bf16[4,8,8,1280]{3,2,1,0:T(8,128)(2,1)S(1)}, u32[]{:S(2)}, u32[]{:S(2)}) collective-permute-start(bf16[4,8,8,1280]{3,2,1,0:T(8,128)(2,1)S(1)} %get-tuple-element.14), channel_id=1, source_target_pairs={{0,128},{1,385},{128,0},{129,257},{256,384},{257,129},{384,256},{3... | collective-permute-start | bytes 1966088 | tf_op jit(solution)/shard_map/ppermute | solution.py:48
  53.9 14.2 %collective-permute-start.10 = (bf16[4,8,8,1280]{3,2,1,0:T(8,128)(2,1)S(1)}, bf16[4,8,8,1280]{3,2,1,0:T(8,128)(2,1)S(1)}, u32[]{:S(2)}, u32[]{:S(2)}) collective-permute-start(bf16[4,8,8,1280]{3,2,1,0:T(8,128)(2,1)S(1)} %get-tuple-element.12), channel_id=1, source_target_pairs={{0,64},{1,67},{64,0},{65,3},{2,66},{3,65},{66,2},{67,1},{4,68},{5,... | collective-permute-start | bytes 1966088 | tf_op jit(solution)/shard_map/ppermute | solution.py:39
  66.2 29.4 %collective-permute-start.7 = (bf16[2,4,8,8,1280]{4,3,2,1,0:T(8,128)(2,1)S(1)}, bf16[2,4,8,8,1280]{4,3,2,1,0:T(8,128)(2,1)}, u32[]{:S(2)}, u32[]{:S(2)}) collective-permute-start(bf16[2,4,8,8,1280]{4,3,2,1,0:T(8,128)(2,1)S(1)} %pad_maximum_fusion), channel_id=1, source_target_pairs={{0,384},{1,129},{128,256},{129,1},{256,128},{257,385},{384,0},{385... | collective-permute-start | bytes 3932168 | tf_op jit(solution)/shard_map/ppermute | solution.py:48
  68.1 2.7 %copy-start.1 = (s32[2,16,20]{2,1,0:T(8,128)S(1)}, s32[2,16,20]{2,1,0:T(8,128)}, u32[]{:S(2)}) copy-start(s32[2,16,20]{2,1,0:T(8,128)} %param.7) | copy-start | bytes 7684
  68.2 29.8 %collective-permute-start.11 = (bf16[2,4,8,8,1280]{4,3,2,1,0:T(8,128)(2,1)S(1)}, bf16[2,4,8,8,1280]{4,3,2,1,0:T(8,128)(2,1)}, u32[]{:S(2)}, u32[]{:S(2)}) collective-permute-start(bf16[2,4,8,8,1280]{4,3,2,1,0:T(8,128)(2,1)S(1)} %pad_maximum_fusion.1), channel_id=1, source_target_pairs={{0,66},{1,65},{64,2},{65,1},{2,64},{3,67},{66,0},{67,3},{4,70},{5,... | collective-permute-start | bytes 3932168 | tf_op jit(solution)/shard_map/ppermute | solution.py:39
  72.4 36.9 %collective-permute-start = (bf16[2,7,16,128]{3,2,1,0:T(8,128)(2,1)S(1)}, bf16[2,7,16,128]{3,2,1,0:T(8,128)(2,1)S(1)}, u32[]{:S(2)}, u32[]{:S(2)}) collective-permute-start(bf16[2,7,16,128]{3,2,1,0:T(8,128)(2,1)S(1)} %pad_maximum_fusion.8), channel_id=1, source_target_pairs={{0,4},{4,8},{8,12},{12,16},{16,20},{20,24},{24,28},{28,32},{32,36}... | collective-permute-start | bytes 172040 | tf_op jit(solution)/shard_map/ppermute | solution.py:280
  74.6 56.7 %collective-permute-start.12 = (bf16[2,4,8,8,1280]{4,3,2,1,0:T(8,128)(2,1)S(1)}, bf16[2,4,8,8,1280]{4,3,2,1,0:T(8,128)(2,1)}, u32[]{:S(2)}, u32[]{:S(2)}) collective-permute-start(bf16[2,4,8,8,1280]{4,3,2,1,0:T(8,128)(2,1)S(1)} %pad_maximum_fusion), channel_id=1, source_target_pairs={{0,1},{1,0},{2,3},{3,2},{4,5},{5,4},{6,7},{7,6},{8,9},{9,8},{10,11... | collective-permute-start | bytes 3932168 | tf_op jit(solution)/shard_map/ppermute | solution.py:52
  93.7 37.6 %collective-permute-start.14 = (bf16[2,4,8,8,1280]{4,3,2,1,0:T(8,128)(2,1)S(1)}, bf16[2,4,8,8,1280]{4,3,2,1,0:T(8,128)(2,1)}, u32[]{:S(2)}, u32[]{:S(2)}) collective-permute-start(bf16[2,4,8,8,1280]{4,3,2,1,0:T(8,128)(2,1)S(1)} %pad_maximum_fusion.1), channel_id=1, source_target_pairs={{0,1},{1,0},{2,3},{3,2},{4,5},{5,4},{6,7},{7,6},{8,9},{9,8},{10,11... | collective-permute-start | bytes 3932168 | tf_op jit(solution)/shard_map/ppermute | solution.py:52
  95.6 35.7 %collective-permute-start.13 = (bf16[2,4,8,8,1280]{4,3,2,1,0:T(8,128)(2,1)}, bf16[2,4,8,8,1280]{4,3,2,1,0:T(8,128)(2,1)}, u32[]{:S(2)}, u32[]{:S(2)}) collective-permute-start(bf16[2,4,8,8,1280]{4,3,2,1,0:T(8,128)(2,1)} %collective-permute-done.7), channel_id=1, source_target_pairs={{0,1},{1,0},{2,3},{3,2},{4,5},{5,4},{6,7},{7,6},{8,9},{9,8},{10,11... | collective-permute-start | bytes 3932168 | tf_op jit(solution)/shard_map/ppermute | solution.py:52
  98.0 33.3 %collective-permute-start.15 = (bf16[2,4,8,8,1280]{4,3,2,1,0:T(8,128)(2,1)}, bf16[2,4,8,8,1280]{4,3,2,1,0:T(8,128)(2,1)}, u32[]{:S(2)}, u32[]{:S(2)}) collective-permute-start(bf16[2,4,8,8,1280]{4,3,2,1,0:T(8,128)(2,1)} %collective-permute-done.11), channel_id=1, source_target_pairs={{0,1},{1,0},{2,3},{3,2},{4,5},{5,4},{6,7},{7,6},{8,9},{9,8},{10,11... | collective-permute-start | bytes 3932168 | tf_op jit(solution)/shard_map/ppermute | solution.py:52
  109.3 5.4 %collective-permute-start.1 = (bf16[2,7,16,128]{3,2,1,0:T(8,128)(2,1)S(1)}, bf16[2,7,16,128]{3,2,1,0:T(8,128)(2,1)S(1)}, u32[]{:S(2)}, u32[]{:S(2)}) collective-permute-start(bf16[2,7,16,128]{3,2,1,0:T(8,128)(2,1)S(1)} %pad_maximum_fusion.9), channel_id=1, source_target_pairs={{4,0},{8,4},{12,8},{16,12},{20,16},{24,20},{28,24},{32,28},{36,32}... | collective-permute-start | bytes 172040 | tf_op jit(solution)/shard_map/ppermute | solution.py:283
  114.9 4.0 %collective-permute-start.2 = (bf16[22,7,2,128]{3,2,1,0:T(2,128)(2,1)S(1)}, bf16[22,7,2,128]{3,2,1,0:T(2,128)(2,1)S(1)}, u32[]{:S(2)}, u32[]{:S(2)}) collective-permute-start(bf16[22,7,2,128]{3,2,1,0:T(2,128)(2,1)S(1)} %pad_maximum_fusion.6), channel_id=1, source_target_pairs={{0,1},{1,2},{2,3},{4,5},{5,6},{6,7},{8,9},{9,10},{10,11},{12,13},{... | collective-permute-start | bytes 236552 | tf_op jit(solution)/shard_map/ppermute | solution.py:293
  118.9 7.9 %collective-permute-start.3 = (bf16[22,7,2,128]{3,2,1,0:T(2,128)(2,1)S(1)}, bf16[22,7,2,128]{3,2,1,0:T(2,128)(2,1)S(1)}, u32[]{:S(2)}, u32[]{:S(2)}) collective-permute-start(bf16[22,7,2,128]{3,2,1,0:T(2,128)(2,1)S(1)} %pad_maximum_fusion.7), channel_id=1, source_target_pairs={{1,0},{2,1},{3,2},{5,4},{6,5},{7,6},{9,8},{10,9},{11,10},{13,12},{... | collective-permute-start | bytes 236552 | tf_op jit(solution)/shard_map/ppermute | solution.py:294
  126.8 1.2 copy-start

commit v3 on v2

--- a/solution.py
+++ b/solution.py
@@ -263,8 +263,12 @@
 
 def shards(fields, day_mask, w_in, w_mid, w_out):
     y, xl, xh, core = (lax.axis_index(a) for a in ("y", "xl", "xh", "core"))
+    at = ((y * 2 + xl) * 2 + xh) * 2 + core
+    table = lax.dynamic_slice(jnp.asarray(position_table()), (at, 0), (1, 32))[0]
+
     joined = jnp.concatenate([w_in, w_mid, w_out], axis=2)
     block = lax.dynamic_slice(joined, (core, 0, xh * HALF), (1, 8, HALF))[0]
+    block, table = lax.optimization_barrier((block, table))
     pieces = gather_weights(block)
 
     ft = fields.transpose(1, 2, 0, 3)
@@ -274,7 +278,7 @@
     lon_n, lat_n_blocks = 128, 4
 
     def packed(cols, rows):
-        part = ft[cols, :, rows].astype(jnp.bfloat16)
+        part = lax.optimization_barrier(ft[cols, :, rows]).astype(jnp.bfloat16)
         return jnp.concatenate([part, masks[0][cols, None, rows].astype(jnp.bfloat16)], axis=1)
 
     lon_w = lax.ppermute(
@@ -306,13 +310,10 @@
             pltpu.VMEM((C + 4, F, 32, L), jnp.float32),
             pltpu.VMEM((WIDE, F, 8, L), jnp.float32),
         ],
-        compiler_params=pltpu.CompilerParams(vmem_limit_bytes=12 << 20),
+        compiler_params=pltpu.CompilerParams(vmem_limit_bytes=10 << 20),
         name="prepare",
     )
     moved1, x1, mask0 = prepare(ft, masks[0], lon_w, lon_e, lat_s, lat_n)
-
-    at = ((y * 2 + xl) * 2 + xh) * 2 + core
-    table = lax.dynamic_slice(jnp.asarray(position_table()), (at, 0), (1, 32))[0]
 
     result = pl.pallas_call(
         step_kernel,
@@ -331,7 +332,7 @@
             pltpu.VMEM((C * R, IN), jnp.float32),
             pltpu.SemaphoreType.DMA((64,)),
         ],
-        compiler_params=pltpu.CompilerParams(vmem_limit_bytes=36 << 20),
+        compiler_params=pltpu.CompilerParams(vmem_limit_bytes=26 << 20),
         name="steps",
     )(table, x1, moved1, mask0, masks[1].reshape(C * R, L), *pieces)
     return result.transpose(2, 0, 1, 3)

time: 151 us -> 153 us (1.013)
  local copies, waits for them, and re-layouts: 3.33 us -> 5.44 us
    ppermute x4, waiting for transfers between devices: 8.5 us -> 4.42 us  [y_exchange(): return lax.ppermute(a, ('y', 'core'), pairs)]
    ppermute x4, waiting for transfers between devices: 4.59 us -> 8.42 us  [x_exchange(): return lax.ppermute(a, ('xl', 'xh', 'core'), pairs)]
    slice x2, local copies, waits for them, and re-layouts: 0.11 us -> 2.23 us  [packed(): part = lax.optimization_barrier(ft[cols, :, rows]).astype(jnp.bfloat16)]
    ppermute x4, starting transfers between devices: 12.3 us -> 14 us  [y_exchange(): return lax.ppermute(a, ('y', 'core'), pairs)]
where the time goes in v3:
time: 153 us; the launch traced here: 152 us
  starting transfers between devices  68.7 us (45%)
  blocking collectives  30.8 us (20%)
  waiting for transfers between devices  23.2 us (15%)
  Pallas kernels  21.9 us (14%)
  local copies, waits for them, and re-layouts  5.44 us (4%)
    ppermute x4, starting transfers between devices, core_swap(): return lax.ppermute(a, 'core', [(0, 1), (1, 0)])  35 us
    all_gather x1, blocking collectives, gather_weights(): z = lax.all_gather(block, 'z', axis=0)  30.8 us
    pallas_call x1, Pallas kernels, shards(): pl.pallas_call(step_kernel, out_shape=jax.ShapeDtypeStruct((C, F, R, L),...  18.7 us
    ppermute x4, starting transfers between devices, y_exchange(): return lax.ppermute(a, ('y', 'core'), pairs)  14 us
    ppermute x4, starting transfers between devices, x_exchange(): return lax.ppermute(a, ('xl', 'xh', 'core'), pairs)  11.8 us
    ppermute x4, waiting for transfers between devices, x_exchange(): return lax.ppermute(a, ('xl', 'xh', 'core'), pairs)  8.42 us
    ppermute x1, waiting for transfers between devices, shards(): lat_n = lax.ppermute(wide(slice(0, 2)), LAT, [(i + 1, i) for i in ends])  5.69 us
    ppermute x4, waiting for transfers between devices, y_exchange(): return lax.ppermute(a, ('y', 'core'), pairs)  4.42 us
  transfers between devices with their start and end apart: 16, of which 6 were waited for; matrix products, arithmetic and copies ran while one was open for 3% of the time, Pallas kernels for 2%

profile of v3, /device:TPU:1, one launch (start us, length us, event | category | flops | bytes accessed | tf_op | source)
XLA Modules:
  0.0 152.0 jit_solution(1920842770034562200)
XLA Ops:
  0.0 0.7 fusion.3.table
  0.7 0.7 fusion.2
  1.4 30.8 %all-gather = bf16[128,1280]{1,0:T(8,128)(2,1)S(1)} all-gather(bf16[8,1280]{1,0:T(8,128)(2,1)S(1)} %fusion.2), channel_id=2, replica_groups=mesh['y'=4,'xl'=2,'z'=16,'xh'=2,'core'=2] {'z'}, dimensions={0}, use_global_device_ids=true | all-gather | bytes 348160 | tf_op jit(solution)/shard_map/all_gather | solution.py:56
  32.2 4.6 %collective-permute-start.8 = (bf16[8,8,1280]{2,1,0:T(8,128)(2,1)S(1)}, bf16[8,8,1280]{2,1,0:T(8,128)(2,1)S(1)}, u32[]{:S(2)}, u32[]{:S(2)}) collective-permute-start(bf16[8,8,1280]{2,1,0:T(8,128)(2,1)S(1)} %get-tuple-element.26), channel_id=1, source_target_pairs={{0,128},{1,385},{128,0},{129,257},{256,384},{257,129},{384,256},{3... | collective-permute-start | bytes 491528 | tf_op jit(solution)/shard_map/ppermute | solution.py:48
  36.9 4.4 %collective-permute-start.4 = (bf16[8,8,1280]{2,1,0:T(8,128)(2,1)S(1)}, bf16[8,8,1280]{2,1,0:T(8,128)(2,1)S(1)}, u32[]{:S(2)}, u32[]{:S(2)}) collective-permute-start(bf16[8,8,1280]{2,1,0:T(8,128)(2,1)S(1)} %get-tuple-element.25), channel_id=1, source_target_pairs={{0,64},{1,67},{64,0},{65,3},{2,66},{3,65},{66,2},{67,1},{4,68},{5,... | collective-permute-start | bytes 491528 | tf_op jit(solution)/shard_map/ppermute | solution.py:39
  41.4 1.9 %collective-permute-start.9 = (bf16[2,8,8,1280]{3,2,1,0:T(8,128)(2,1)S(1)}, bf16[2,8,8,1280]{3,2,1,0:T(8,128)(2,1)S(1)}, u32[]{:S(2)}, u32[]{:S(2)}) collective-permute-start(bf16[2,8,8,1280]{3,2,1,0:T(8,128)(2,1)S(1)} %pad_maximum_fusion.5), channel_id=1, source_target_pairs={{0,384},{1,129},{128,256},{129,1},{256,128},{257,385},{384,0},{385... | collective-permute-start | bytes 983048 | tf_op jit(solution)/shard_map/ppermute | solution.py:48
  43.3 0.9 collective-permute-done.4
  44.2 1.9 %collective-permute-start.5 = (bf16[2,8,8,1280]{3,2,1,0:T(8,128)(2,1)S(1)}, bf16[2,8,8,1280]{3,2,1,0:T(8,128)(2,1)S(1)}, u32[]{:S(2)}, u32[]{:S(2)}) collective-permute-start(bf16[2,8,8,1280]{3,2,1,0:T(8,128)(2,1)S(1)} %pad_maximum_fusion.4), channel_id=1, source_target_pairs={{0,66},{1,65},{64,2},{65,1},{2,64},{3,67},{66,0},{67,3},{4,70},{5,... | collective-permute-start | bytes 983048 | tf_op jit(solution)/shard_map/ppermute | solution.py:39
  46.1 4.4 %collective-permute-done.9 = bf16[2,8,8,1280]{3,2,1,0:T(8,128)(2,1)S(1)} collective-permute-done((bf16[2,8,8,1280]{3,2,1,0:T(8,128)(2,1)S(1)}, bf16[2,8,8,1280]{3,2,1,0:T(8,128)(2,1)S(1)}, u32[]{:S(2)}, u32[]{:S(2)}) %collective-permute-start.9) | collective-permute-done | bytes 327712 | tf_op jit(solution)/shard_map/ppermute | solution.py:48
  50.5 0.1 fusion.6
  50.6 3.5 %collective-permute-start.10 = (bf16[4,8,8,1280]{3,2,1,0:T(8,128)(2,1)S(1)}, bf16[4,8,8,1280]{3,2,1,0:T(8,128)(2,1)S(1)}, u32[]{:S(2)}, u32[]{:S(2)}) collective-permute-start(bf16[4,8,8,1280]{3,2,1,0:T(8,128)(2,1)S(1)} %get-tuple-element.20), channel_id=1, source_target_pairs={{0,64},{1,67},{64,0},{65,3},{2,66},{3,65},{66,2},{67,1},{4,68},{5,... | collective-permute-start | bytes 1966088 | tf_op jit(solution)/shard_map/ppermute | solution.py:39
  54.2 0.1 fusion.7
  54.3 4.6 %collective-permute-start.6 = (bf16[4,8,8,1280]{3,2,1,0:T(8,128)(2,1)S(1)}, bf16[4,8,8,1280]{3,2,1,0:T(8,128)(2,1)S(1)}, u32[]{:S(2)}, u32[]{:S(2)}) collective-permute-start(bf16[4,8,8,1280]{3,2,1,0:T(8,128)(2,1)S(1)} %get-tuple-element.22), channel_id=1, source_target_pairs={{0,128},{1,385},{128,0},{129,257},{256,384},{257,129},{384,256},{3... | collective-permute-start | bytes 1966088 | tf_op jit(solution)/shard_map/ppermute | solution.py:48
  58.9 7.5 %collective-permute-done.10 = bf16[4,8,8,1280]{3,2,1,0:T(8,128)(2,1)S(1)} collective-permute-done((bf16[4,8,8,1280]{3,2,1,0:T(8,128)(2,1)S(1)}, bf16[4,8,8,1280]{3,2,1,0:T(8,128)(2,1)S(1)}, u32[]{:S(2)}, u32[]{:S(2)}) %collective-permute-start.10) | collective-permute-done | bytes 655392 | tf_op jit(solution)/shard_map/ppermute | solution.py:39
  66.5 0.1 pad_maximum_fusion.1
  66.6 1.9 %collective-permute-start.11 = (bf16[2,4,8,8,1280]{4,3,2,1,0:T(8,128)(2,1)S(1)}, bf16[2,4,8,8,1280]{4,3,2,1,0:T(8,128)(2,1)}, u32[]{:S(2)}, u32[]{:S(2)}) collective-permute-start(bf16[2,4,8,8,1280]{4,3,2,1,0:T(8,128)(2,1)S(1)} %pad_maximum_fusion.1), channel_id=1, source_target_pairs={{0,66},{1,65},{64,2},{65,1},{2,64},{3,67},{66,0},{67,3},{4,70},{5,... | collective-permute-start | bytes 3932168 | tf_op jit(solution)/shard_map/ppermute | solution.py:39
  68.6 0.1 pad_maximum_fusion
  68.7 2.8 %collective-permute-start.7 = (bf16[2,4,8,8,1280]{4,3,2,1,0:T(8,128)(2,1)S(1)}, bf16[2,4,8,8,1280]{4,3,2,1,0:T(8,128)(2,1)}, u32[]{:S(2)}, u32[]{:S(2)}) collective-permute-start(bf16[2,4,8,8,1280]{4,3,2,1,0:T(8,128)(2,1)S(1)} %pad_maximum_fusion), channel_id=1, source_target_pairs={{0,384},{1,129},{128,256},{129,1},{256,128},{257,385},{384,0},{385... | collective-permute-start | bytes 3932168 | tf_op jit(solution)/shard_map/ppermute | solution.py:48
  71.5 0.1 fusion.13
  71.6 0.1 copy.13
  71.7 1.0 fusion.9
  72.8 1.9 %collective-permute-start = (bf16[2,7,16,128]{3,2,1,0:T(8,128)(2,1)S(1)}, bf16[2,7,16,128]{3,2,1,0:T(8,128)(2,1)S(1)}, u32[]{:S(2)}, u32[]{:S(2)}) collective-permute-start(bf16[2,7,16,128]{3,2,1,0:T(8,128)(2,1)S(1)} %pad_maximum_fusion.8), channel_id=1, source_target_pairs={{0,4},{4,8},{8,12},{12,16},{16,20},{20,24},{24,28},{28,32},{32,36}... | collective-permute-start | bytes 172040 | tf_op jit(solution)/shard_map/ppermute | solution.py:284
  74.7 19.0 %collective-permute-start.14 = (bf16[2,4,8,8,1280]{4,3,2,1,0:T(8,128)(2,1)S(1)}, bf16[2,4,8,8,1280]{4,3,2,1,0:T(8,128)(2,1)}, u32[]{:S(2)}, u32[]{:S(2)}) collective-permute-start(bf16[2,4,8,8,1280]{4,3,2,1,0:T(8,128)(2,1)S(1)} %pad_maximum_fusion.1), channel_id=1, source_target_pairs={{0,1},{1,0},{2,3},{3,2},{4,5},{5,4},{6,7},{7,6},{8,9},{9,8},{10,11... | collective-permute-start | bytes 3932168 | tf_op jit(solution)/shard_map/ppermute | solution.py:52
  93.7 1.9 %collective-permute-start.12 = (bf16[2,4,8,8,1280]{4,3,2,1,0:T(8,128)(2,1)S(1)}, bf16[2,4,8,8,1280]{4,3,2,1,0:T(8,128)(2,1)}, u32[]{:S(2)}, u32[]{:S(2)}) collective-permute-start(bf16[2,4,8,8,1280]{4,3,2,1,0:T(8,128)(2,1)S(1)} %pad_maximum_fusion), channel_id=1, source_target_pairs={{0,1},{1,0},{2,3},{3,2},{4,5},{5,4},{6,7},{7,6},{8,9},{9,8},{10,11... | collective-permute-start | bytes 3932168 | tf_op jit(solution)/shard_map/ppermute | solution.py:52
  95.7 2.4 %collective-permute-start.15 = (bf16[2,4,8,8,1280]{4,3,2,1,0:T(8,128)(2,1)}, bf16[2,4,8,8,1280]{4,3,2,1,0:T(8,128)(2,1)}, u32[]{:S(2)}, u32[]{:S(2)}) collective-permute-start(bf16[2,4,8,8,1280]{4,3,2,1,0:T(8,128)(2,1)} %collective-permute-done.11), channel_id=1, source_target_pairs={{0,1},{1,0},{2,3},{3,2},{4,5},{5,4},{6,7},{7,6},{8,9},{9,8},{10,11... | collective-permute-start | bytes 3932168 | tf_op jit(solution)/shard_map/ppermute | solution.py:52
  98.1 11.6 %collective-permute-start.13 = (bf16[2,4,8,8,1280]{4,3,2,1,0:T(8,128)(2,1)}, bf16[2,4,8,8,1280]{4,3,2,1,0:T(8,128)(2,1)}, u32[]{:S(2)}, u32[]{:S(2)}) collective-permute-start(bf16[2,4,8,8,1280]{4,3,2,1,0:T(8,128)(2,1)} %collective-permute-done.7), channel_id=1, source_target_pairs={{0,1},{1,0},{2,3},{3,2},{4,5},{5,4},{6,7},{7,6},{8,9},{9,8},{10,11... | collective-permute-start | bytes 3932168 | tf_op jit(solution)/shard_map/ppermute | solution.py:52
  109.7 0.1 copy.14
  109.8 0.1 copy.16
  109.9 0.1 copy.15
  110.0 1.3 fusion.8
  111.4 1.9 %collective-permute-start.1 = (bf16[2,7,16,128]{3,2,1,0:T(8,128)(2,1)S(1)}, bf16[2,7,16,128]{3,2,1,0:T(8,128)(2,1)S(1)}, u32[]{:S(2)}, u32[]{:S(2)}) collective-permute-start(bf16[2,7,16,128]{3,2,1,0:T(8,128)(2,1)S(1)} %pad_maximum_fusion.9), channel_id=1, source_target_pairs={{4,0},{8,4},{12,8},{16,12},{20,16},{24,20},{28,24},{32,28},{36,32}... | collective-permute-start | bytes 172040 | tf_op jit(solution)/shard_map/ppermute | solution.py:287
  113.3 3.4 %collective-permute-done.1.lon_e = bf16[2,7,16,128]{3,2,1,0:T(8,128)(2,1)S(1)} collective-permute-done((bf16[2,7,16,128]{3,2,1,0:T(8,128)(2,1)S(1)}, bf16[2,7,16,128]{3,2,1,0:T(8,128)(2,1)S(1)}, u32[]{:S(2)}, u32[]{:S(2)}) %collective-permute-start.1) | collective-permute-done | bytes 57376 | tf_op jit(solution)/shard_map/ppermute | solution.py:287
  116.8 0.1 convert_element_type.50
  116.9 0.1 pad_maximum_fusion.6
  117.0 2.2 %collective-permute-start.2 = (bf16[22,7,2,128]{3,2,1,0:T(2,128)(2,1)S(1)}, bf16[22,7,2,128]{3,2,1,0:T(2,128)(2,1)S(1)}, u32[]{:S(2)}, u32[]{:S(2)}) collective-permute-start(bf16[22,7,2,128]{3,2,1,0:T(2,128)(2,1)S(1)} %pad_maximum_fusion.6), channel_id=1, source_target_pairs={{0,1},{1,2},{2,3},{4,5},{5,6},{6,7},{8,9},{9,10},{10,11},{12,13},{... | collective-permute-start | bytes 236552 | tf_op jit(solution)/shard_map/ppermute | solution.py:297
  119.2 0.1 convert_element_type.52
  119.3 0.1 pad_maximum_fusion.7
  119.5 1.2 collective-permute-done.2.lat_s
  120.7 1.9 %collective-permute-start.3 = (bf16[22,7,2,128]{3,2,1,0:T(2,128)(2,1)S(1)}, bf16[22,7,2,128]{3,2,1,0:T(2,128)(2,1)S(1)}, u32[]{:S(2)}, u32[]{:S(2)}) collective-permute-start(bf16[22,7,2,128]{3,2,1,0:T(2,128)(2,1)S(1)} %pad_maximum_fusion.7), channel_id=1, source_target_pairs={{1,0},{2,1},{3,2},{5,4},{6,5},{7,6},{9,8},{10,9},{11,10},{13,12},{... | collective-permute-start | bytes 236552 | tf_op jit(solution)/shard_map/ppermute | solution.py:298
  122.6 0.1 copy.17
  122.7 0.1 broadcast_in_dim.24
  122.8 0.1 copy.12
  122.9 5.7 %collective-permute-done.3.lat_n = bf16[22,7,2,128]{3,2,1,0:T(2,128)(2,1)S(1)} collective-permute-done((bf16[22,7,2,128]{3,2,1,0:T(2,128)(2,1)S(1)}, bf16[22,7,2,128]{3,2,1,0:T(2,128)(2,1)S(1)}, u32[]{:S(2)}, u32[]{:S(2)}) %collective-permute-start.3) | collective-permute-done | bytes 78880 | tf_op jit(solution)/shard_map/ppermute | solution.py:298
  128.5 0.1 broadcast_in_dim.21.mask
  128.7 1.2 copy-done
  129.9 3.2 %prepare.1 = (f32[400,768]{1,0:T(8,128)S(1)}, bf16[400,768]{1,0:T(8,128)(2,1)S(1)}, f32[400,128]{1,0:T(8,128)S(1)}) custom-call(f32[20,6,16,128]{3,2,1,0:T(8,128)S(1)} %bitcast.44, f32[20,16,128]{2,1,0:T(8,128)S(1)} %broadcast_in_dim.21.mask, bf16[2,7,16,128]{3,2,1,0:T(8,128)(2,1)S(1)} %collective-permute-done.lon_w, ...), custom_call_target="tpu_custom_call" | custom-call | tf_op jit(solution)/shard_map/prepare/pallas_call | solution.py:316
  133.1 0.1 broadcast_in_dim.25.mask1
  133.3 18.7 %steps.1 = f32[20,6,16,128]{3,2,1,0:T(8,128)} custom-call(s32[32]{0:T(128)S(1)} %fusion.3.table, bf16[400,768]{1,0:T(8,128)(2,1)S(1)} %get-tuple-element.11.x1, f32[400,768]{1,0:T(8,128)S(1)} %get-tuple-element.12.moved1, f32[400,128]{1,0:T(8,128)S(1)} %get-tuple-element.13.mask0, f32[320,128]{1,0:T(8,128)S(1)} %broadcast_in_dim.25.mask1, ...), custom_call_target="tpu_custom_call" | custom-call | tf_op jit(solution)/shard_map/steps/pallas_call | solution.py:318
  (26 shorter events, 0.3 us)
Async XLA Ops:
  32.2 9.1 %collective-permute-start.8 = (bf16[8,8,1280]{2,1,0:T(8,128)(2,1)S(1)}, bf16[8,8,1280]{2,1,0:T(8,128)(2,1)S(1)}, u32[]{:S(2)}, u32[]{:S(2)}) collective-permute-start(bf16[8,8,1280]{2,1,0:T(8,128)(2,1)S(1)} %get-tuple-element.26), channel_id=1, source_target_pairs={{0,128},{1,385},{128,0},{129,257},{256,384},{257,129},{384,256},{3... | collective-permute-start | bytes 491528 | tf_op jit(solution)/shard_map/ppermute | solution.py:48
  36.9 7.3 %collective-permute-start.4 = (bf16[8,8,1280]{2,1,0:T(8,128)(2,1)S(1)}, bf16[8,8,1280]{2,1,0:T(8,128)(2,1)S(1)}, u32[]{:S(2)}, u32[]{:S(2)}) collective-permute-start(bf16[8,8,1280]{2,1,0:T(8,128)(2,1)S(1)} %get-tuple-element.25), channel_id=1, source_target_pairs={{0,64},{1,67},{64,0},{65,3},{2,66},{3,65},{66,2},{67,1},{4,68},{5,... | collective-permute-start | bytes 491528 | tf_op jit(solution)/shard_map/ppermute | solution.py:39
  41.4 9.2 %collective-permute-start.9 = (bf16[2,8,8,1280]{3,2,1,0:T(8,128)(2,1)S(1)}, bf16[2,8,8,1280]{3,2,1,0:T(8,128)(2,1)S(1)}, u32[]{:S(2)}, u32[]{:S(2)}) collective-permute-start(bf16[2,8,8,1280]{3,2,1,0:T(8,128)(2,1)S(1)} %pad_maximum_fusion.5), channel_id=1, source_target_pairs={{0,384},{1,129},{128,256},{129,1},{256,128},{257,385},{384,0},{385... | collective-permute-start | bytes 983048 | tf_op jit(solution)/shard_map/ppermute | solution.py:48
  44.2 10.0 %collective-permute-start.5 = (bf16[2,8,8,1280]{3,2,1,0:T(8,128)(2,1)S(1)}, bf16[2,8,8,1280]{3,2,1,0:T(8,128)(2,1)S(1)}, u32[]{:S(2)}, u32[]{:S(2)}) collective-permute-start(bf16[2,8,8,1280]{3,2,1,0:T(8,128)(2,1)S(1)} %pad_maximum_fusion.4), channel_id=1, source_target_pairs={{0,66},{1,65},{64,2},{65,1},{2,64},{3,67},{66,0},{67,3},{4,70},{5,... | collective-permute-start | bytes 983048 | tf_op jit(solution)/shard_map/ppermute | solution.py:39
  50.6 15.8 %collective-permute-start.10 = (bf16[4,8,8,1280]{3,2,1,0:T(8,128)(2,1)S(1)}, bf16[4,8,8,1280]{3,2,1,0:T(8,128)(2,1)S(1)}, u32[]{:S(2)}, u32[]{:S(2)}) collective-permute-start(bf16[4,8,8,1280]{3,2,1,0:T(8,128)(2,1)S(1)} %get-tuple-element.20), channel_id=1, source_target_pairs={{0,64},{1,67},{64,0},{65,3},{2,66},{3,65},{66,2},{67,1},{4,68},{5,... | collective-permute-start | bytes 1966088 | tf_op jit(solution)/shard_map/ppermute | solution.py:39
  54.3 14.2 %collective-permute-start.6 = (bf16[4,8,8,1280]{3,2,1,0:T(8,128)(2,1)S(1)}, bf16[4,8,8,1280]{3,2,1,0:T(8,128)(2,1)S(1)}, u32[]{:S(2)}, u32[]{:S(2)}) collective-permute-start(bf16[4,8,8,1280]{3,2,1,0:T(8,128)(2,1)S(1)} %get-tuple-element.22), channel_id=1, source_target_pairs={{0,128},{1,385},{128,0},{129,257},{256,384},{257,129},{384,256},{3... | collective-permute-start | bytes 1966088 | tf_op jit(solution)/shard_map/ppermute | solution.py:48
  66.6 29.1 %collective-permute-start.11 = (bf16[2,4,8,8,1280]{4,3,2,1,0:T(8,128)(2,1)S(1)}, bf16[2,4,8,8,1280]{4,3,2,1,0:T(8,128)(2,1)}, u32[]{:S(2)}, u32[]{:S(2)}) collective-permute-start(bf16[2,4,8,8,1280]{4,3,2,1,0:T(8,128)(2,1)S(1)} %pad_maximum_fusion.1), channel_id=1, source_target_pairs={{0,66},{1,65},{64,2},{65,1},{2,64},{3,67},{66,0},{67,3},{4,70},{5,... | collective-permute-start | bytes 3932168 | tf_op jit(solution)/shard_map/ppermute | solution.py:39
  68.5 3.0 %copy-start.1 = (s32[2,16,20]{2,1,0:T(8,128)S(1)}, s32[2,16,20]{2,1,0:T(8,128)}, u32[]{:S(2)}) copy-start(s32[2,16,20]{2,1,0:T(8,128)} %param.7) | copy-start | bytes 7684
  68.7 29.4 %collective-permute-start.7 = (bf16[2,4,8,8,1280]{4,3,2,1,0:T(8,128)(2,1)S(1)}, bf16[2,4,8,8,1280]{4,3,2,1,0:T(8,128)(2,1)}, u32[]{:S(2)}, u32[]{:S(2)}) collective-permute-start(bf16[2,4,8,8,1280]{4,3,2,1,0:T(8,128)(2,1)S(1)} %pad_maximum_fusion), channel_id=1, source_target_pairs={{0,384},{1,129},{128,256},{129,1},{256,128},{257,385},{384,0},{385... | collective-permute-start | bytes 3932168 | tf_op jit(solution)/shard_map/ppermute | solution.py:48
  72.8 38.6 %collective-permute-start = (bf16[2,7,16,128]{3,2,1,0:T(8,128)(2,1)S(1)}, bf16[2,7,16,128]{3,2,1,0:T(8,128)(2,1)S(1)}, u32[]{:S(2)}, u32[]{:S(2)}) collective-permute-start(bf16[2,7,16,128]{3,2,1,0:T(8,128)(2,1)S(1)} %pad_maximum_fusion.8), channel_id=1, source_target_pairs={{0,4},{4,8},{8,12},{12,16},{16,20},{20,24},{24,28},{28,32},{32,36}... | collective-permute-start | bytes 172040 | tf_op jit(solution)/shard_map/ppermute | solution.py:284
  74.7 58.4 %collective-permute-start.14 = (bf16[2,4,8,8,1280]{4,3,2,1,0:T(8,128)(2,1)S(1)}, bf16[2,4,8,8,1280]{4,3,2,1,0:T(8,128)(2,1)}, u32[]{:S(2)}, u32[]{:S(2)}) collective-permute-start(bf16[2,4,8,8,1280]{4,3,2,1,0:T(8,128)(2,1)S(1)} %pad_maximum_fusion.1), channel_id=1, source_target_pairs={{0,1},{1,0},{2,3},{3,2},{4,5},{5,4},{6,7},{7,6},{8,9},{9,8},{10,11... | collective-permute-start | bytes 3932168 | tf_op jit(solution)/shard_map/ppermute | solution.py:52
  93.7 39.4 %collective-permute-start.12 = (bf16[2,4,8,8,1280]{4,3,2,1,0:T(8,128)(2,1)S(1)}, bf16[2,4,8,8,1280]{4,3,2,1,0:T(8,128)(2,1)}, u32[]{:S(2)}, u32[]{:S(2)}) collective-permute-start(bf16[2,4,8,8,1280]{4,3,2,1,0:T(8,128)(2,1)S(1)} %pad_maximum_fusion), channel_id=1, source_target_pairs={{0,1},{1,0},{2,3},{3,2},{4,5},{5,4},{6,7},{7,6},{8,9},{9,8},{10,11... | collective-permute-start | bytes 3932168 | tf_op jit(solution)/shard_map/ppermute | solution.py:52
  95.7 37.5 %collective-permute-start.15 = (bf16[2,4,8,8,1280]{4,3,2,1,0:T(8,128)(2,1)}, bf16[2,4,8,8,1280]{4,3,2,1,0:T(8,128)(2,1)}, u32[]{:S(2)}, u32[]{:S(2)}) collective-permute-start(bf16[2,4,8,8,1280]{4,3,2,1,0:T(8,128)(2,1)} %collective-permute-done.11), channel_id=1, source_target_pairs={{0,1},{1,0},{2,3},{3,2},{4,5},{5,4},{6,7},{7,6},{8,9},{9,8},{10,11... | collective-permute-start | bytes 3932168 | tf_op jit(solution)/shard_map/ppermute | solution.py:52
  98.1 35.0 %collective-permute-start.13 = (bf16[2,4,8,8,1280]{4,3,2,1,0:T(8,128)(2,1)}, bf16[2,4,8,8,1280]{4,3,2,1,0:T(8,128)(2,1)}, u32[]{:S(2)}, u32[]{:S(2)}) collective-permute-start(bf16[2,4,8,8,1280]{4,3,2,1,0:T(8,128)(2,1)} %collective-permute-done.7), channel_id=1, source_target_pairs={{0,1},{1,0},{2,3},{3,2},{4,5},{5,4},{6,7},{7,6},{8,9},{9,8},{10,11... | collective-permute-start | bytes 3932168 | tf_op jit(solution)/shard_map/ppermute | solution.py:52
  111.4 5.4 %collective-permute-start.1 = (bf16[2,7,16,128]{3,2,1,0:T(8,128)(2,1)S(1)}, bf16[2,7,16,128]{3,2,1,0:T(8,128)(2,1)S(1)}, u32[]{:S(2)}, u32[]{:S(2)}) collective-permute-start(bf16[2,7,16,128]{3,2,1,0:T(8,128)(2,1)S(1)} %pad_maximum_fusion.9), channel_id=1, source_target_pairs={{4,0},{8,4},{12,8},{16,12},{20,16},{24,20},{28,24},{32,28},{36,32}... | collective-permute-start | bytes 172040 | tf_op jit(solution)/shard_map/ppermute | solution.py:287
  117.0 3.7 %collective-permute-start.2 = (bf16[22,7,2,128]{3,2,1,0:T(2,128)(2,1)S(1)}, bf16[22,7,2,128]{3,2,1,0:T(2,128)(2,1)S(1)}, u32[]{:S(2)}, u32[]{:S(2)}) collective-permute-start(bf16[22,7,2,128]{3,2,1,0:T(2,128)(2,1)S(1)} %pad_maximum_fusion.6), channel_id=1, source_target_pairs={{0,1},{1,2},{2,3},{4,5},{5,6},{6,7},{8,9},{9,10},{10,11},{12,13},{... | collective-permute-start | bytes 236552 | tf_op jit(solution)/shard_map/ppermute | solution.py:297
  120.7 7.9 %collective-permute-start.3 = (bf16[22,7,2,128]{3,2,1,0:T(2,128)(2,1)S(1)}, bf16[22,7,2,128]{3,2,1,0:T(2,128)(2,1)S(1)}, u32[]{:S(2)}, u32[]{:S(2)}) collective-permute-start(bf16[22,7,2,128]{3,2,1,0:T(2,128)(2,1)S(1)} %pad_maximum_fusion.7), channel_id=1, source_target_pairs={{1,0},{2,1},{3,2},{5,4},{6,5},{7,6},{9,8},{10,9},{11,10},{13,12},{... | collective-permute-start | bytes 236552 | tf_op jit(solution)/shard_map/ppermute | solution.py:298
  128.7 1.2 copy-start

commit v4 on v3

--- a/solution.py
+++ b/solution.py
@@ -164,7 +164,7 @@
             w = weights[n, :, IN + t * TILE : IN + (t + 1) * TILE]
             d = jnp.dot(h1[0:rows, :], w, preferred_element_type=jnp.float32)
             h2[0:rows, t * TILE : (t + 1) * TILE] = silu(d)
-        pick = mask_ref[...] == want
+        pick = mask_ref[...].reshape(rows, L) == want
         pick = jnp.concatenate([pick, pick], axis=1)
         for t in range(IN // TILE):
             cols = slice(t * TILE, (t + 1) * TILE)
@@ -176,11 +176,17 @@
     lax.fori_loop(0, 2, net, 0)
 
 
-def step_kernel(table, x1, moved1, mask0, mask1, *rest):
+def step_kernel(positions, x1, moved1_any, mask0, mask1, *rest):
     pieces = rest[:8]
     result = rest[8]
-    weights, h1, h2, out, ext, x2, moved2, sems = rest[9:]
-    core = table[16]
+    weights, h1, h2, out, ext, x2, moved2, moved1, sems, moved_sem = rest[9:]
+    at = lax.axis_index("y") * 8 + lax.axis_index("xl") * 4 + lax.axis_index("xh") * 2 + lax.axis_index("core")
+    base = at * 32
+
+    def table(k):
+        return positions[base + k]
+
+    core = table(16)
     for k in range(8):
         net = core if k < 4 else 1 - core
         colour = (k // 2) % 2
@@ -188,8 +194,8 @@
         for p in range(2):
             for q in range(4):
                 j, i = (late + p, q) if colour == 0 else (q, late + p)
-                x = table[net * 8 + i]
-                y = table[net * 8 + 4 + j]
+                x = table(net * 8 + i)
+                y = table(net * 8 + 4 + j)
                 row = pl.multiple_of(y * 256 + (x % 2) * 128 + colour * 64, 64)
                 col = pl.multiple_of((x // 2) * HALF, 128)
                 src = pieces[k].at[pl.ds((p * 4 + q) * 64, 64), :]
@@ -197,6 +203,9 @@
                 sem = (net * 2 + x // 2) * 16 + y * 4 + (x % 2) * 2 + colour
                 pltpu.make_async_copy(src, dst, sems.at[sem]).start()
 
+    arrived = pltpu.make_async_copy(moved1_any, moved1, moved_sem)
+    arrived.start()
+
     def arrive(net, half):
         for k in range(16):
             src = pieces[0].at[pl.ds(0, 64), :]
@@ -204,6 +213,7 @@
             pltpu.make_async_copy(src, dst, sems.at[(net * 2 + half) * 16 + k]).wait()
 
     networks(x1, mask0, weights, h1, h2, out, ROWS, arrive)
+    arrived.wait()
 
     def spread(c, carry):
         row = pl.multiple_of(c * R, R)
@@ -217,7 +227,7 @@
         for k, (at, flag) in enumerate(((7, 17), (8 + R, 18))):
             row = MAIN + k * C + c
             value = moved1[row : row + 1, :] + out[row : row + 1, :]
-            value = jnp.where(table[flag] == 1, value, jnp.zeros_like(value))
+            value = jnp.where(table(flag) == 1, value, jnp.zeros_like(value))
             for f in range(F):
                 ext[c + 1, f, at : at + 1, :] = value[:, lanes(f)]
 
@@ -262,13 +272,9 @@
 
 
 def shards(fields, day_mask, w_in, w_mid, w_out):
-    y, xl, xh, core = (lax.axis_index(a) for a in ("y", "xl", "xh", "core"))
-    at = ((y * 2 + xl) * 2 + xh) * 2 + core
-    table = lax.dynamic_slice(jnp.asarray(position_table()), (at, 0), (1, 32))[0]
-
+    xh, core = lax.axis_index("xh"), lax.axis_index("core")
     joined = jnp.concatenate([w_in, w_mid, w_out], axis=2)
     block = lax.dynamic_slice(joined, (core, 0, xh * HALF), (1, 8, HALF))[0]
-    block, table = lax.optimization_barrier((block, table))
     pieces = gather_weights(block)
 
     ft = fields.transpose(1, 2, 0, 3)
@@ -310,7 +316,7 @@
             pltpu.VMEM((C + 4, F, 32, L), jnp.float32),
             pltpu.VMEM((WIDE, F, 8, L), jnp.float32),
         ],
-        compiler_params=pltpu.CompilerParams(vmem_limit_bytes=10 << 20),
+        compiler_params=pltpu.CompilerParams(vmem_limit_bytes=4 << 20),
         name="prepare",
     )
     moved1, x1, mask0 = prepare(ft, masks[0], lon_w, lon_e, lat_s, lat_n)
@@ -319,7 +325,9 @@
         step_kernel,
         out_shape=jax.ShapeDtypeStruct((C, F, R, L), jnp.float32),
         in_specs=[pl.BlockSpec(memory_space=pltpu.SMEM)]
-        + vmem(4)
+        + vmem(1)
+        + [pl.BlockSpec(memory_space=pl.ANY)]
+        + vmem(2)
         + [pl.BlockSpec(memory_space=pl.ANY)] * 8,
         out_specs=pl.BlockSpec(memory_space=pltpu.VMEM),
         scratch_shapes=[
@@ -330,11 +338,13 @@
             pltpu.VMEM((WIDE, F, 32, L), jnp.float32),
             pltpu.VMEM((C * R, IN), jnp.bfloat16),
             pltpu.VMEM((C * R, IN), jnp.float32),
+            pltpu.VMEM((ROWS, IN), jnp.float32),
             pltpu.SemaphoreType.DMA((64,)),
+            pltpu.SemaphoreType.DMA,
         ],
         compiler_params=pltpu.CompilerParams(vmem_limit_bytes=26 << 20),
         name="steps",
-    )(table, x1, moved1, mask0, masks[1].reshape(C * R, L), *pieces)
+    )(position_table().reshape(-1), x1, moved1, mask0, masks[1], *pieces)
     return result.transpose(2, 0, 1, 3)
 
 

time: 153 us -> 152 us (level)
    ppermute x4, waiting for transfers between devices: 4.42 us -> 8.5 us  [y_exchange(): return lax.ppermute(a, ('y', 'core'), pairs)]
    ppermute x4, waiting for transfers between devices: 8.42 us -> 4.59 us  [x_exchange(): return lax.ppermute(a, ('xl', 'xh', 'core'), pairs)]
    ppermute x4, starting transfers between devices: 14 us -> 12.3 us  [y_exchange(): return lax.ppermute(a, ('y', 'core'), pairs)]
where the time goes in v4:
time: 152 us; the launch traced here: 151 us
  starting transfers between devices  68.6 us (45%)
  blocking collectives  30.8 us (20%)
  waiting for transfers between devices  23.5 us (15%)
  Pallas kernels  22 us (14%)
  local copies, waits for them, and re-layouts  4.68 us (3%)
  other arithmetic  1.52 us (1%)
    ppermute x4, starting transfers between devices, core_swap(): return lax.ppermute(a, 'core', [(0, 1), (1, 0)])  34.7 us
    all_gather x1, blocking collectives, gather_weights(): z = lax.all_gather(block, 'z', axis=0)  30.8 us
    pallas_call x1, Pallas kernels, shards(): pl.pallas_call(step_kernel, out_shape=jax.ShapeDtypeStruct((C, F, R, L),...  18.8 us
    ppermute x4, starting transfers between devices, x_exchange(): return lax.ppermute(a, ('xl', 'xh', 'core'), pairs)  13.3 us
    ppermute x4, starting transfers between devices, y_exchange(): return lax.ppermute(a, ('y', 'core'), pairs)  12.3 us
    ppermute x4, waiting for transfers between devices, y_exchange(): return lax.ppermute(a, ('y', 'core'), pairs)  8.5 us
    ppermute x1, waiting for transfers between devices, shards(): lat_n = lax.ppermute(wide(slice(0, 2)), LAT, [(i + 1, i) for i in ends])  5.77 us
    ppermute x4, waiting for transfers between devices, x_exchange(): return lax.ppermute(a, ('xl', 'xh', 'core'), pairs)  4.59 us
  transfers between devices with their start and end apart: 16, of which 6 were waited for; matrix products, arithmetic and copies ran while one was open for 3% of the time, Pallas kernels for 2%

profile of v4, /device:TPU:1, one launch (start us, length us, event | category | flops | bytes accessed | tf_op | source)
XLA Modules:
  0.0 151.4 jit_solution(14273486874109531721)
XLA Ops:
  0.0 0.7 fusion.1
  0.7 30.8 %all_gather.3 = bf16[16,8,1280]{2,1,0:T(8,128)(2,1)S(1)} all-gather(bf16[1,8,1280]{2,1,0:T(8,128)(2,1)S(1)} %fusion.1), channel_id=1, replica_groups=mesh['y'=4,'xl'=2,'z'=16,'xh'=2,'core'=2] {'z'}, dimensions={0}, use_global_device_ids=true | all-gather | bytes 348160 | tf_op jit(solution)/shard_map/all_gather | solution.py:56
  31.6 4.4 %collective-permute-start.4 = (bf16[8,8,1280]{2,1,0:T(8,128)(2,1)S(1)}, bf16[8,8,1280]{2,1,0:T(8,128)(2,1)S(1)}, u32[]{:S(2)}, u32[]{:S(2)}) collective-permute-start(bf16[8,8,1280]{2,1,0:T(8,128)(2,1)S(1)} %get-tuple-element.22), channel_id=1, source_target_pairs={{0,64},{1,67},{64,0},{65,3},{2,66},{3,65},{66,2},{67,1},{4,68},{5,... | collective-permute-start | bytes 491528 | tf_op jit(solution)/shard_map/ppermute | solution.py:39
  36.0 4.6 %collective-permute-start.8 = (bf16[8,8,1280]{2,1,0:T(8,128)(2,1)S(1)}, bf16[8,8,1280]{2,1,0:T(8,128)(2,1)S(1)}, u32[]{:S(2)}, u32[]{:S(2)}) collective-permute-start(bf16[8,8,1280]{2,1,0:T(8,128)(2,1)S(1)} %get-tuple-element.21), channel_id=1, source_target_pairs={{0,128},{1,385},{128,0},{129,257},{256,384},{257,129},{384,256},{3... | collective-permute-start | bytes 491528 | tf_op jit(solution)/shard_map/ppermute | solution.py:48
  40.7 1.9 %collective-permute-start.5 = (bf16[2,8,8,1280]{3,2,1,0:T(8,128)(2,1)S(1)}, bf16[2,8,8,1280]{3,2,1,0:T(8,128)(2,1)S(1)}, u32[]{:S(2)}, u32[]{:S(2)}) collective-permute-start(bf16[2,8,8,1280]{3,2,1,0:T(8,128)(2,1)S(1)} %pad_maximum_fusion.4), channel_id=1, source_target_pairs={{0,66},{1,65},{64,2},{65,1},{2,64},{3,67},{66,0},{67,3},{4,70},{5,... | collective-permute-start | bytes 983048 | tf_op jit(solution)/shard_map/ppermute | solution.py:39
  42.6 0.7 collective-permute-done.8
  43.3 1.9 %collective-permute-start.9 = (bf16[2,8,8,1280]{3,2,1,0:T(8,128)(2,1)S(1)}, bf16[2,8,8,1280]{3,2,1,0:T(8,128)(2,1)S(1)}, u32[]{:S(2)}, u32[]{:S(2)}) collective-permute-start(bf16[2,8,8,1280]{3,2,1,0:T(8,128)(2,1)S(1)} %pad_maximum_fusion.5), channel_id=1, source_target_pairs={{0,384},{1,129},{128,256},{129,1},{256,128},{257,385},{384,0},{385... | collective-permute-start | bytes 983048 | tf_op jit(solution)/shard_map/ppermute | solution.py:48
  45.3 4.6 %collective-permute-done.5 = bf16[2,8,8,1280]{3,2,1,0:T(8,128)(2,1)S(1)} collective-permute-done((bf16[2,8,8,1280]{3,2,1,0:T(8,128)(2,1)S(1)}, bf16[2,8,8,1280]{3,2,1,0:T(8,128)(2,1)S(1)}, u32[]{:S(2)}, u32[]{:S(2)}) %collective-permute-start.5) | collective-permute-done | bytes 327712 | tf_op jit(solution)/shard_map/ppermute | solution.py:39
  49.9 0.1 fusion.5
  50.0 3.8 %collective-permute-start.6 = (bf16[4,8,8,1280]{3,2,1,0:T(8,128)(2,1)S(1)}, bf16[4,8,8,1280]{3,2,1,0:T(8,128)(2,1)S(1)}, u32[]{:S(2)}, u32[]{:S(2)}) collective-permute-start(bf16[4,8,8,1280]{3,2,1,0:T(8,128)(2,1)S(1)} %get-tuple-element.18), channel_id=1, source_target_pairs={{0,128},{1,385},{128,0},{129,257},{256,384},{257,129},{384,256},{3... | collective-permute-start | bytes 1966088 | tf_op jit(solution)/shard_map/ppermute | solution.py:48
  53.7 0.1 fusion.4
  53.9 4.4 %collective-permute-start.10 = (bf16[4,8,8,1280]{3,2,1,0:T(8,128)(2,1)S(1)}, bf16[4,8,8,1280]{3,2,1,0:T(8,128)(2,1)S(1)}, u32[]{:S(2)}, u32[]{:S(2)}) collective-permute-start(bf16[4,8,8,1280]{3,2,1,0:T(8,128)(2,1)S(1)} %get-tuple-element.16), channel_id=1, source_target_pairs={{0,64},{1,67},{64,0},{65,3},{2,66},{3,65},{66,2},{67,1},{4,68},{5,... | collective-permute-start | bytes 1966088 | tf_op jit(solution)/shard_map/ppermute | solution.py:39
  58.3 7.8 %collective-permute-done.6 = bf16[4,8,8,1280]{3,2,1,0:T(8,128)(2,1)S(1)} collective-permute-done((bf16[4,8,8,1280]{3,2,1,0:T(8,128)(2,1)S(1)}, bf16[4,8,8,1280]{3,2,1,0:T(8,128)(2,1)S(1)}, u32[]{:S(2)}, u32[]{:S(2)}) %collective-permute-start.6) | collective-permute-done | bytes 655392 | tf_op jit(solution)/shard_map/ppermute | solution.py:48
  66.0 0.1 pad_maximum_fusion
  66.2 1.9 %collective-permute-start.7 = (bf16[2,4,8,8,1280]{4,3,2,1,0:T(8,128)(2,1)S(1)}, bf16[2,4,8,8,1280]{4,3,2,1,0:T(8,128)(2,1)}, u32[]{:S(2)}, u32[]{:S(2)}) collective-permute-start(bf16[2,4,8,8,1280]{4,3,2,1,0:T(8,128)(2,1)S(1)} %pad_maximum_fusion), channel_id=1, source_target_pairs={{0,384},{1,129},{128,256},{129,1},{256,128},{257,385},{384,0},{385... | collective-permute-start | bytes 3932168 | tf_op jit(solution)/shard_map/ppermute | solution.py:48
  68.1 0.1 pad_maximum_fusion.1
  68.2 2.6 %collective-permute-start.11 = (bf16[2,4,8,8,1280]{4,3,2,1,0:T(8,128)(2,1)S(1)}, bf16[2,4,8,8,1280]{4,3,2,1,0:T(8,128)(2,1)}, u32[]{:S(2)}, u32[]{:S(2)}) collective-permute-start(bf16[2,4,8,8,1280]{4,3,2,1,0:T(8,128)(2,1)S(1)} %pad_maximum_fusion.1), channel_id=1, source_target_pairs={{0,66},{1,65},{64,2},{65,1},{2,64},{3,67},{66,0},{67,3},{4,70},{5,... | collective-permute-start | bytes 3932168 | tf_op jit(solution)/shard_map/ppermute | solution.py:39
  70.8 0.1 fusion.10
  70.9 0.1 copy.14
  71.0 1.0 fusion.7
  72.0 0.1 broadcast_in_dim.22
  72.1 1.9 %collective-permute-start = (bf16[2,7,16,128]{3,2,1,0:T(8,128)(2,1)S(1)}, bf16[2,7,16,128]{3,2,1,0:T(8,128)(2,1)S(1)}, u32[]{:S(2)}, u32[]{:S(2)}) collective-permute-start(bf16[2,7,16,128]{3,2,1,0:T(8,128)(2,1)S(1)} %pad_maximum_fusion.8), channel_id=1, source_target_pairs={{0,4},{4,8},{8,12},{12,16},{16,20},{20,24},{24,28},{28,32},{32,36}... | collective-permute-start | bytes 172040 | tf_op jit(solution)/shard_map/ppermute | solution.py:290
  74.0 19.1 %collective-permute-start.12 = (bf16[2,4,8,8,1280]{4,3,2,1,0:T(8,128)(2,1)S(1)}, bf16[2,4,8,8,1280]{4,3,2,1,0:T(8,128)(2,1)}, u32[]{:S(2)}, u32[]{:S(2)}) collective-permute-start(bf16[2,4,8,8,1280]{4,3,2,1,0:T(8,128)(2,1)S(1)} %pad_maximum_fusion), channel_id=1, source_target_pairs={{0,1},{1,0},{2,3},{3,2},{4,5},{5,4},{6,7},{7,6},{8,9},{9,8},{10,11... | collective-permute-start | bytes 3932168 | tf_op jit(solution)/shard_map/ppermute | solution.py:52
  93.1 1.9 %collective-permute-start.14 = (bf16[2,4,8,8,1280]{4,3,2,1,0:T(8,128)(2,1)S(1)}, bf16[2,4,8,8,1280]{4,3,2,1,0:T(8,128)(2,1)}, u32[]{:S(2)}, u32[]{:S(2)}) collective-permute-start(bf16[2,4,8,8,1280]{4,3,2,1,0:T(8,128)(2,1)S(1)} %pad_maximum_fusion.1), channel_id=1, source_target_pairs={{0,1},{1,0},{2,3},{3,2},{4,5},{5,4},{6,7},{7,6},{8,9},{9,8},{10,11... | collective-permute-start | bytes 3932168 | tf_op jit(solution)/shard_map/ppermute | solution.py:52
  95.0 2.4 %collective-permute-start.13 = (bf16[2,4,8,8,1280]{4,3,2,1,0:T(8,128)(2,1)}, bf16[2,4,8,8,1280]{4,3,2,1,0:T(8,128)(2,1)}, u32[]{:S(2)}, u32[]{:S(2)}) collective-permute-start(bf16[2,4,8,8,1280]{4,3,2,1,0:T(8,128)(2,1)} %collective-permute-done.7), channel_id=1, source_target_pairs={{0,1},{1,0},{2,3},{3,2},{4,5},{5,4},{6,7},{7,6},{8,9},{9,8},{10,11... | collective-permute-start | bytes 3932168 | tf_op jit(solution)/shard_map/ppermute | solution.py:52
  97.4 11.3 %collective-permute-start.15 = (bf16[2,4,8,8,1280]{4,3,2,1,0:T(8,128)(2,1)}, bf16[2,4,8,8,1280]{4,3,2,1,0:T(8,128)(2,1)}, u32[]{:S(2)}, u32[]{:S(2)}) collective-permute-start(bf16[2,4,8,8,1280]{4,3,2,1,0:T(8,128)(2,1)} %collective-permute-done.11), channel_id=1, source_target_pairs={{0,1},{1,0},{2,3},{3,2},{4,5},{5,4},{6,7},{7,6},{8,9},{9,8},{10,11... | collective-permute-start | bytes 3932168 | tf_op jit(solution)/shard_map/ppermute | solution.py:52
  108.8 0.1 copy.15
  108.9 0.1 copy.17
  109.0 0.1 copy.16
  109.1 1.3 fusion.6
  110.4 0.1 broadcast_in_dim.23
  110.5 1.9 %collective-permute-start.1 = (bf16[2,7,16,128]{3,2,1,0:T(8,128)(2,1)S(1)}, bf16[2,7,16,128]{3,2,1,0:T(8,128)(2,1)S(1)}, u32[]{:S(2)}, u32[]{:S(2)}) collective-permute-start(bf16[2,7,16,128]{3,2,1,0:T(8,128)(2,1)S(1)} %pad_maximum_fusion.9), channel_id=1, source_target_pairs={{4,0},{8,4},{12,8},{16,12},{20,16},{24,20},{28,24},{32,28},{36,32}... | collective-permute-start | bytes 172040 | tf_op jit(solution)/shard_map/ppermute | solution.py:293
  112.4 3.4 %collective-permute-done.1.lon_e = bf16[2,7,16,128]{3,2,1,0:T(8,128)(2,1)S(1)} collective-permute-done((bf16[2,7,16,128]{3,2,1,0:T(8,128)(2,1)S(1)}, bf16[2,7,16,128]{3,2,1,0:T(8,128)(2,1)S(1)}, u32[]{:S(2)}, u32[]{:S(2)}) %collective-permute-start.1) | collective-permute-done | bytes 57376 | tf_op jit(solution)/shard_map/ppermute | solution.py:293
  115.8 0.1 convert_element_type.50
  115.9 0.1 pad_maximum_fusion.6
  116.1 2.5 %collective-permute-start.2 = (bf16[22,7,2,128]{3,2,1,0:T(2,128)(2,1)S(1)}, bf16[22,7,2,128]{3,2,1,0:T(2,128)(2,1)S(1)}, u32[]{:S(2)}, u32[]{:S(2)}) collective-permute-start(bf16[22,7,2,128]{3,2,1,0:T(2,128)(2,1)S(1)} %pad_maximum_fusion.6), channel_id=1, source_target_pairs={{0,1},{1,2},{2,3},{4,5},{5,6},{6,7},{8,9},{9,10},{10,11},{12,13},{... | collective-permute-start | bytes 236552 | tf_op jit(solution)/shard_map/ppermute | solution.py:303
  118.6 0.1 convert_element_type.52
  118.7 0.1 pad_maximum_fusion.7
  118.9 1.2 collective-permute-done.2.lat_s
  120.1 1.9 %collective-permute-start.3 = (bf16[22,7,2,128]{3,2,1,0:T(2,128)(2,1)S(1)}, bf16[22,7,2,128]{3,2,1,0:T(2,128)(2,1)S(1)}, u32[]{:S(2)}, u32[]{:S(2)}) collective-permute-start(bf16[22,7,2,128]{3,2,1,0:T(2,128)(2,1)S(1)} %pad_maximum_fusion.7), channel_id=1, source_target_pairs={{1,0},{2,1},{3,2},{5,4},{6,5},{7,6},{9,8},{10,9},{11,10},{13,12},{... | collective-permute-start | bytes 236552 | tf_op jit(solution)/shard_map/ppermute | solution.py:304
  122.0 0.1 copy.18
  122.1 0.1 copy.13
  122.2 5.8 %collective-permute-done.3.lat_n = bf16[22,7,2,128]{3,2,1,0:T(2,128)(2,1)S(1)} collective-permute-done((bf16[22,7,2,128]{3,2,1,0:T(2,128)(2,1)S(1)}, bf16[22,7,2,128]{3,2,1,0:T(2,128)(2,1)S(1)}, u32[]{:S(2)}, u32[]{:S(2)}) %collective-permute-start.3) | collective-permute-done | bytes 78880 | tf_op jit(solution)/shard_map/ppermute | solution.py:304
  127.9 0.1 broadcast_in_dim.21.mask
  128.0 1.2 copy-done
  129.2 3.2 %prepare.1 = (f32[400,768]{1,0:T(8,128)S(1)}, bf16[400,768]{1,0:T(8,128)(2,1)S(1)}, f32[400,128]{1,0:T(8,128)S(1)}) custom-call(f32[20,6,16,128]{3,2,1,0:T(8,128)S(1)} %bitcast.38, f32[20,16,128]{2,1,0:T(8,128)S(1)} %broadcast_in_dim.21.mask, bf16[2,7,16,128]{3,2,1,0:T(8,128)(2,1)S(1)} %collective-permute-done.lon_w, ...), custom_call_target="tpu_custom_call" | custom-call | tf_op jit(solution)/shard_map/prepare/pallas_call | solution.py:322
  132.5 0.1 broadcast_in_dim.25.mask1
  132.6 18.8 %steps.1 = f32[20,6,16,128]{3,2,1,0:T(8,128)} custom-call(s32[1024]{0:T(1024)S(1)} %copy-done.1, bf16[400,768]{1,0:T(8,128)(2,1)S(1)} %get-tuple-element.8.x1, f32[400,768]{1,0:T(8,128)S(1)} %get-tuple-element.9.moved1_any, f32[400,128]{1,0:T(8,128)S(1)} %get-tuple-element.10.mask0, f32[20,16,128]{2,1,0:T(8,128)S(1)} %broadcast_in_dim.25.mask1, ...), custom_call_target="tpu_custom_call" | custom-call | tf_op jit(solution)/shard_map/steps/pallas_call | solution.py:324
  (26 shorter events, 0.2 us)
Async XLA Ops:
  31.6 9.1 %collective-permute-start.4 = (bf16[8,8,1280]{2,1,0:T(8,128)(2,1)S(1)}, bf16[8,8,1280]{2,1,0:T(8,128)(2,1)S(1)}, u32[]{:S(2)}, u32[]{:S(2)}) collective-permute-start(bf16[8,8,1280]{2,1,0:T(8,128)(2,1)S(1)} %get-tuple-element.22), channel_id=1, source_target_pairs={{0,64},{1,67},{64,0},{65,3},{2,66},{3,65},{66,2},{67,1},{4,68},{5,... | collective-permute-start | bytes 491528 | tf_op jit(solution)/shard_map/ppermute | solution.py:39
  36.0 7.3 %collective-permute-start.8 = (bf16[8,8,1280]{2,1,0:T(8,128)(2,1)S(1)}, bf16[8,8,1280]{2,1,0:T(8,128)(2,1)S(1)}, u32[]{:S(2)}, u32[]{:S(2)}) collective-permute-start(bf16[8,8,1280]{2,1,0:T(8,128)(2,1)S(1)} %get-tuple-element.21), channel_id=1, source_target_pairs={{0,128},{1,385},{128,0},{129,257},{256,384},{257,129},{384,256},{3... | collective-permute-start | bytes 491528 | tf_op jit(solution)/shard_map/ppermute | solution.py:48
  40.7 9.2 %collective-permute-start.5 = (bf16[2,8,8,1280]{3,2,1,0:T(8,128)(2,1)S(1)}, bf16[2,8,8,1280]{3,2,1,0:T(8,128)(2,1)S(1)}, u32[]{:S(2)}, u32[]{:S(2)}) collective-permute-start(bf16[2,8,8,1280]{3,2,1,0:T(8,128)(2,1)S(1)} %pad_maximum_fusion.4), channel_id=1, source_target_pairs={{0,66},{1,65},{64,2},{65,1},{2,64},{3,67},{66,0},{67,3},{4,70},{5,... | collective-permute-start | bytes 983048 | tf_op jit(solution)/shard_map/ppermute | solution.py:39
  43.3 10.4 %collective-permute-start.9 = (bf16[2,8,8,1280]{3,2,1,0:T(8,128)(2,1)S(1)}, bf16[2,8,8,1280]{3,2,1,0:T(8,128)(2,1)S(1)}, u32[]{:S(2)}, u32[]{:S(2)}) collective-permute-start(bf16[2,8,8,1280]{3,2,1,0:T(8,128)(2,1)S(1)} %pad_maximum_fusion.5), channel_id=1, source_target_pairs={{0,384},{1,129},{128,256},{129,1},{256,128},{257,385},{384,0},{385... | collective-permute-start | bytes 983048 | tf_op jit(solution)/shard_map/ppermute | solution.py:48
  50.0 16.1 %collective-permute-start.6 = (bf16[4,8,8,1280]{3,2,1,0:T(8,128)(2,1)S(1)}, bf16[4,8,8,1280]{3,2,1,0:T(8,128)(2,1)S(1)}, u32[]{:S(2)}, u32[]{:S(2)}) collective-permute-start(bf16[4,8,8,1280]{3,2,1,0:T(8,128)(2,1)S(1)} %get-tuple-element.18), channel_id=1, source_target_pairs={{0,128},{1,385},{128,0},{129,257},{256,384},{257,129},{384,256},{3... | collective-permute-start | bytes 1966088 | tf_op jit(solution)/shard_map/ppermute | solution.py:48
  53.9 14.2 %collective-permute-start.10 = (bf16[4,8,8,1280]{3,2,1,0:T(8,128)(2,1)S(1)}, bf16[4,8,8,1280]{3,2,1,0:T(8,128)(2,1)S(1)}, u32[]{:S(2)}, u32[]{:S(2)}) collective-permute-start(bf16[4,8,8,1280]{3,2,1,0:T(8,128)(2,1)S(1)} %get-tuple-element.16), channel_id=1, source_target_pairs={{0,64},{1,67},{64,0},{65,3},{2,66},{3,65},{66,2},{67,1},{4,68},{5,... | collective-permute-start | bytes 1966088 | tf_op jit(solution)/shard_map/ppermute | solution.py:39
  66.2 28.8 %collective-permute-start.7 = (bf16[2,4,8,8,1280]{4,3,2,1,0:T(8,128)(2,1)S(1)}, bf16[2,4,8,8,1280]{4,3,2,1,0:T(8,128)(2,1)}, u32[]{:S(2)}, u32[]{:S(2)}) collective-permute-start(bf16[2,4,8,8,1280]{4,3,2,1,0:T(8,128)(2,1)S(1)} %pad_maximum_fusion), channel_id=1, source_target_pairs={{0,384},{1,129},{128,256},{129,1},{256,128},{257,385},{384,0},{385... | collective-permute-start | bytes 3932168 | tf_op jit(solution)/shard_map/ppermute | solution.py:48
  68.1 2.7 %copy-start.2 = (s32[2,16,20]{2,1,0:T(8,128)S(1)}, s32[2,16,20]{2,1,0:T(8,128)}, u32[]{:S(2)}) copy-start(s32[2,16,20]{2,1,0:T(8,128)} %param.7) | copy-start | bytes 7684
  68.2 29.2 %collective-permute-start.11 = (bf16[2,4,8,8,1280]{4,3,2,1,0:T(8,128)(2,1)S(1)}, bf16[2,4,8,8,1280]{4,3,2,1,0:T(8,128)(2,1)}, u32[]{:S(2)}, u32[]{:S(2)}) collective-permute-start(bf16[2,4,8,8,1280]{4,3,2,1,0:T(8,128)(2,1)S(1)} %pad_maximum_fusion.1), channel_id=1, source_target_pairs={{0,66},{1,65},{64,2},{65,1},{2,64},{3,67},{66,0},{67,3},{4,70},{5,... | collective-permute-start | bytes 3932168 | tf_op jit(solution)/shard_map/ppermute | solution.py:39
  72.1 38.4 %collective-permute-start = (bf16[2,7,16,128]{3,2,1,0:T(8,128)(2,1)S(1)}, bf16[2,7,16,128]{3,2,1,0:T(8,128)(2,1)S(1)}, u32[]{:S(2)}, u32[]{:S(2)}) collective-permute-start(bf16[2,7,16,128]{3,2,1,0:T(8,128)(2,1)S(1)} %pad_maximum_fusion.8), channel_id=1, source_target_pairs={{0,4},{4,8},{8,12},{12,16},{16,20},{20,24},{24,28},{28,32},{32,36}... | collective-permute-start | bytes 172040 | tf_op jit(solution)/shard_map/ppermute | solution.py:290
  74.0 58.5 %collective-permute-start.12 = (bf16[2,4,8,8,1280]{4,3,2,1,0:T(8,128)(2,1)S(1)}, bf16[2,4,8,8,1280]{4,3,2,1,0:T(8,128)(2,1)}, u32[]{:S(2)}, u32[]{:S(2)}) collective-permute-start(bf16[2,4,8,8,1280]{4,3,2,1,0:T(8,128)(2,1)S(1)} %pad_maximum_fusion), channel_id=1, source_target_pairs={{0,1},{1,0},{2,3},{3,2},{4,5},{5,4},{6,7},{7,6},{8,9},{9,8},{10,11... | collective-permute-start | bytes 3932168 | tf_op jit(solution)/shard_map/ppermute | solution.py:52
  93.1 39.4 %collective-permute-start.14 = (bf16[2,4,8,8,1280]{4,3,2,1,0:T(8,128)(2,1)S(1)}, bf16[2,4,8,8,1280]{4,3,2,1,0:T(8,128)(2,1)}, u32[]{:S(2)}, u32[]{:S(2)}) collective-permute-start(bf16[2,4,8,8,1280]{4,3,2,1,0:T(8,128)(2,1)S(1)} %pad_maximum_fusion.1), channel_id=1, source_target_pairs={{0,1},{1,0},{2,3},{3,2},{4,5},{5,4},{6,7},{7,6},{8,9},{9,8},{10,11... | collective-permute-start | bytes 3932168 | tf_op jit(solution)/shard_map/ppermute | solution.py:52
  95.0 37.5 %collective-permute-start.13 = (bf16[2,4,8,8,1280]{4,3,2,1,0:T(8,128)(2,1)}, bf16[2,4,8,8,1280]{4,3,2,1,0:T(8,128)(2,1)}, u32[]{:S(2)}, u32[]{:S(2)}) collective-permute-start(bf16[2,4,8,8,1280]{4,3,2,1,0:T(8,128)(2,1)} %collective-permute-done.7), channel_id=1, source_target_pairs={{0,1},{1,0},{2,3},{3,2},{4,5},{5,4},{6,7},{7,6},{8,9},{9,8},{10,11... | collective-permute-start | bytes 3932168 | tf_op jit(solution)/shard_map/ppermute | solution.py:52
  97.4 35.1 %collective-permute-start.15 = (bf16[2,4,8,8,1280]{4,3,2,1,0:T(8,128)(2,1)}, bf16[2,4,8,8,1280]{4,3,2,1,0:T(8,128)(2,1)}, u32[]{:S(2)}, u32[]{:S(2)}) collective-permute-start(bf16[2,4,8,8,1280]{4,3,2,1,0:T(8,128)(2,1)} %collective-permute-done.11), channel_id=1, source_target_pairs={{0,1},{1,0},{2,3},{3,2},{4,5},{5,4},{6,7},{7,6},{8,9},{9,8},{10,11... | collective-permute-start | bytes 3932168 | tf_op jit(solution)/shard_map/ppermute | solution.py:52
  109.1 23.5 %copy-start.1 = (s32[1024]{0:T(1024)S(1)}, s32[1024]{0:T(1024)}, u32[]{:S(2)}) copy-start(s32[1024]{0:T(1024)} %constant.16.clone.positions) | copy-start | bytes 12292
  110.5 5.4 %collective-permute-start.1 = (bf16[2,7,16,128]{3,2,1,0:T(8,128)(2,1)S(1)}, bf16[2,7,16,128]{3,2,1,0:T(8,128)(2,1)S(1)}, u32[]{:S(2)}, u32[]{:S(2)}) collective-permute-start(bf16[2,7,16,128]{3,2,1,0:T(8,128)(2,1)S(1)} %pad_maximum_fusion.9), channel_id=1, source_target_pairs={{4,0},{8,4},{12,8},{16,12},{20,16},{24,20},{28,24},{32,28},{36,32}... | collective-permute-start | bytes 172040 | tf_op jit(solution)/shard_map/ppermute | solution.py:293
  116.1 4.0 %collective-permute-start.2 = (bf16[22,7,2,128]{3,2,1,0:T(2,128)(2,1)S(1)}, bf16[22,7,2,128]{3,2,1,0:T(2,128)(2,1)S(1)}, u32[]{:S(2)}, u32[]{:S(2)}) collective-permute-start(bf16[22,7,2,128]{3,2,1,0:T(2,128)(2,1)S(1)} %pad_maximum_fusion.6), channel_id=1, source_target_pairs={{0,1},{1,2},{2,3},{4,5},{5,6},{6,7},{8,9},{9,10},{10,11},{12,13},{... | collective-permute-start | bytes 236552 | tf_op jit(solution)/shard_map/ppermute | solution.py:303
  120.1 7.9 %collective-permute-start.3 = (bf16[22,7,2,128]{3,2,1,0:T(2,128)(2,1)S(1)}, bf16[22,7,2,128]{3,2,1,0:T(2,128)(2,1)S(1)}, u32[]{:S(2)}, u32[]{:S(2)}) collective-permute-start(bf16[22,7,2,128]{3,2,1,0:T(2,128)(2,1)S(1)} %pad_maximum_fusion.7), channel_id=1, source_target_pairs={{1,0},{2,1},{3,2},{5,4},{6,5},{7,6},{9,8},{10,9},{11,10},{13,12},{... | collective-permute-start | bytes 236552 | tf_op jit(solution)/shard_map/ppermute | solution.py:304
  128.0 1.2 copy-start

commit v5 on v4

--- a/solution.py
+++ b/solution.py
@@ -22,6 +22,7 @@
 HID = 1024
 HALF = 1280
 TILE = 256
+BLOCK = 128
 
 
 def ring_partner(i, kind):
@@ -30,22 +31,20 @@
     return (i + 1) % 4 if i % 2 else (i - 1) % 4
 
 
-def x_exchange(a, rnd):
+def exchange(a, kind, first):
     pairs = []
-    for x in range(4):
-        for c in range(2):
-            p = ring_partner(x, c if rnd == 0 else 1 - c)
-            pairs.append(((x % 2) * 4 + (x // 2) * 2 + c, (p % 2) * 4 + (p // 2) * 2 + c))
-    return lax.ppermute(a, ("xl", "xh", "core"), pairs)
-
-
-def y_exchange(a, rnd):
-    pairs = []
-    for y in range(4):
-        for c in range(2):
-            p = ring_partner(y, c if rnd == 0 else 1 - c)
-            pairs.append((y * 2 + c, p * 2 + c))
-    return lax.ppermute(a, ("y", "core"), pairs)
+    for y, xl, xh, core in np.ndindex(4, 2, 2, 2):
+        x = xh * 2 + xl
+        if (core == 0) == (first == "x"):
+            px, py = ring_partner(x, kind), y
+        else:
+            px, py = x, ring_partner(y, kind)
+        pairs.append((device_at(y, x, core), device_at(py, px, core)))
+    return lax.ppermute(a, ("y", "xl", "xh", "core"), pairs)
+
+
+def device_at(y, x, core):
+    return ((y * 2 + x % 2) * 2 + x // 2) * 2 + core
 
 
 def core_swap(a):
@@ -54,17 +53,15 @@
 
 def gather_weights(block):
     z = lax.all_gather(block, "z", axis=0)
-    a, b = z[:8], z[8:]
-    a1, b1 = x_exchange(a, 0), y_exchange(b, 0)
-    a2, b2 = jnp.stack([a, a1]), jnp.stack([b, b1])
-    a3, b3 = x_exchange(a2, 1), y_exchange(b2, 1)
-    a4, b4 = jnp.concatenate([a2, a3]), jnp.concatenate([b2, b3])
-    a5, b5 = y_exchange(a4, 0), x_exchange(b4, 0)
-    a6, b6 = jnp.stack([a4, a5]), jnp.stack([b4, b5])
-    a7, b7 = y_exchange(a6, 1), x_exchange(b6, 1)
+    z1 = exchange(z, 0, "x")
+    a = jnp.stack([z, z1])
+    b = exchange(a, 1, "x")
+    a5, b5 = exchange(a, 0, "y"), exchange(b, 1, "y")
+    a6, b6 = jnp.stack([a, a5]), jnp.stack([b, b5])
+    a7, b7 = exchange(a6, 1, "y"), exchange(b6, 0, "y")
     ca6, cb6 = core_swap(a6), core_swap(b6)
     ca7, cb7 = core_swap(a7), core_swap(b7)
-    return [p.reshape(8 * 64, HALF) for p in (a6, a7, b6, b7, ca6, ca7, cb6, cb7)]
+    return [p.reshape(4 * BLOCK, HALF) for p in (a6, a7, b6, b7, ca6, ca7, cb6, cb7)]
 
 
 def moved_of(cen, east, west, u, v):
@@ -89,6 +86,13 @@
 
 def lanes(f):
     return slice(f * L, (f + 1) * L)
+
+
+def mask_kernel(days, first, second):
+    for out, step in ((first, 0), (second, 1)):
+        m = days[step].astype(jnp.float32)
+        for c in range(C):
+            out[c] = jnp.broadcast_to(m[:, c : c + 1], (R, L))
 
 
 def prepare_kernel(ft, mask, lon_w, lon_e, lat_s, lat_n, moved, normed, mk, ext, edge):
@@ -182,35 +186,24 @@
     weights, h1, h2, out, ext, x2, moved2, moved1, sems, moved_sem = rest[9:]
     at = lax.axis_index("y") * 8 + lax.axis_index("xl") * 4 + lax.axis_index("xh") * 2 + lax.axis_index("core")
     base = at * 32
-
-    def table(k):
-        return positions[base + k]
-
-    core = table(16)
+    lat = lax.axis_index("xh") * 2 + lax.axis_index("core")
     for k in range(8):
-        net = core if k < 4 else 1 - core
-        colour = (k // 2) % 2
-        late = (k % 2) * 2
-        for p in range(2):
-            for q in range(4):
-                j, i = (late + p, q) if colour == 0 else (q, late + p)
-                x = table(net * 8 + i)
-                y = table(net * 8 + 4 + j)
-                row = pl.multiple_of(y * 256 + (x % 2) * 128 + colour * 64, 64)
-                col = pl.multiple_of((x // 2) * HALF, 128)
-                src = pieces[k].at[pl.ds((p * 4 + q) * 64, 64), :]
-                dst = weights.at[net, pl.ds(row, 64), pl.ds(col, HALF)]
-                sem = (net * 2 + x // 2) * 16 + y * 4 + (x % 2) * 2 + colour
-                pltpu.make_async_copy(src, dst, sems.at[sem]).start()
+        for slot in range(4):
+            code = positions[base + k * 4 + slot]
+            row = pl.multiple_of((code % 8) * BLOCK, BLOCK)
+            col = pl.multiple_of(((code // 8) % 2) * HALF, 128)
+            src = pieces[k].at[pl.ds(slot * BLOCK, BLOCK), :]
+            dst = weights.at[code // 16, pl.ds(row, BLOCK), pl.ds(col, HALF)]
+            pltpu.make_async_copy(src, dst, sems.at[code]).start()
 
     arrived = pltpu.make_async_copy(moved1_any, moved1, moved_sem)
     arrived.start()
 
     def arrive(net, half):
-        for k in range(16):
-            src = pieces[0].at[pl.ds(0, 64), :]
-            dst = weights.at[net, pl.ds(k * 64, 64), pl.ds(half * HALF, HALF)]
-            pltpu.make_async_copy(src, dst, sems.at[(net * 2 + half) * 16 + k]).wait()
+        for k in range(8):
+            src = pieces[0].at[pl.ds(0, BLOCK), :]
+            dst = weights.at[net, pl.ds(k * BLOCK, BLOCK), pl.ds(half * HALF, HALF)]
+            pltpu.make_async_copy(src, dst, sems.at[(net * 2 + half) * 8 + k]).wait()
 
     networks(x1, mask0, weights, h1, h2, out, ROWS, arrive)
     arrived.wait()
@@ -224,10 +217,10 @@
     lax.fori_loop(0, WIDE, spread, 0)
 
     for c in range(C):
-        for k, (at, flag) in enumerate(((7, 17), (8 + R, 18))):
+        for k, (at, exists) in enumerate(((7, lat > 0), (8 + R, lat < 3))):
             row = MAIN + k * C + c
             value = moved1[row : row + 1, :] + out[row : row + 1, :]
-            value = jnp.where(table(flag) == 1, value, jnp.zeros_like(value))
+            value = jnp.where(exists, value, jnp.zeros_like(value))
             for f in range(F):
                 ext[c + 1, f, at : at + 1, :] = value[:, lanes(f)]
 
@@ -255,15 +248,21 @@
 def position_table():
     out = np.zeros((32, 32), np.int32)
 
-    def order(i, net):
-        p = ring_partner(i, net)
-        n = ring_partner(i, 1 - net)
-        return [i, p, n, ring_partner(n, net)]
-
-    for y, xl, xh, core in np.ndindex(4, 2, 2, 2):
-        x, lat = xh * 2 + xl, xh * 2 + core
-        row = order(x, 0) + order(y, 0) + order(x, 1) + order(y, 1) + [core, int(lat > 0), int(lat < 3)]
-        out[((y * 2 + xl) * 2 + xh) * 2 + core, : len(row)] = row
+    def order(i, kind):
+        n = ring_partner(i, 1 - kind)
+        return [i, ring_partner(i, kind), n, ring_partner(n, kind)]
+
+    for y, x, core in np.ndindex(4, 4, 2):
+        codes = []
+        for k, p, q in np.ndindex(8, 2, 2):
+            net = core if k < 4 else 1 - core
+            half, late = (k // 2) % 2, (k % 2) * 2
+            if net == 0:
+                bx, by = order(x, 0)[2 * half + q], order(y, half)[late + p]
+            else:
+                bx, by = order(x, half)[late + p], order(y, 0)[2 * half + q]
+            codes.append((net * 2 + bx // 2) * 8 + by * 2 + bx % 2)
+        out[device_at(y, x, core)] = codes
     return out
 
 
@@ -278,9 +277,15 @@
     pieces = gather_weights(block)
 
     ft = fields.transpose(1, 2, 0, 3)
-    masks = jnp.broadcast_to(
-        day_mask.transpose(0, 2, 1)[..., None].astype(jnp.float32), (2, C, R, L)
-    )
+    spread_masks = pl.pallas_call(
+        mask_kernel,
+        out_shape=(jax.ShapeDtypeStruct((C, R, L), jnp.float32),) * 2,
+        in_specs=vmem(1),
+        out_specs=vmem(2),
+        compiler_params=pltpu.CompilerParams(vmem_limit_bytes=4 << 20),
+        name="masks",
+    )
+    masks = spread_masks(day_mask)
     lon_n, lat_n_blocks = 128, 4
 
     def packed(cols, rows):
@@ -339,7 +344,7 @@
             pltpu.VMEM((C * R, IN), jnp.bfloat16),
             pltpu.VMEM((C * R, IN), jnp.float32),
             pltpu.VMEM((ROWS, IN), jnp.float32),
-            pltpu.SemaphoreType.DMA((64,)),
+            pltpu.SemaphoreType.DMA((32,)),
             pltpu.SemaphoreType.DMA,
         ],
         compiler_params=pltpu.CompilerParams(vmem_limit_bytes=26 << 20),

time: 152 us -> 146 us (0.961)
  waiting for transfers between devices: 23.5 us -> 28.4 us
  local copies, waits for them, and re-layouts: 4.68 us -> 0.16 us
  starting transfers between devices: 68.6 us -> 64.2 us
  Pallas kernels: 22 us -> 20.1 us
    ppermute x8 -> x6, waiting for transfers between devices: 13.1 us -> 17.8 us  [exchange(): return lax.ppermute(a, ('y', 'xl', 'xh', 'core'), pairs)]
    ppermute x8 -> x6, starting transfers between devices: 25.6 us -> 21 us  [exchange(): return lax.ppermute(a, ('y', 'xl', 'xh', 'core'), pairs)]
    slice x2, local copies, waits for them, and re-layouts: 2.24 us -> 0.1 us  [packed(): part = lax.optimization_barrier(ft[cols, :, rows]).astype(jnp.bfloat16)]
    pallas_call x1, Pallas kernels: 18.8 us -> 16.6 us  [shards(): pl.pallas_call(step_kernel, out_shape=jax.ShapeDtypeStruct((C, F, R, L),...]
    ppermute x1, starting transfers between devices: 2.54 us -> 4.21 us  [shards(): lat_s = lax.ppermute(wide(slice(R - 2, R)), LAT, [(i, i + 1) for i in ends])]
  transfers between devices with their start and end apart: 16 -> 14, of which waited for: 6 -> 6; matrix products, arithmetic and copies ran while one was open for 3% -> 0% of each run, Pallas kernels for 2% -> 2%
where the time goes in v5:
time: 146 us; the launch traced here: 145 us
  starting transfers between devices  64.2 us (44%)
  blocking collectives  30.8 us (21%)
  waiting for transfers between devices  28.4 us (19%)
  Pallas kernels  20.1 us (14%)
    ppermute x4, starting transfers between devices, core_swap(): return lax.ppermute(a, 'core', [(0, 1), (1, 0)])  33.2 us
    all_gather x1, blocking collectives, gather_weights(): z = lax.all_gather(block, 'z', axis=0)  30.8 us
    ppermute x6, starting transfers between devices, exchange(): return lax.ppermute(a, ('y', 'xl', 'xh', 'core'), pairs)  21 us
    ppermute x6, waiting for transfers between devices, exchange(): return lax.ppermute(a, ('y', 'xl', 'xh', 'core'), pairs)  17.8 us
    pallas_call x1, Pallas kernels, shards(): pl.pallas_call(step_kernel, out_shape=jax.ShapeDtypeStruct((C, F, R, L),...  16.6 us
    ppermute x1, waiting for transfers between devices, shards(): lat_n = lax.ppermute(wide(slice(0, 2)), LAT, [(i + 1, i) for i in ends])  5.95 us
    ppermute x1, starting transfers between devices, shards(): lat_s = lax.ppermute(wide(slice(R - 2, R)), LAT, [(i, i + 1) for i in ends])  4.21 us
    ppermute x1, waiting for transfers between devices, shards(): lax.ppermute(packed(slice(0, 2), slice(0, R)), LON, [((i + 1) % lon_n, i)...  3.41 us
  transfers between devices with their start and end apart: 14, of which 6 were waited for; matrix products, arithmetic and copies ran while one was open for 0% of the time, Pallas kernels for 2%

profile of v5, /device:TPU:1, one launch (start us, length us, event | category | flops | bytes accessed | tf_op | source)
XLA Modules:
  0.0 145.3 jit_solution(16979209939879304044)
XLA Ops:
  0.0 0.7 fusion.1
  0.7 30.8 %all_gather.3 = bf16[16,8,1280]{2,1,0:T(8,128)(2,1)S(1)} all-gather(bf16[1,8,1280]{2,1,0:T(8,128)(2,1)S(1)} %fusion.1), channel_id=1, replica_groups=mesh['y'=4,'xl'=2,'z'=16,'xh'=2,'core'=2] {'z'}, dimensions={0}, use_global_device_ids=true | all-gather | bytes 348160 | tf_op jit(solution)/shard_map/all_gather | solution.py:55
  31.5 3.2 %collective-permute-start.4 = (bf16[16,8,1280]{2,1,0:T(8,128)(2,1)S(1)}, bf16[16,8,1280]{2,1,0:T(8,128)(2,1)S(1)}, u32[]{:S(2)}, u32[]{:S(2)}) collective-permute-start(bf16[16,8,1280]{2,1,0:T(8,128)(2,1)S(1)} %all_gather.3), channel_id=1, source_target_pairs={{0,64},{1,129},{2,66},{3,131},{64,0},{65,193},{66,2},{67,195},{128... | collective-permute-start | bytes 983048 | tf_op jit(solution)/shard_map/ppermute | solution.py:43
  34.7 4.6 %collective-permute-done.4 = bf16[16,8,1280]{2,1,0:T(8,128)(2,1)S(1)} collective-permute-done((bf16[16,8,1280]{2,1,0:T(8,128)(2,1)S(1)}, bf16[16,8,1280]{2,1,0:T(8,128)(2,1)S(1)}, u32[]{:S(2)}, u32[]{:S(2)}) %collective-permute-start.4) | collective-permute-done | bytes 327712 | tf_op jit(solution)/shard_map/ppermute | solution.py:43
  39.3 0.1 fusion.2
  39.4 4.6 %collective-permute-start.7 = (bf16[2,16,8,1280]{3,2,1,0:T(8,128)(2,1)S(1)}, bf16[2,16,8,1280]{3,2,1,0:T(8,128)(2,1)S(1)}, u32[]{:S(2)}, u32[]{:S(2)}) collective-permute-start(bf16[2,16,8,1280]{3,2,1,0:T(8,128)(2,1)S(1)} %get-tuple-element.20), channel_id=1, source_target_pairs={{0,66},{1,385},{2,64},{3,387},{64,2},{65,449},{66,0},{67,451},{128... | collective-permute-start | bytes 1966088 | tf_op jit(solution)/shard_map/ppermute | solution.py:43
  44.1 3.1 %collective-permute-start.5 = (bf16[2,16,8,1280]{3,2,1,0:T(8,128)(2,1)S(1)}, bf16[2,16,8,1280]{3,2,1,0:T(8,128)(2,1)S(1)}, u32[]{:S(2)}, u32[]{:S(2)}) collective-permute-start(bf16[2,16,8,1280]{3,2,1,0:T(8,128)(2,1)S(1)} %get-tuple-element.20), channel_id=1, source_target_pairs={{0,128},{1,65},{2,130},{3,67},{64,192},{65,1},{66,194},{67,3},{128... | collective-permute-start | bytes 1966088 | tf_op jit(solution)/shard_map/ppermute | solution.py:43
  47.2 4.8 %collective-permute-done.7 = bf16[2,16,8,1280]{3,2,1,0:T(8,128)(2,1)S(1)} collective-permute-done((bf16[2,16,8,1280]{3,2,1,0:T(8,128)(2,1)S(1)}, bf16[2,16,8,1280]{3,2,1,0:T(8,128)(2,1)S(1)}, u32[]{:S(2)}, u32[]{:S(2)}) %collective-permute-start.7) | collective-permute-done | bytes 655392 | tf_op jit(solution)/shard_map/ppermute | solution.py:43
  52.0 4.4 %collective-permute-start.8 = (bf16[2,16,8,1280]{3,2,1,0:T(8,128)(2,1)S(1)}, bf16[2,16,8,1280]{3,2,1,0:T(8,128)(2,1)S(1)}, u32[]{:S(2)}, u32[]{:S(2)}) collective-permute-start(bf16[2,16,8,1280]{3,2,1,0:T(8,128)(2,1)S(1)} %collective-permute-done.7), channel_id=1, source_target_pairs={{0,384},{1,67},{2,386},{3,65},{64,448},{65,3},{66,450},{67,1},{128... | collective-permute-start | bytes 1966088 | tf_op jit(solution)/shard_map/ppermute | solution.py:43
  56.4 0.0 collective-permute-done.5
  56.4 0.1 pad_maximum_fusion
  56.6 3.7 %collective-permute-start.6 = (bf16[2,2,16,8,1280]{4,3,2,1,0:T(8,128)(2,1)S(1)}, bf16[2,2,16,8,1280]{4,3,2,1,0:T(8,128)(2,1)S(1)}, u32[]{:S(2)}, u32[]{:S(2)}) collective-permute-start(bf16[2,2,16,8,1280]{4,3,2,1,0:T(8,128)(2,1)S(1)} %pad_maximum_fusion), channel_id=1, source_target_pairs={{0,384},{1,67},{2,386},{3,65},{64,448},{65,3},{66,450},{67,1},{128... | collective-permute-start | bytes 3932168 | tf_op jit(solution)/shard_map/ppermute | solution.py:43
  60.2 8.3 %collective-permute-done.8 = bf16[2,16,8,1280]{3,2,1,0:T(8,128)(2,1)S(1)} collective-permute-done((bf16[2,16,8,1280]{3,2,1,0:T(8,128)(2,1)S(1)}, bf16[2,16,8,1280]{3,2,1,0:T(8,128)(2,1)S(1)}, u32[]{:S(2)}, u32[]{:S(2)}) %collective-permute-start.8) | collective-permute-done | bytes 655392 | tf_op jit(solution)/shard_map/ppermute | solution.py:43
  68.5 0.0 copy-start
  68.6 0.0 copy-start.1
  68.6 0.1 pad_maximum_fusion.1
  68.7 2.1 %collective-permute-start.9 = (bf16[2,2,16,8,1280]{4,3,2,1,0:T(8,128)(2,1)S(1)}, bf16[2,2,16,8,1280]{4,3,2,1,0:T(8,128)(2,1)S(1)}, u32[]{:S(2)}, u32[]{:S(2)}) collective-permute-start(bf16[2,2,16,8,1280]{4,3,2,1,0:T(8,128)(2,1)S(1)} %pad_maximum_fusion.1), channel_id=1, source_target_pairs={{0,128},{1,65},{2,130},{3,67},{64,192},{65,1},{66,194},{67,3},{128... | collective-permute-start | bytes 3932168 | tf_op jit(solution)/shard_map/ppermute | solution.py:43
  70.7 0.0 copy-done
  70.8 0.0 copy-done.1
  70.8 0.0 copy-start.2
  70.8 0.2 masks.1
  71.0 1.9 %collective-permute-start = (bf16[2,7,16,128]{3,2,1,0:T(8,128)(2,1)S(1)}, bf16[2,7,16,128]{3,2,1,0:T(8,128)(2,1)S(1)}, u32[]{:S(2)}, u32[]{:S(2)}) collective-permute-start(bf16[2,7,16,128]{3,2,1,0:T(8,128)(2,1)S(1)} %pad_maximum_fusion.5), channel_id=1, source_target_pairs={{0,4},{4,8},{8,12},{12,16},{16,20},{20,24},{24,28},{28,32},{32,36}... | collective-permute-start | bytes 172040 | tf_op jit(solution)/shard_map/ppermute | solution.py:295
  73.0 18.3 %collective-permute-start.10 = (bf16[2,2,16,8,1280]{4,3,2,1,0:T(8,128)(2,1)S(1)}, bf16[2,2,16,8,1280]{4,3,2,1,0:T(8,128)(2,1)S(1)}, u32[]{:S(2)}, u32[]{:S(2)}) collective-permute-start(bf16[2,2,16,8,1280]{4,3,2,1,0:T(8,128)(2,1)S(1)} %pad_maximum_fusion), channel_id=1, source_target_pairs={{0,1},{1,0},{2,3},{3,2},{4,5},{5,4},{6,7},{7,6},{8,9},{9,8},{10,11... | collective-permute-start | bytes 3932168 | tf_op jit(solution)/shard_map/ppermute | solution.py:51
  91.3 1.9 %collective-permute-start.12 = (bf16[2,2,16,8,1280]{4,3,2,1,0:T(8,128)(2,1)S(1)}, bf16[2,2,16,8,1280]{4,3,2,1,0:T(8,128)(2,1)S(1)}, u32[]{:S(2)}, u32[]{:S(2)}) collective-permute-start(bf16[2,2,16,8,1280]{4,3,2,1,0:T(8,128)(2,1)S(1)} %pad_maximum_fusion.1), channel_id=1, source_target_pairs={{0,1},{1,0},{2,3},{3,2},{4,5},{5,4},{6,7},{7,6},{8,9},{9,8},{10,11... | collective-permute-start | bytes 3932168 | tf_op jit(solution)/shard_map/ppermute | solution.py:51
  93.2 0.0 collective-permute-done.6
  93.2 7.9 %collective-permute-start.11 = (bf16[2,2,16,8,1280]{4,3,2,1,0:T(8,128)(2,1)S(1)}, bf16[2,2,16,8,1280]{4,3,2,1,0:T(8,128)(2,1)S(1)}, u32[]{:S(2)}, u32[]{:S(2)}) collective-permute-start(bf16[2,2,16,8,1280]{4,3,2,1,0:T(8,128)(2,1)S(1)} %collective-permute-done.6), channel_id=1, source_target_pairs={{0,1},{1,0},{2,3},{3,2},{4,5},{5,4},{6,7},{7,6},{8,9},{9,8},{10,11... | collective-permute-start | bytes 3932168 | tf_op jit(solution)/shard_map/ppermute | solution.py:51
  101.1 0.0 collective-permute-done.9
  101.1 5.1 %collective-permute-start.13 = (bf16[2,2,16,8,1280]{4,3,2,1,0:T(8,128)(2,1)S(1)}, bf16[2,2,16,8,1280]{4,3,2,1,0:T(8,128)(2,1)S(1)}, u32[]{:S(2)}, u32[]{:S(2)}) collective-permute-start(bf16[2,2,16,8,1280]{4,3,2,1,0:T(8,128)(2,1)S(1)} %collective-permute-done.9), channel_id=1, source_target_pairs={{0,1},{1,0},{2,3},{3,2},{4,5},{5,4},{6,7},{7,6},{8,9},{9,8},{10,11... | collective-permute-start | bytes 3932168 | tf_op jit(solution)/shard_map/ppermute | solution.py:51
  106.2 0.1 fusion.3
  106.4 0.0 collective-permute-done.lon_w
  106.4 1.9 %collective-permute-start.1 = (bf16[2,7,16,128]{3,2,1,0:T(8,128)(2,1)S(1)}, bf16[2,7,16,128]{3,2,1,0:T(8,128)(2,1)S(1)}, u32[]{:S(2)}, u32[]{:S(2)}) collective-permute-start(bf16[2,7,16,128]{3,2,1,0:T(8,128)(2,1)S(1)} %pad_maximum_fusion.6), channel_id=1, source_target_pairs={{4,0},{8,4},{12,8},{16,12},{20,16},{24,20},{28,24},{32,28},{36,32}... | collective-permute-start | bytes 172040 | tf_op jit(solution)/shard_map/ppermute | solution.py:298
  108.3 3.4 %collective-permute-done.1.lon_e = bf16[2,7,16,128]{3,2,1,0:T(8,128)(2,1)S(1)} collective-permute-done((bf16[2,7,16,128]{3,2,1,0:T(8,128)(2,1)S(1)}, bf16[2,7,16,128]{3,2,1,0:T(8,128)(2,1)S(1)}, u32[]{:S(2)}, u32[]{:S(2)}) %collective-permute-start.1) | collective-permute-done | bytes 57376 | tf_op jit(solution)/shard_map/ppermute | solution.py:298
  111.8 0.1 pad_maximum_fusion.3
  111.9 4.2 %collective-permute-start.2 = (bf16[22,7,2,128]{3,2,1,0:T(2,128)(2,1)S(1)}, bf16[22,7,2,128]{3,2,1,0:T(2,128)(2,1)S(1)}, u32[]{:S(2)}, u32[]{:S(2)}) collective-permute-start(bf16[22,7,2,128]{3,2,1,0:T(2,128)(2,1)S(1)} %pad_maximum_fusion.3), channel_id=1, source_target_pairs={{0,1},{1,2},{2,3},{4,5},{5,6},{6,7},{8,9},{9,10},{10,11},{12,13},{... | collective-permute-start | bytes 236552 | tf_op jit(solution)/shard_map/ppermute | solution.py:308
  116.1 0.1 pad_maximum_fusion.4
  116.2 1.3 collective-permute-done.2.lat_s
  117.5 1.9 %collective-permute-start.3 = (bf16[22,7,2,128]{3,2,1,0:T(2,128)(2,1)S(1)}, bf16[22,7,2,128]{3,2,1,0:T(2,128)(2,1)S(1)}, u32[]{:S(2)}, u32[]{:S(2)}) collective-permute-start(bf16[22,7,2,128]{3,2,1,0:T(2,128)(2,1)S(1)} %pad_maximum_fusion.4), channel_id=1, source_target_pairs={{1,0},{2,1},{3,2},{5,4},{6,5},{7,6},{9,8},{10,9},{11,10},{13,12},{... | collective-permute-start | bytes 236552 | tf_op jit(solution)/shard_map/ppermute | solution.py:309
  119.5 5.9 %collective-permute-done.3.lat_n = bf16[22,7,2,128]{3,2,1,0:T(2,128)(2,1)S(1)} collective-permute-done((bf16[22,7,2,128]{3,2,1,0:T(2,128)(2,1)S(1)}, bf16[22,7,2,128]{3,2,1,0:T(2,128)(2,1)S(1)}, u32[]{:S(2)}, u32[]{:S(2)}) %collective-permute-start.3) | collective-permute-done | bytes 78880 | tf_op jit(solution)/shard_map/ppermute | solution.py:309
  125.4 3.2 %prepare.1 = (f32[400,768]{1,0:T(8,128)S(1)}, bf16[400,768]{1,0:T(8,128)(2,1)S(1)}, f32[400,128]{1,0:T(8,128)S(1)}) custom-call(f32[20,6,16,128]{3,2,1,0:T(8,128)S(1)} %bitcast.35, f32[20,16,128]{2,1,0:T(8,128)S(1)} %get-tuple-element.10.mask, bf16[2,7,16,128]{3,2,1,0:T(8,128)(2,1)S(1)} %collective-permute-done.lon_w, ...), custom_call_target="tpu_custom_call" | custom-call | tf_op jit(solution)/shard_map/prepare/pallas_call | solution.py:327
  128.7 0.0 collective-permute-done.10
  128.7 0.0 collective-permute-done.12
  128.7 0.0 collective-permute-done.11
  128.7 0.0 collective-permute-done.13
  128.7 0.0 copy-done.2
  128.7 16.6 %steps.1 = f32[20,6,16,128]{3,2,1,0:T(8,128)} custom-call(s32[1024]{0:T(1024)S(1)} %copy-done.2, bf16[400,768]{1,0:T(8,128)(2,1)S(1)} %get-tuple-element.11.x1, f32[400,768]{1,0:T(8,128)S(1)} %get-tuple-element.12.moved1_any, f32[400,128]{1,0:T(8,128)S(1)} %get-tuple-element.13.mask0, f32[20,16,128]{2,1,0:T(8,128)S(1)} %get-tuple-element.14.mask1, ...), custom_call_target="tpu_custom_call" | custom-call | tf_op jit(solution)/shard_map/steps/pallas_call | solution.py:329
  (8 shorter events, 0.1 us)
Async XLA Ops:
  31.5 7.8 %collective-permute-start.4 = (bf16[16,8,1280]{2,1,0:T(8,128)(2,1)S(1)}, bf16[16,8,1280]{2,1,0:T(8,128)(2,1)S(1)}, u32[]{:S(2)}, u32[]{:S(2)}) collective-permute-start(bf16[16,8,1280]{2,1,0:T(8,128)(2,1)S(1)} %all_gather.3), channel_id=1, source_target_pairs={{0,64},{1,129},{2,66},{3,131},{64,0},{65,193},{66,2},{67,195},{128... | collective-permute-start | bytes 983048 | tf_op jit(solution)/shard_map/ppermute | solution.py:43
  39.4 12.6 %collective-permute-start.7 = (bf16[2,16,8,1280]{3,2,1,0:T(8,128)(2,1)S(1)}, bf16[2,16,8,1280]{3,2,1,0:T(8,128)(2,1)S(1)}, u32[]{:S(2)}, u32[]{:S(2)}) collective-permute-start(bf16[2,16,8,1280]{3,2,1,0:T(8,128)(2,1)S(1)} %get-tuple-element.20), channel_id=1, source_target_pairs={{0,66},{1,385},{2,64},{3,387},{64,2},{65,449},{66,0},{67,451},{128... | collective-permute-start | bytes 1966088 | tf_op jit(solution)/shard_map/ppermute | solution.py:43
  44.1 12.4 %collective-permute-start.5 = (bf16[2,16,8,1280]{3,2,1,0:T(8,128)(2,1)S(1)}, bf16[2,16,8,1280]{3,2,1,0:T(8,128)(2,1)S(1)}, u32[]{:S(2)}, u32[]{:S(2)}) collective-permute-start(bf16[2,16,8,1280]{3,2,1,0:T(8,128)(2,1)S(1)} %get-tuple-element.20), channel_id=1, source_target_pairs={{0,128},{1,65},{2,130},{3,67},{64,192},{65,1},{66,194},{67,3},{128... | collective-permute-start | bytes 1966088 | tf_op jit(solution)/shard_map/ppermute | solution.py:43
  52.0 16.5 %collective-permute-start.8 = (bf16[2,16,8,1280]{3,2,1,0:T(8,128)(2,1)S(1)}, bf16[2,16,8,1280]{3,2,1,0:T(8,128)(2,1)S(1)}, u32[]{:S(2)}, u32[]{:S(2)}) collective-permute-start(bf16[2,16,8,1280]{3,2,1,0:T(8,128)(2,1)S(1)} %collective-permute-done.7), channel_id=1, source_target_pairs={{0,384},{1,67},{2,386},{3,65},{64,448},{65,3},{66,450},{67,1},{128... | collective-permute-start | bytes 1966088 | tf_op jit(solution)/shard_map/ppermute | solution.py:43
  56.6 36.6 %collective-permute-start.6 = (bf16[2,2,16,8,1280]{4,3,2,1,0:T(8,128)(2,1)S(1)}, bf16[2,2,16,8,1280]{4,3,2,1,0:T(8,128)(2,1)S(1)}, u32[]{:S(2)}, u32[]{:S(2)}) collective-permute-start(bf16[2,2,16,8,1280]{4,3,2,1,0:T(8,128)(2,1)S(1)} %pad_maximum_fusion), channel_id=1, source_target_pairs={{0,384},{1,67},{2,386},{3,65},{64,448},{65,3},{66,450},{67,1},{128... | collective-permute-start | bytes 3932168 | tf_op jit(solution)/shard_map/ppermute | solution.py:43
  68.5 2.2 %copy-start = (f32[16,20,6,128]{3,0,2,1:T(8,128)S(1)}, f32[16,20,6,128]{3,0,2,1:T(8,128)}, u32[]{:S(2)}) copy-start(f32[16,20,6,128]{3,0,2,1:T(8,128)} %param.6) | copy-start | bytes 2949124
  68.6 2.2 %copy-start.1 = (s32[2,16,20]{2,1,0:T(8,128)S(1)}, s32[2,16,20]{2,1,0:T(8,128)}, u32[]{:S(2)}) copy-start(s32[2,16,20]{2,1,0:T(8,128)} %days.1) | copy-start | bytes 7684
  68.7 32.5 %collective-permute-start.9 = (bf16[2,2,16,8,1280]{4,3,2,1,0:T(8,128)(2,1)S(1)}, bf16[2,2,16,8,1280]{4,3,2,1,0:T(8,128)(2,1)S(1)}, u32[]{:S(2)}, u32[]{:S(2)}) collective-permute-start(bf16[2,2,16,8,1280]{4,3,2,1,0:T(8,128)(2,1)S(1)} %pad_maximum_fusion.1), channel_id=1, source_target_pairs={{0,128},{1,65},{2,130},{3,67},{64,192},{65,1},{66,194},{67,3},{128... | collective-permute-start | bytes 3932168 | tf_op jit(solution)/shard_map/ppermute | solution.py:43
  70.8 57.9 %copy-start.2 = (s32[1024]{0:T(1024)S(1)}, s32[1024]{0:T(1024)}, u32[]{:S(2)}) copy-start(s32[1024]{0:T(1024)} %constant.16.clone.positions) | copy-start | bytes 12292
  71.0 35.3 %collective-permute-start = (bf16[2,7,16,128]{3,2,1,0:T(8,128)(2,1)S(1)}, bf16[2,7,16,128]{3,2,1,0:T(8,128)(2,1)S(1)}, u32[]{:S(2)}, u32[]{:S(2)}) collective-permute-start(bf16[2,7,16,128]{3,2,1,0:T(8,128)(2,1)S(1)} %pad_maximum_fusion.5), channel_id=1, source_target_pairs={{0,4},{4,8},{8,12},{12,16},{16,20},{20,24},{24,28},{28,32},{32,36}... | collective-permute-start | bytes 172040 | tf_op jit(solution)/shard_map/ppermute | solution.py:295
  73.0 55.7 %collective-permute-start.10 = (bf16[2,2,16,8,1280]{4,3,2,1,0:T(8,128)(2,1)S(1)}, bf16[2,2,16,8,1280]{4,3,2,1,0:T(8,128)(2,1)S(1)}, u32[]{:S(2)}, u32[]{:S(2)}) collective-permute-start(bf16[2,2,16,8,1280]{4,3,2,1,0:T(8,128)(2,1)S(1)} %pad_maximum_fusion), channel_id=1, source_target_pairs={{0,1},{1,0},{2,3},{3,2},{4,5},{5,4},{6,7},{7,6},{8,9},{9,8},{10,11... | collective-permute-start | bytes 3932168 | tf_op jit(solution)/shard_map/ppermute | solution.py:51
  91.3 37.4 %collective-permute-start.12 = (bf16[2,2,16,8,1280]{4,3,2,1,0:T(8,128)(2,1)S(1)}, bf16[2,2,16,8,1280]{4,3,2,1,0:T(8,128)(2,1)S(1)}, u32[]{:S(2)}, u32[]{:S(2)}) collective-permute-start(bf16[2,2,16,8,1280]{4,3,2,1,0:T(8,128)(2,1)S(1)} %pad_maximum_fusion.1), channel_id=1, source_target_pairs={{0,1},{1,0},{2,3},{3,2},{4,5},{5,4},{6,7},{7,6},{8,9},{9,8},{10,11... | collective-permute-start | bytes 3932168 | tf_op jit(solution)/shard_map/ppermute | solution.py:51
  93.2 35.5 %collective-permute-start.11 = (bf16[2,2,16,8,1280]{4,3,2,1,0:T(8,128)(2,1)S(1)}, bf16[2,2,16,8,1280]{4,3,2,1,0:T(8,128)(2,1)S(1)}, u32[]{:S(2)}, u32[]{:S(2)}) collective-permute-start(bf16[2,2,16,8,1280]{4,3,2,1,0:T(8,128)(2,1)S(1)} %collective-permute-done.6), channel_id=1, source_target_pairs={{0,1},{1,0},{2,3},{3,2},{4,5},{5,4},{6,7},{7,6},{8,9},{9,8},{10,11... | collective-permute-start | bytes 3932168 | tf_op jit(solution)/shard_map/ppermute | solution.py:51
  101.1 27.5 %collective-permute-start.13 = (bf16[2,2,16,8,1280]{4,3,2,1,0:T(8,128)(2,1)S(1)}, bf16[2,2,16,8,1280]{4,3,2,1,0:T(8,128)(2,1)S(1)}, u32[]{:S(2)}, u32[]{:S(2)}) collective-permute-start(bf16[2,2,16,8,1280]{4,3,2,1,0:T(8,128)(2,1)S(1)} %collective-permute-done.9), channel_id=1, source_target_pairs={{0,1},{1,0},{2,3},{3,2},{4,5},{5,4},{6,7},{7,6},{8,9},{9,8},{10,11... | collective-permute-start | bytes 3932168 | tf_op jit(solution)/shard_map/ppermute | solution.py:51
  106.4 5.4 %collective-permute-start.1 = (bf16[2,7,16,128]{3,2,1,0:T(8,128)(2,1)S(1)}, bf16[2,7,16,128]{3,2,1,0:T(8,128)(2,1)S(1)}, u32[]{:S(2)}, u32[]{:S(2)}) collective-permute-start(bf16[2,7,16,128]{3,2,1,0:T(8,128)(2,1)S(1)} %pad_maximum_fusion.6), channel_id=1, source_target_pairs={{4,0},{8,4},{12,8},{16,12},{20,16},{24,20},{28,24},{32,28},{36,32}... | collective-permute-start | bytes 172040 | tf_op jit(solution)/shard_map/ppermute | solution.py:298
  111.9 5.7 %collective-permute-start.2 = (bf16[22,7,2,128]{3,2,1,0:T(2,128)(2,1)S(1)}, bf16[22,7,2,128]{3,2,1,0:T(2,128)(2,1)S(1)}, u32[]{:S(2)}, u32[]{:S(2)}) collective-permute-start(bf16[22,7,2,128]{3,2,1,0:T(2,128)(2,1)S(1)} %pad_maximum_fusion.3), channel_id=1, source_target_pairs={{0,1},{1,2},{2,3},{4,5},{5,6},{6,7},{8,9},{9,10},{10,11},{12,13},{... | collective-permute-start | bytes 236552 | tf_op jit(solution)/shard_map/ppermute | solution.py:308
  117.5 7.9 %collective-permute-start.3 = (bf16[22,7,2,128]{3,2,1,0:T(2,128)(2,1)S(1)}, bf16[22,7,2,128]{3,2,1,0:T(2,128)(2,1)S(1)}, u32[]{:S(2)}, u32[]{:S(2)}) collective-permute-start(bf16[22,7,2,128]{3,2,1,0:T(2,128)(2,1)S(1)} %pad_maximum_fusion.4), channel_id=1, source_target_pairs={{1,0},{2,1},{3,2},{5,4},{6,5},{7,6},{9,8},{10,9},{11,10},{13,12},{... | collective-permute-start | bytes 236552 | tf_op jit(solution)/shard_map/ppermute | solution.py:309

commit v6 on v5

--- a/solution.py
+++ b/solution.py
@@ -77,6 +77,20 @@
     return [moved_of(cen[f], ext[c + 1, f], ext[c - 1, f], cen[0], cen[1]) for f in range(F)]
 
 
+def own_moved(ext, c):
+    rows = slice(8, 8 + R)
+    cen = [ext[c, f, rows, :] for f in range(F)]
+    u, v = COURANT * cen[0], COURANT * cen[1]
+    out = []
+    for f in range(F):
+        east, west = ext[c + 1, f, rows, :], ext[c - 1, f, rows, :]
+        north, south = ext[c, f, 9 : 9 + R, :], ext[c, f, 7 : 7 + R, :]
+        advected = u * (east - west) + v * (north - south)
+        smoothed = (east + west) + (north + south) - 4.0 * cen[f]
+        out.append(cen[f] - advected + DIFFUSE * smoothed)
+    return out
+
+
 def rs_of(parts):
     ss = parts[0] * parts[0]
     for p in parts[1:]:
@@ -153,8 +167,8 @@
     return (half + half * jnp.tanh(half)).astype(jnp.bfloat16)
 
 
-def networks(x, mask_ref, weights, h1, h2, out, rows, arrive):
-    def net(n, carry):
+def networks(core, x, mask_ref, weights, h1, h2, out, rows, arrive):
+    def net(n, initial):
         if arrive:
             arrive(n, 0)
         want = (1 - n).astype(jnp.float32)
@@ -174,10 +188,10 @@
             cols = slice(t * TILE, (t + 1) * TILE)
             w = weights[n, :, IN + HID + t * TILE : IN + HID + (t + 1) * TILE]
             d = jnp.dot(h2[0:rows, :], w, preferred_element_type=jnp.float32)
-            out[0:rows, cols] = jnp.where(pick, d, out[0:rows, cols])
-        return carry
-
-    lax.fori_loop(0, 2, net, 0)
+            out[0:rows, cols] = jnp.where(pick, d, 0.0 if initial else out[0:rows, cols])
+
+    net(core, True)
+    net(1 - core, False)
 
 
 def step_kernel(positions, x1, moved1_any, mask0, mask1, *rest):
@@ -185,6 +199,7 @@
     result = rest[8]
     weights, h1, h2, out, ext, x2, moved2, moved1, sems, moved_sem = rest[9:]
     at = lax.axis_index("y") * 8 + lax.axis_index("xl") * 4 + lax.axis_index("xh") * 2 + lax.axis_index("core")
+    core = lax.axis_index("core")
     base = at * 32
     lat = lax.axis_index("xh") * 2 + lax.axis_index("core")
     for k in range(8):
@@ -205,7 +220,7 @@
             dst = weights.at[net, pl.ds(k * BLOCK, BLOCK), pl.ds(half * HALF, HALF)]
             pltpu.make_async_copy(src, dst, sems.at[(net * 2 + half) * 8 + k]).wait()
 
-    networks(x1, mask0, weights, h1, h2, out, ROWS, arrive)
+    networks(core, x1, mask0, weights, h1, h2, out, ROWS, arrive)
     arrived.wait()
 
     def spread(c, carry):
@@ -214,7 +229,7 @@
             ext[c, f, 8 : 8 + R, :] = moved1[pl.ds(row, R), lanes(f)] + out[pl.ds(row, R), lanes(f)]
         return carry
 
-    lax.fori_loop(0, WIDE, spread, 0)
+    lax.fori_loop(0, WIDE, spread, 0, unroll=True)
 
     for c in range(C):
         for k, (at, exists) in enumerate(((7, lat > 0), (8 + R, lat < 3))):
@@ -225,16 +240,16 @@
                 ext[c + 1, f, at : at + 1, :] = value[:, lanes(f)]
 
     def second(c, carry):
-        parts = column_moved(ext, c + 1)
+        parts = own_moved(ext, c + 1)
         rs = rs_of(parts)
         row = pl.multiple_of(c * R, R)
         for f in range(F):
-            moved2[pl.ds(row, R), lanes(f)] = parts[f][8 : 8 + R]
-            x2[pl.ds(row, R), lanes(f)] = (parts[f] * rs)[8 : 8 + R].astype(jnp.bfloat16)
-        return carry
-
-    lax.fori_loop(0, C, second, 0)
-    networks(x2, mask1, weights, h1, h2, out, C * R, None)
+            moved2[pl.ds(row, R), lanes(f)] = parts[f]
+            x2[pl.ds(row, R), lanes(f)] = (parts[f] * rs).astype(jnp.bfloat16)
+        return carry
+
+    lax.fori_loop(0, C, second, 0, unroll=5)
+    networks(core, x2, mask1, weights, h1, h2, out, C * R, None)
 
     def finish(c, carry):
         row = pl.multiple_of(c * R, R)
@@ -242,7 +257,7 @@
             result[c, f] = moved2[pl.ds(row, R), lanes(f)] + out[pl.ds(row, R), lanes(f)]
         return carry
 
-    lax.fori_loop(0, C, finish, 0)
+    lax.fori_loop(0, C, finish, 0, unroll=True)
 
 
 def position_table():
@@ -270,63 +285,8 @@
     return [pl.BlockSpec(memory_space=pltpu.VMEM)] * n
 
 
-def shards(fields, day_mask, w_in, w_mid, w_out):
-    xh, core = lax.axis_index("xh"), lax.axis_index("core")
-    joined = jnp.concatenate([w_in, w_mid, w_out], axis=2)
-    block = lax.dynamic_slice(joined, (core, 0, xh * HALF), (1, 8, HALF))[0]
-    pieces = gather_weights(block)
-
-    ft = fields.transpose(1, 2, 0, 3)
-    spread_masks = pl.pallas_call(
-        mask_kernel,
-        out_shape=(jax.ShapeDtypeStruct((C, R, L), jnp.float32),) * 2,
-        in_specs=vmem(1),
-        out_specs=vmem(2),
-        compiler_params=pltpu.CompilerParams(vmem_limit_bytes=4 << 20),
-        name="masks",
-    )
-    masks = spread_masks(day_mask)
-    lon_n, lat_n_blocks = 128, 4
-
-    def packed(cols, rows):
-        part = lax.optimization_barrier(ft[cols, :, rows]).astype(jnp.bfloat16)
-        return jnp.concatenate([part, masks[0][cols, None, rows].astype(jnp.bfloat16)], axis=1)
-
-    lon_w = lax.ppermute(
-        packed(slice(C - 2, C), slice(0, R)), LON, [(i, (i + 1) % lon_n) for i in range(lon_n)]
-    )
-    lon_e = lax.ppermute(
-        packed(slice(0, 2), slice(0, R)), LON, [((i + 1) % lon_n, i) for i in range(lon_n)]
-    )
-
-    def wide(rows):
-        return jnp.concatenate(
-            [lon_w[1:, :, rows], packed(slice(0, C), rows), lon_e[:1, :, rows]], axis=0
-        )
-
-    ends = range(lat_n_blocks - 1)
-    lat_s = lax.ppermute(wide(slice(R - 2, R)), LAT, [(i, i + 1) for i in ends])
-    lat_n = lax.ppermute(wide(slice(0, 2)), LAT, [(i + 1, i) for i in ends])
-
-    prepare = pl.pallas_call(
-        prepare_kernel,
-        out_shape=(
-            jax.ShapeDtypeStruct((ROWS, IN), jnp.float32),
-            jax.ShapeDtypeStruct((ROWS, IN), jnp.bfloat16),
-            jax.ShapeDtypeStruct((ROWS, L), jnp.float32),
-        ),
-        in_specs=vmem(6),
-        out_specs=vmem(3),
-        scratch_shapes=[
-            pltpu.VMEM((C + 4, F, 32, L), jnp.float32),
-            pltpu.VMEM((WIDE, F, 8, L), jnp.float32),
-        ],
-        compiler_params=pltpu.CompilerParams(vmem_limit_bytes=4 << 20),
-        name="prepare",
-    )
-    moved1, x1, mask0 = prepare(ft, masks[0], lon_w, lon_e, lat_s, lat_n)
-
-    result = pl.pallas_call(
+def steps_call():
+    return pl.pallas_call(
         step_kernel,
         out_shape=jax.ShapeDtypeStruct((C, F, R, L), jnp.float32),
         in_specs=[pl.BlockSpec(memory_space=pltpu.SMEM)]
@@ -349,7 +309,66 @@
         ],
         compiler_params=pltpu.CompilerParams(vmem_limit_bytes=26 << 20),
         name="steps",
-    )(position_table().reshape(-1), x1, moved1, mask0, masks[1], *pieces)
+    )
+
+
+def shards(fields, day_mask, w_in, w_mid, w_out):
+    xh, core = lax.axis_index("xh"), lax.axis_index("core")
+    joined = jnp.concatenate([w_in, w_mid, w_out], axis=2)
+    block = lax.dynamic_slice(joined, (core, 0, xh * HALF), (1, 8, HALF))[0]
+    pieces = gather_weights(block)
+
+    ft = fields.transpose(1, 2, 0, 3)
+    spread_masks = pl.pallas_call(
+        mask_kernel,
+        out_shape=(jax.ShapeDtypeStruct((C, R, L), jnp.float32),) * 2,
+        in_specs=vmem(1),
+        out_specs=vmem(2),
+        compiler_params=pltpu.CompilerParams(vmem_limit_bytes=4 << 20),
+        name="masks",
+    )
+    masks = spread_masks(day_mask)
+    lon_n, lat_n_blocks = 128, 4
+
+    def packed(cols, rows):
+        part = lax.optimization_barrier(ft[cols, :, rows]).astype(jnp.bfloat16)
+        return jnp.concatenate([part, masks[0][cols, None, rows].astype(jnp.bfloat16)], axis=1)
+
+    lon_w = lax.ppermute(
+        packed(slice(C - 2, C), slice(0, R)), LON, [(i, (i + 1) % lon_n) for i in range(lon_n)]
+    )
+    lon_e = lax.ppermute(
+        packed(slice(0, 2), slice(0, R)), LON, [((i + 1) % lon_n, i) for i in range(lon_n)]
+    )
+
+    def wide(rows):
+        return jnp.concatenate(
+            [lon_w[1:, :, rows], packed(slice(0, C), rows), lon_e[:1, :, rows]], axis=0
+        )
+
+    ends = range(lat_n_blocks - 1)
+    lat_s = lax.ppermute(wide(slice(R - 2, R)), LAT, [(i, i + 1) for i in ends])
+    lat_n = lax.ppermute(wide(slice(0, 2)), LAT, [(i + 1, i) for i in ends])
+
+    prepare = pl.pallas_call(
+        prepare_kernel,
+        out_shape=(
+            jax.ShapeDtypeStruct((ROWS, IN), jnp.float32),
+            jax.ShapeDtypeStruct((ROWS, IN), jnp.bfloat16),
+            jax.ShapeDtypeStruct((ROWS, L), jnp.float32),
+        ),
+        in_specs=vmem(6),
+        out_specs=vmem(3),
+        scratch_shapes=[
+            pltpu.VMEM((C + 4, F, 32, L), jnp.float32),
+            pltpu.VMEM((WIDE, F, 8, L), jnp.float32),
+        ],
+        compiler_params=pltpu.CompilerParams(vmem_limit_bytes=4 << 20),
+        name="prepare",
+    )
+    moved1, x1, mask0 = prepare(ft, masks[0], lon_w, lon_e, lat_s, lat_n)
+
+    result = steps_call()(position_table().reshape(-1), x1, moved1, mask0, masks[1], *pieces)
     return result.transpose(2, 0, 1, 3)
 
 

time: 146 us -> 144 us (0.986)
  Pallas kernels: 20.1 us -> 17.9 us
    pallas_call x1, Pallas kernels: 16.6 us -> 14.5 us  [shards(): steps_call()]
where the time goes in v6:
time: 144 us; the launch traced here: 143 us
  starting transfers between devices  64.4 us (45%)
  blocking collectives  30.8 us (21%)
  waiting for transfers between devices  28.3 us (20%)
  Pallas kernels  17.9 us (12%)
    ppermute x4, starting transfers between devices, core_swap(): return lax.ppermute(a, 'core', [(0, 1), (1, 0)])  33.2 us
    all_gather x1, blocking collectives, gather_weights(): z = lax.all_gather(block, 'z', axis=0)  30.8 us
    ppermute x6, starting transfers between devices, exchange(): return lax.ppermute(a, ('y', 'xl', 'xh', 'core'), pairs)  21 us
    ppermute x6, waiting for transfers between devices, exchange(): return lax.ppermute(a, ('y', 'xl', 'xh', 'core'), pairs)  17.8 us
    pallas_call x1, Pallas kernels, shards(): steps_call()  14.5 us
    ppermute x1, waiting for transfers between devices, shards(): lat_n = lax.ppermute(wide(slice(0, 2)), LAT, [(i + 1, i) for i in ends])  5.77 us
    ppermute x1, starting transfers between devices, shards(): lat_s = lax.ppermute(wide(slice(R - 2, R)), LAT, [(i, i + 1) for i in ends])  4.21 us
    ppermute x1, waiting for transfers between devices, shards(): lax.ppermute(packed(slice(0, 2), slice(0, R)), LON, [((i + 1) % lon_n, i)...  3.41 us
  transfers between devices with their start and end apart: 14, of which 6 were waited for; matrix products, arithmetic and copies ran while one was open for 0% of the time, Pallas kernels for 2%

profile of v6, /device:TPU:1, one launch (start us, length us, event | category | flops | bytes accessed | tf_op | source)
XLA Modules:
  0.0 143.4 jit_solution(9097979108697117441)
XLA Ops:
  0.0 0.7 fusion.1
  0.7 30.8 %all_gather.3 = bf16[16,8,1280]{2,1,0:T(8,128)(2,1)S(1)} all-gather(bf16[1,8,1280]{2,1,0:T(8,128)(2,1)S(1)} %fusion.1), channel_id=1, replica_groups=mesh['y'=4,'xl'=2,'z'=16,'xh'=2,'core'=2] {'z'}, dimensions={0}, use_global_device_ids=true | all-gather | bytes 348160 | tf_op jit(solution)/shard_map/all_gather | solution.py:55
  31.5 3.2 %collective-permute-start.4 = (bf16[16,8,1280]{2,1,0:T(8,128)(2,1)S(1)}, bf16[16,8,1280]{2,1,0:T(8,128)(2,1)S(1)}, u32[]{:S(2)}, u32[]{:S(2)}) collective-permute-start(bf16[16,8,1280]{2,1,0:T(8,128)(2,1)S(1)} %all_gather.3), channel_id=1, source_target_pairs={{0,64},{1,129},{2,66},{3,131},{64,0},{65,193},{66,2},{67,195},{128... | collective-permute-start | bytes 983048 | tf_op jit(solution)/shard_map/ppermute | solution.py:43
  34.7 4.6 %collective-permute-done.4 = bf16[16,8,1280]{2,1,0:T(8,128)(2,1)S(1)} collective-permute-done((bf16[16,8,1280]{2,1,0:T(8,128)(2,1)S(1)}, bf16[16,8,1280]{2,1,0:T(8,128)(2,1)S(1)}, u32[]{:S(2)}, u32[]{:S(2)}) %collective-permute-start.4) | collective-permute-done | bytes 327712 | tf_op jit(solution)/shard_map/ppermute | solution.py:43
  39.3 0.1 fusion.2
  39.4 4.6 %collective-permute-start.7 = (bf16[2,16,8,1280]{3,2,1,0:T(8,128)(2,1)S(1)}, bf16[2,16,8,1280]{3,2,1,0:T(8,128)(2,1)S(1)}, u32[]{:S(2)}, u32[]{:S(2)}) collective-permute-start(bf16[2,16,8,1280]{3,2,1,0:T(8,128)(2,1)S(1)} %get-tuple-element.20), channel_id=1, source_target_pairs={{0,66},{1,385},{2,64},{3,387},{64,2},{65,449},{66,0},{67,451},{128... | collective-permute-start | bytes 1966088 | tf_op jit(solution)/shard_map/ppermute | solution.py:43
  44.1 3.1 %collective-permute-start.5 = (bf16[2,16,8,1280]{3,2,1,0:T(8,128)(2,1)S(1)}, bf16[2,16,8,1280]{3,2,1,0:T(8,128)(2,1)S(1)}, u32[]{:S(2)}, u32[]{:S(2)}) collective-permute-start(bf16[2,16,8,1280]{3,2,1,0:T(8,128)(2,1)S(1)} %get-tuple-element.20), channel_id=1, source_target_pairs={{0,128},{1,65},{2,130},{3,67},{64,192},{65,1},{66,194},{67,3},{128... | collective-permute-start | bytes 1966088 | tf_op jit(solution)/shard_map/ppermute | solution.py:43
  47.2 4.8 %collective-permute-done.7 = bf16[2,16,8,1280]{3,2,1,0:T(8,128)(2,1)S(1)} collective-permute-done((bf16[2,16,8,1280]{3,2,1,0:T(8,128)(2,1)S(1)}, bf16[2,16,8,1280]{3,2,1,0:T(8,128)(2,1)S(1)}, u32[]{:S(2)}, u32[]{:S(2)}) %collective-permute-start.7) | collective-permute-done | bytes 655392 | tf_op jit(solution)/shard_map/ppermute | solution.py:43
  52.0 4.4 %collective-permute-start.8 = (bf16[2,16,8,1280]{3,2,1,0:T(8,128)(2,1)S(1)}, bf16[2,16,8,1280]{3,2,1,0:T(8,128)(2,1)S(1)}, u32[]{:S(2)}, u32[]{:S(2)}) collective-permute-start(bf16[2,16,8,1280]{3,2,1,0:T(8,128)(2,1)S(1)} %collective-permute-done.7), channel_id=1, source_target_pairs={{0,384},{1,67},{2,386},{3,65},{64,448},{65,3},{66,450},{67,1},{128... | collective-permute-start | bytes 1966088 | tf_op jit(solution)/shard_map/ppermute | solution.py:43
  56.4 0.0 collective-permute-done.5
  56.4 0.1 pad_maximum_fusion
  56.6 3.7 %collective-permute-start.6 = (bf16[2,2,16,8,1280]{4,3,2,1,0:T(8,128)(2,1)S(1)}, bf16[2,2,16,8,1280]{4,3,2,1,0:T(8,128)(2,1)S(1)}, u32[]{:S(2)}, u32[]{:S(2)}) collective-permute-start(bf16[2,2,16,8,1280]{4,3,2,1,0:T(8,128)(2,1)S(1)} %pad_maximum_fusion), channel_id=1, source_target_pairs={{0,384},{1,67},{2,386},{3,65},{64,448},{65,3},{66,450},{67,1},{128... | collective-permute-start | bytes 3932168 | tf_op jit(solution)/shard_map/ppermute | solution.py:43
  60.2 8.3 %collective-permute-done.8 = bf16[2,16,8,1280]{3,2,1,0:T(8,128)(2,1)S(1)} collective-permute-done((bf16[2,16,8,1280]{3,2,1,0:T(8,128)(2,1)S(1)}, bf16[2,16,8,1280]{3,2,1,0:T(8,128)(2,1)S(1)}, u32[]{:S(2)}, u32[]{:S(2)}) %collective-permute-start.8) | collective-permute-done | bytes 655392 | tf_op jit(solution)/shard_map/ppermute | solution.py:43
  68.5 0.0 copy-start
  68.6 0.0 copy-start.1
  68.6 0.1 pad_maximum_fusion.1
  68.7 2.1 %collective-permute-start.9 = (bf16[2,2,16,8,1280]{4,3,2,1,0:T(8,128)(2,1)S(1)}, bf16[2,2,16,8,1280]{4,3,2,1,0:T(8,128)(2,1)S(1)}, u32[]{:S(2)}, u32[]{:S(2)}) collective-permute-start(bf16[2,2,16,8,1280]{4,3,2,1,0:T(8,128)(2,1)S(1)} %pad_maximum_fusion.1), channel_id=1, source_target_pairs={{0,128},{1,65},{2,130},{3,67},{64,192},{65,1},{66,194},{67,3},{128... | collective-permute-start | bytes 3932168 | tf_op jit(solution)/shard_map/ppermute | solution.py:43
  70.7 0.0 copy-done
  70.8 0.0 copy-done.1
  70.8 0.0 copy-start.2
  70.8 0.2 masks.1
  71.0 1.9 %collective-permute-start = (bf16[2,7,16,128]{3,2,1,0:T(8,128)(2,1)S(1)}, bf16[2,7,16,128]{3,2,1,0:T(8,128)(2,1)S(1)}, u32[]{:S(2)}, u32[]{:S(2)}) collective-permute-start(bf16[2,7,16,128]{3,2,1,0:T(8,128)(2,1)S(1)} %pad_maximum_fusion.5), channel_id=1, source_target_pairs={{0,4},{4,8},{8,12},{12,16},{16,20},{20,24},{24,28},{28,32},{32,36}... | collective-permute-start | bytes 172040 | tf_op jit(solution)/shard_map/ppermute | solution.py:337
  73.0 18.3 %collective-permute-start.10 = (bf16[2,2,16,8,1280]{4,3,2,1,0:T(8,128)(2,1)S(1)}, bf16[2,2,16,8,1280]{4,3,2,1,0:T(8,128)(2,1)S(1)}, u32[]{:S(2)}, u32[]{:S(2)}) collective-permute-start(bf16[2,2,16,8,1280]{4,3,2,1,0:T(8,128)(2,1)S(1)} %pad_maximum_fusion), channel_id=1, source_target_pairs={{0,1},{1,0},{2,3},{3,2},{4,5},{5,4},{6,7},{7,6},{8,9},{9,8},{10,11... | collective-permute-start | bytes 3932168 | tf_op jit(solution)/shard_map/ppermute | solution.py:51
  91.3 1.9 %collective-permute-start.12 = (bf16[2,2,16,8,1280]{4,3,2,1,0:T(8,128)(2,1)S(1)}, bf16[2,2,16,8,1280]{4,3,2,1,0:T(8,128)(2,1)S(1)}, u32[]{:S(2)}, u32[]{:S(2)}) collective-permute-start(bf16[2,2,16,8,1280]{4,3,2,1,0:T(8,128)(2,1)S(1)} %pad_maximum_fusion.1), channel_id=1, source_target_pairs={{0,1},{1,0},{2,3},{3,2},{4,5},{5,4},{6,7},{7,6},{8,9},{9,8},{10,11... | collective-permute-start | bytes 3932168 | tf_op jit(solution)/shard_map/ppermute | solution.py:51
  93.2 0.0 collective-permute-done.6
  93.2 7.9 %collective-permute-start.11 = (bf16[2,2,16,8,1280]{4,3,2,1,0:T(8,128)(2,1)S(1)}, bf16[2,2,16,8,1280]{4,3,2,1,0:T(8,128)(2,1)S(1)}, u32[]{:S(2)}, u32[]{:S(2)}) collective-permute-start(bf16[2,2,16,8,1280]{4,3,2,1,0:T(8,128)(2,1)S(1)} %collective-permute-done.6), channel_id=1, source_target_pairs={{0,1},{1,0},{2,3},{3,2},{4,5},{5,4},{6,7},{7,6},{8,9},{9,8},{10,11... | collective-permute-start | bytes 3932168 | tf_op jit(solution)/shard_map/ppermute | solution.py:51
  101.1 0.0 collective-permute-done.9
  101.1 5.1 %collective-permute-start.13 = (bf16[2,2,16,8,1280]{4,3,2,1,0:T(8,128)(2,1)S(1)}, bf16[2,2,16,8,1280]{4,3,2,1,0:T(8,128)(2,1)S(1)}, u32[]{:S(2)}, u32[]{:S(2)}) collective-permute-start(bf16[2,2,16,8,1280]{4,3,2,1,0:T(8,128)(2,1)S(1)} %collective-permute-done.9), channel_id=1, source_target_pairs={{0,1},{1,0},{2,3},{3,2},{4,5},{5,4},{6,7},{7,6},{8,9},{9,8},{10,11... | collective-permute-start | bytes 3932168 | tf_op jit(solution)/shard_map/ppermute | solution.py:51
  106.2 0.1 fusion.3
  106.4 0.0 collective-permute-done.lon_w
  106.4 1.9 %collective-permute-start.1 = (bf16[2,7,16,128]{3,2,1,0:T(8,128)(2,1)S(1)}, bf16[2,7,16,128]{3,2,1,0:T(8,128)(2,1)S(1)}, u32[]{:S(2)}, u32[]{:S(2)}) collective-permute-start(bf16[2,7,16,128]{3,2,1,0:T(8,128)(2,1)S(1)} %pad_maximum_fusion.6), channel_id=1, source_target_pairs={{4,0},{8,4},{12,8},{16,12},{20,16},{24,20},{28,24},{32,28},{36,32}... | collective-permute-start | bytes 172040 | tf_op jit(solution)/shard_map/ppermute | solution.py:340
  108.3 3.4 %collective-permute-done.1.lon_e = bf16[2,7,16,128]{3,2,1,0:T(8,128)(2,1)S(1)} collective-permute-done((bf16[2,7,16,128]{3,2,1,0:T(8,128)(2,1)S(1)}, bf16[2,7,16,128]{3,2,1,0:T(8,128)(2,1)S(1)}, u32[]{:S(2)}, u32[]{:S(2)}) %collective-permute-start.1) | collective-permute-done | bytes 57376 | tf_op jit(solution)/shard_map/ppermute | solution.py:340
  111.8 0.1 pad_maximum_fusion.3
  111.9 4.2 %collective-permute-start.2 = (bf16[22,7,2,128]{3,2,1,0:T(2,128)(2,1)S(1)}, bf16[22,7,2,128]{3,2,1,0:T(2,128)(2,1)S(1)}, u32[]{:S(2)}, u32[]{:S(2)}) collective-permute-start(bf16[22,7,2,128]{3,2,1,0:T(2,128)(2,1)S(1)} %pad_maximum_fusion.3), channel_id=1, source_target_pairs={{0,1},{1,2},{2,3},{4,5},{5,6},{6,7},{8,9},{9,10},{10,11},{12,13},{... | collective-permute-start | bytes 236552 | tf_op jit(solution)/shard_map/ppermute | solution.py:350
  116.1 0.1 pad_maximum_fusion.4
  116.2 1.3 collective-permute-done.2.lat_s
  117.5 2.1 %collective-permute-start.3 = (bf16[22,7,2,128]{3,2,1,0:T(2,128)(2,1)S(1)}, bf16[22,7,2,128]{3,2,1,0:T(2,128)(2,1)S(1)}, u32[]{:S(2)}, u32[]{:S(2)}) collective-permute-start(bf16[22,7,2,128]{3,2,1,0:T(2,128)(2,1)S(1)} %pad_maximum_fusion.4), channel_id=1, source_target_pairs={{1,0},{2,1},{3,2},{5,4},{6,5},{7,6},{9,8},{10,9},{11,10},{13,12},{... | collective-permute-start | bytes 236552 | tf_op jit(solution)/shard_map/ppermute | solution.py:351
  119.6 5.8 %collective-permute-done.3.lat_n = bf16[22,7,2,128]{3,2,1,0:T(2,128)(2,1)S(1)} collective-permute-done((bf16[22,7,2,128]{3,2,1,0:T(2,128)(2,1)S(1)}, bf16[22,7,2,128]{3,2,1,0:T(2,128)(2,1)S(1)}, u32[]{:S(2)}, u32[]{:S(2)}) %collective-permute-start.3) | collective-permute-done | bytes 78880 | tf_op jit(solution)/shard_map/ppermute | solution.py:351
  125.4 3.2 %prepare.1 = (f32[400,768]{1,0:T(8,128)S(1)}, bf16[400,768]{1,0:T(8,128)(2,1)S(1)}, f32[400,128]{1,0:T(8,128)S(1)}) custom-call(f32[20,6,16,128]{3,2,1,0:T(8,128)S(1)} %bitcast.35, f32[20,16,128]{2,1,0:T(8,128)S(1)} %get-tuple-element.10.mask, bf16[2,7,16,128]{3,2,1,0:T(8,128)(2,1)S(1)} %collective-permute-done.lon_w, ...), custom_call_target="tpu_custom_call" | custom-call | tf_op jit(solution)/shard_map/prepare/pallas_call | solution.py:369
  128.7 0.0 collective-permute-done.10
  128.7 0.0 collective-permute-done.12
  128.7 0.0 collective-permute-done.11
  128.7 0.0 collective-permute-done.13
  128.7 0.0 copy-done.2
  128.7 14.5 %steps.1 = f32[20,6,16,128]{3,2,1,0:T(8,128)} custom-call(s32[1024]{0:T(1024)S(1)} %copy-done.2, bf16[400,768]{1,0:T(8,128)(2,1)S(1)} %get-tuple-element.11.x1, f32[400,768]{1,0:T(8,128)S(1)} %get-tuple-element.12.moved1_any, f32[400,128]{1,0:T(8,128)S(1)} %get-tuple-element.13.mask0, f32[20,16,128]{2,1,0:T(8,128)S(1)} %get-tuple-element.14.mask1, ...), custom_call_target="tpu_custom_call" | custom-call | tf_op jit(solution)/shard_map/steps/pallas_call | solution.py:371
  (8 shorter events, 0.1 us)
Async XLA Ops:
  31.5 7.8 %collective-permute-start.4 = (bf16[16,8,1280]{2,1,0:T(8,128)(2,1)S(1)}, bf16[16,8,1280]{2,1,0:T(8,128)(2,1)S(1)}, u32[]{:S(2)}, u32[]{:S(2)}) collective-permute-start(bf16[16,8,1280]{2,1,0:T(8,128)(2,1)S(1)} %all_gather.3), channel_id=1, source_target_pairs={{0,64},{1,129},{2,66},{3,131},{64,0},{65,193},{66,2},{67,195},{128... | collective-permute-start | bytes 983048 | tf_op jit(solution)/shard_map/ppermute | solution.py:43
  39.4 12.6 %collective-permute-start.7 = (bf16[2,16,8,1280]{3,2,1,0:T(8,128)(2,1)S(1)}, bf16[2,16,8,1280]{3,2,1,0:T(8,128)(2,1)S(1)}, u32[]{:S(2)}, u32[]{:S(2)}) collective-permute-start(bf16[2,16,8,1280]{3,2,1,0:T(8,128)(2,1)S(1)} %get-tuple-element.20), channel_id=1, source_target_pairs={{0,66},{1,385},{2,64},{3,387},{64,2},{65,449},{66,0},{67,451},{128... | collective-permute-start | bytes 1966088 | tf_op jit(solution)/shard_map/ppermute | solution.py:43
  44.1 12.4 %collective-permute-start.5 = (bf16[2,16,8,1280]{3,2,1,0:T(8,128)(2,1)S(1)}, bf16[2,16,8,1280]{3,2,1,0:T(8,128)(2,1)S(1)}, u32[]{:S(2)}, u32[]{:S(2)}) collective-permute-start(bf16[2,16,8,1280]{3,2,1,0:T(8,128)(2,1)S(1)} %get-tuple-element.20), channel_id=1, source_target_pairs={{0,128},{1,65},{2,130},{3,67},{64,192},{65,1},{66,194},{67,3},{128... | collective-permute-start | bytes 1966088 | tf_op jit(solution)/shard_map/ppermute | solution.py:43
  52.0 16.5 %collective-permute-start.8 = (bf16[2,16,8,1280]{3,2,1,0:T(8,128)(2,1)S(1)}, bf16[2,16,8,1280]{3,2,1,0:T(8,128)(2,1)S(1)}, u32[]{:S(2)}, u32[]{:S(2)}) collective-permute-start(bf16[2,16,8,1280]{3,2,1,0:T(8,128)(2,1)S(1)} %collective-permute-done.7), channel_id=1, source_target_pairs={{0,384},{1,67},{2,386},{3,65},{64,448},{65,3},{66,450},{67,1},{128... | collective-permute-start | bytes 1966088 | tf_op jit(solution)/shard_map/ppermute | solution.py:43
  56.6 36.6 %collective-permute-start.6 = (bf16[2,2,16,8,1280]{4,3,2,1,0:T(8,128)(2,1)S(1)}, bf16[2,2,16,8,1280]{4,3,2,1,0:T(8,128)(2,1)S(1)}, u32[]{:S(2)}, u32[]{:S(2)}) collective-permute-start(bf16[2,2,16,8,1280]{4,3,2,1,0:T(8,128)(2,1)S(1)} %pad_maximum_fusion), channel_id=1, source_target_pairs={{0,384},{1,67},{2,386},{3,65},{64,448},{65,3},{66,450},{67,1},{128... | collective-permute-start | bytes 3932168 | tf_op jit(solution)/shard_map/ppermute | solution.py:43
  68.5 2.2 %copy-start = (f32[16,20,6,128]{3,0,2,1:T(8,128)S(1)}, f32[16,20,6,128]{3,0,2,1:T(8,128)}, u32[]{:S(2)}) copy-start(f32[16,20,6,128]{3,0,2,1:T(8,128)} %param.6) | copy-start | bytes 2949124
  68.6 2.2 %copy-start.1 = (s32[2,16,20]{2,1,0:T(8,128)S(1)}, s32[2,16,20]{2,1,0:T(8,128)}, u32[]{:S(2)}) copy-start(s32[2,16,20]{2,1,0:T(8,128)} %days.1) | copy-start | bytes 7684
  68.7 32.5 %collective-permute-start.9 = (bf16[2,2,16,8,1280]{4,3,2,1,0:T(8,128)(2,1)S(1)}, bf16[2,2,16,8,1280]{4,3,2,1,0:T(8,128)(2,1)S(1)}, u32[]{:S(2)}, u32[]{:S(2)}) collective-permute-start(bf16[2,2,16,8,1280]{4,3,2,1,0:T(8,128)(2,1)S(1)} %pad_maximum_fusion.1), channel_id=1, source_target_pairs={{0,128},{1,65},{2,130},{3,67},{64,192},{65,1},{66,194},{67,3},{128... | collective-permute-start | bytes 3932168 | tf_op jit(solution)/shard_map/ppermute | solution.py:43
  70.8 57.9 %copy-start.2 = (s32[1024]{0:T(1024)S(1)}, s32[1024]{0:T(1024)}, u32[]{:S(2)}) copy-start(s32[1024]{0:T(1024)} %constant.16.clone.positions) | copy-start | bytes 12292
  71.0 35.3 %collective-permute-start = (bf16[2,7,16,128]{3,2,1,0:T(8,128)(2,1)S(1)}, bf16[2,7,16,128]{3,2,1,0:T(8,128)(2,1)S(1)}, u32[]{:S(2)}, u32[]{:S(2)}) collective-permute-start(bf16[2,7,16,128]{3,2,1,0:T(8,128)(2,1)S(1)} %pad_maximum_fusion.5), channel_id=1, source_target_pairs={{0,4},{4,8},{8,12},{12,16},{16,20},{20,24},{24,28},{28,32},{32,36}... | collective-permute-start | bytes 172040 | tf_op jit(solution)/shard_map/ppermute | solution.py:337
  73.0 55.7 %collective-permute-start.10 = (bf16[2,2,16,8,1280]{4,3,2,1,0:T(8,128)(2,1)S(1)}, bf16[2,2,16,8,1280]{4,3,2,1,0:T(8,128)(2,1)S(1)}, u32[]{:S(2)}, u32[]{:S(2)}) collective-permute-start(bf16[2,2,16,8,1280]{4,3,2,1,0:T(8,128)(2,1)S(1)} %pad_maximum_fusion), channel_id=1, source_target_pairs={{0,1},{1,0},{2,3},{3,2},{4,5},{5,4},{6,7},{7,6},{8,9},{9,8},{10,11... | collective-permute-start | bytes 3932168 | tf_op jit(solution)/shard_map/ppermute | solution.py:51
  91.3 37.4 %collective-permute-start.12 = (bf16[2,2,16,8,1280]{4,3,2,1,0:T(8,128)(2,1)S(1)}, bf16[2,2,16,8,1280]{4,3,2,1,0:T(8,128)(2,1)S(1)}, u32[]{:S(2)}, u32[]{:S(2)}) collective-permute-start(bf16[2,2,16,8,1280]{4,3,2,1,0:T(8,128)(2,1)S(1)} %pad_maximum_fusion.1), channel_id=1, source_target_pairs={{0,1},{1,0},{2,3},{3,2},{4,5},{5,4},{6,7},{7,6},{8,9},{9,8},{10,11... | collective-permute-start | bytes 3932168 | tf_op jit(solution)/shard_map/ppermute | solution.py:51
  93.2 35.5 %collective-permute-start.11 = (bf16[2,2,16,8,1280]{4,3,2,1,0:T(8,128)(2,1)S(1)}, bf16[2,2,16,8,1280]{4,3,2,1,0:T(8,128)(2,1)S(1)}, u32[]{:S(2)}, u32[]{:S(2)}) collective-permute-start(bf16[2,2,16,8,1280]{4,3,2,1,0:T(8,128)(2,1)S(1)} %collective-permute-done.6), channel_id=1, source_target_pairs={{0,1},{1,0},{2,3},{3,2},{4,5},{5,4},{6,7},{7,6},{8,9},{9,8},{10,11... | collective-permute-start | bytes 3932168 | tf_op jit(solution)/shard_map/ppermute | solution.py:51
  101.1 27.5 %collective-permute-start.13 = (bf16[2,2,16,8,1280]{4,3,2,1,0:T(8,128)(2,1)S(1)}, bf16[2,2,16,8,1280]{4,3,2,1,0:T(8,128)(2,1)S(1)}, u32[]{:S(2)}, u32[]{:S(2)}) collective-permute-start(bf16[2,2,16,8,1280]{4,3,2,1,0:T(8,128)(2,1)S(1)} %collective-permute-done.9), channel_id=1, source_target_pairs={{0,1},{1,0},{2,3},{3,2},{4,5},{5,4},{6,7},{7,6},{8,9},{9,8},{10,11... | collective-permute-start | bytes 3932168 | tf_op jit(solution)/shard_map/ppermute | solution.py:51
  106.4 5.4 %collective-permute-start.1 = (bf16[2,7,16,128]{3,2,1,0:T(8,128)(2,1)S(1)}, bf16[2,7,16,128]{3,2,1,0:T(8,128)(2,1)S(1)}, u32[]{:S(2)}, u32[]{:S(2)}) collective-permute-start(bf16[2,7,16,128]{3,2,1,0:T(8,128)(2,1)S(1)} %pad_maximum_fusion.6), channel_id=1, source_target_pairs={{4,0},{8,4},{12,8},{16,12},{20,16},{24,20},{28,24},{32,28},{36,32}... | collective-permute-start | bytes 172040 | tf_op jit(solution)/shard_map/ppermute | solution.py:340
  111.9 5.7 %collective-permute-start.2 = (bf16[22,7,2,128]{3,2,1,0:T(2,128)(2,1)S(1)}, bf16[22,7,2,128]{3,2,1,0:T(2,128)(2,1)S(1)}, u32[]{:S(2)}, u32[]{:S(2)}) collective-permute-start(bf16[22,7,2,128]{3,2,1,0:T(2,128)(2,1)S(1)} %pad_maximum_fusion.3), channel_id=1, source_target_pairs={{0,1},{1,2},{2,3},{4,5},{5,6},{6,7},{8,9},{9,10},{10,11},{12,13},{... | collective-permute-start | bytes 236552 | tf_op jit(solution)/shard_map/ppermute | solution.py:350
  117.5 7.9 %collective-permute-start.3 = (bf16[22,7,2,128]{3,2,1,0:T(2,128)(2,1)S(1)}, bf16[22,7,2,128]{3,2,1,0:T(2,128)(2,1)S(1)}, u32[]{:S(2)}, u32[]{:S(2)}) collective-permute-start(bf16[22,7,2,128]{3,2,1,0:T(2,128)(2,1)S(1)} %pad_maximum_fusion.4), channel_id=1, source_target_pairs={{1,0},{2,1},{3,2},{5,4},{6,5},{7,6},{9,8},{10,9},{11,10},{13,12},{... | collective-permute-start | bytes 236552 | tf_op jit(solution)/shard_map/ppermute | solution.py:351

commit v7 on v6

--- a/solution.py
+++ b/solution.py
@@ -329,22 +329,27 @@
     )
     masks = spread_masks(day_mask)
     lon_n, lat_n_blocks = 128, 4
-
-    def packed(cols, rows):
-        part = lax.optimization_barrier(ft[cols, :, rows]).astype(jnp.bfloat16)
-        return jnp.concatenate([part, masks[0][cols, None, rows].astype(jnp.bfloat16)], axis=1)
-
-    lon_w = lax.ppermute(
-        packed(slice(C - 2, C), slice(0, R)), LON, [(i, (i + 1) % lon_n) for i in range(lon_n)]
-    )
-    lon_e = lax.ppermute(
-        packed(slice(0, 2), slice(0, R)), LON, [((i + 1) % lon_n, i) for i in range(lon_n)]
-    )
+    even = lax.axis_index("z") % 2 == 0
+
+    def as_sent(part, mask):
+        return jnp.concatenate(
+            [part.astype(jnp.bfloat16), mask[:, None].astype(jnp.bfloat16)], axis=1
+        )
+
+    def lon_swap(first, at_end):
+        start = jnp.where(at_end, C - 2, 0)
+        cols = as_sent(*(lax.dynamic_slice_in_dim(v, start, 2, 0) for v in (ft, masks[0])))
+        pairs = []
+        for i in range(first, lon_n + first, 2):
+            pairs += [(i % lon_n, (i + 1) % lon_n), ((i + 1) % lon_n, i % lon_n)]
+        return lax.ppermute(cols, LON, pairs)
+
+    met, other = lon_swap(0, even), lon_swap(1, ~even)
+    lon_w, lon_e = jnp.where(even, other, met), jnp.where(even, met, other)
 
     def wide(rows):
-        return jnp.concatenate(
-            [lon_w[1:, :, rows], packed(slice(0, C), rows), lon_e[:1, :, rows]], axis=0
-        )
+        own = as_sent(lax.optimization_barrier(ft[:, :, rows]), masks[0][:, rows])
+        return jnp.concatenate([lon_w[1:, :, rows], own, lon_e[:1, :, rows]], axis=0)
 
     ends = range(lat_n_blocks - 1)
     lat_s = lax.ppermute(wide(slice(R - 2, R)), LAT, [(i, i + 1) for i in ends])

time: 144 us -> 145 us (level)
  local copies, waits for them, and re-layouts: 0.16 us -> 2.37 us
    ppermute x4, starting transfers between devices: 33.2 us -> 27.8 us  [core_swap(): return lax.ppermute(a, 'core', [(0, 1), (1, 0)])]
    ppermute x2, starting transfers between devices: 3.84 us -> 8.36 us  [lon_swap(): return lax.ppermute(cols, LON, pairs)]
  transfers between devices with their start and end apart: 14 -> 14, of which waited for: 6 -> 6; matrix products, arithmetic and copies ran while one was open for 0% -> 2% of each run, Pallas kernels for 2% -> 2%
where the time goes in v7:
time: 145 us; the launch traced here: 144 us
  starting transfers between devices  63.2 us (44%)
  blocking collectives  30.8 us (21%)
  waiting for transfers between devices  28.4 us (20%)
  Pallas kernels  18 us (12%)
  local copies, waits for them, and re-layouts  2.37 us (2%)
    all_gather x1, blocking collectives, gather_weights(): z = lax.all_gather(block, 'z', axis=0)  30.8 us
    ppermute x4, starting transfers between devices, core_swap(): return lax.ppermute(a, 'core', [(0, 1), (1, 0)])  27.8 us
    ppermute x6, starting transfers between devices, exchange(): return lax.ppermute(a, ('y', 'xl', 'xh', 'core'), pairs)  20.9 us
    ppermute x6, waiting for transfers between devices, exchange(): return lax.ppermute(a, ('y', 'xl', 'xh', 'core'), pairs)  17.8 us
    pallas_call x1, Pallas kernels, shards(): steps_call()  14.5 us
    ppermute x2, starting transfers between devices, lon_swap(): return lax.ppermute(cols, LON, pairs)  8.36 us
    ppermute x1, waiting for transfers between devices, shards(): lat_n = lax.ppermute(wide(slice(0, 2)), LAT, [(i + 1, i) for i in ends])  5.95 us
    ppermute x1, starting transfers between devices, shards(): lat_s = lax.ppermute(wide(slice(R - 2, R)), LAT, [(i, i + 1) for i in ends])  4.21 us
  transfers between devices with their start and end apart: 14, of which 6 were waited for; matrix products, arithmetic and copies ran while one was open for 2% of the time, Pallas kernels for 2%

profile of v7, /device:TPU:1, one launch (start us, length us, event | category | flops | bytes accessed | tf_op | source)
XLA Modules:
  0.0 144.4 jit_solution(13112940362342437905)
XLA Ops:
  0.0 0.7 fusion.3
  0.7 30.8 %all_gather.3 = bf16[16,8,1280]{2,1,0:T(8,128)(2,1)S(1)} all-gather(bf16[1,8,1280]{2,1,0:T(8,128)(2,1)S(1)} %fusion.3), channel_id=1, replica_groups=mesh['y'=4,'xl'=2,'z'=16,'xh'=2,'core'=2] {'z'}, dimensions={0}, use_global_device_ids=true | all-gather | bytes 348160 | tf_op jit(solution)/shard_map/all_gather | solution.py:55
  31.5 3.2 %collective-permute-start.4 = (bf16[16,8,1280]{2,1,0:T(8,128)(2,1)S(1)}, bf16[16,8,1280]{2,1,0:T(8,128)(2,1)S(1)}, u32[]{:S(2)}, u32[]{:S(2)}) collective-permute-start(bf16[16,8,1280]{2,1,0:T(8,128)(2,1)S(1)} %all_gather.3), channel_id=1, source_target_pairs={{0,64},{1,129},{2,66},{3,131},{64,0},{65,193},{66,2},{67,195},{128... | collective-permute-start | bytes 983048 | tf_op jit(solution)/shard_map/ppermute | solution.py:43
  34.7 4.6 %collective-permute-done.4 = bf16[16,8,1280]{2,1,0:T(8,128)(2,1)S(1)} collective-permute-done((bf16[16,8,1280]{2,1,0:T(8,128)(2,1)S(1)}, bf16[16,8,1280]{2,1,0:T(8,128)(2,1)S(1)}, u32[]{:S(2)}, u32[]{:S(2)}) %collective-permute-start.4) | collective-permute-done | bytes 327712 | tf_op jit(solution)/shard_map/ppermute | solution.py:43
  39.3 0.1 fusion.6
  39.4 4.6 %collective-permute-start.7 = (bf16[2,16,8,1280]{3,2,1,0:T(8,128)(2,1)S(1)}, bf16[2,16,8,1280]{3,2,1,0:T(8,128)(2,1)S(1)}, u32[]{:S(2)}, u32[]{:S(2)}) collective-permute-start(bf16[2,16,8,1280]{3,2,1,0:T(8,128)(2,1)S(1)} %get-tuple-element.20), channel_id=1, source_target_pairs={{0,66},{1,385},{2,64},{3,387},{64,2},{65,449},{66,0},{67,451},{128... | collective-permute-start | bytes 1966088 | tf_op jit(solution)/shard_map/ppermute | solution.py:43
  44.1 3.1 %collective-permute-start.5 = (bf16[2,16,8,1280]{3,2,1,0:T(8,128)(2,1)S(1)}, bf16[2,16,8,1280]{3,2,1,0:T(8,128)(2,1)S(1)}, u32[]{:S(2)}, u32[]{:S(2)}) collective-permute-start(bf16[2,16,8,1280]{3,2,1,0:T(8,128)(2,1)S(1)} %get-tuple-element.20), channel_id=1, source_target_pairs={{0,128},{1,65},{2,130},{3,67},{64,192},{65,1},{66,194},{67,3},{128... | collective-permute-start | bytes 1966088 | tf_op jit(solution)/shard_map/ppermute | solution.py:43
  47.2 4.8 %collective-permute-done.7 = bf16[2,16,8,1280]{3,2,1,0:T(8,128)(2,1)S(1)} collective-permute-done((bf16[2,16,8,1280]{3,2,1,0:T(8,128)(2,1)S(1)}, bf16[2,16,8,1280]{3,2,1,0:T(8,128)(2,1)S(1)}, u32[]{:S(2)}, u32[]{:S(2)}) %collective-permute-start.7) | collective-permute-done | bytes 655392 | tf_op jit(solution)/shard_map/ppermute | solution.py:43
  52.0 4.4 %collective-permute-start.8 = (bf16[2,16,8,1280]{3,2,1,0:T(8,128)(2,1)S(1)}, bf16[2,16,8,1280]{3,2,1,0:T(8,128)(2,1)S(1)}, u32[]{:S(2)}, u32[]{:S(2)}) collective-permute-start(bf16[2,16,8,1280]{3,2,1,0:T(8,128)(2,1)S(1)} %collective-permute-done.7), channel_id=1, source_target_pairs={{0,384},{1,67},{2,386},{3,65},{64,448},{65,3},{66,450},{67,1},{128... | collective-permute-start | bytes 1966088 | tf_op jit(solution)/shard_map/ppermute | solution.py:43
  56.4 0.0 collective-permute-done.5
  56.4 0.1 pad_maximum_fusion
  56.6 3.7 %collective-permute-start.6 = (bf16[2,2,16,8,1280]{4,3,2,1,0:T(8,128)(2,1)S(1)}, bf16[2,2,16,8,1280]{4,3,2,1,0:T(8,128)(2,1)}, u32[]{:S(2)}, u32[]{:S(2)}) collective-permute-start(bf16[2,2,16,8,1280]{4,3,2,1,0:T(8,128)(2,1)S(1)} %pad_maximum_fusion), channel_id=1, source_target_pairs={{0,384},{1,67},{2,386},{3,65},{64,448},{65,3},{66,450},{67,1},{128... | collective-permute-start | bytes 3932168 | tf_op jit(solution)/shard_map/ppermute | solution.py:43
  60.2 8.3 %collective-permute-done.8 = bf16[2,16,8,1280]{3,2,1,0:T(8,128)(2,1)S(1)} collective-permute-done((bf16[2,16,8,1280]{3,2,1,0:T(8,128)(2,1)S(1)}, bf16[2,16,8,1280]{3,2,1,0:T(8,128)(2,1)S(1)}, u32[]{:S(2)}, u32[]{:S(2)}) %collective-permute-start.8) | collective-permute-done | bytes 655392 | tf_op jit(solution)/shard_map/ppermute | solution.py:43
  68.5 0.0 copy-start.1
  68.6 0.1 pad_maximum_fusion.1
  68.7 1.9 %collective-permute-start.9 = (bf16[2,2,16,8,1280]{4,3,2,1,0:T(8,128)(2,1)S(1)}, bf16[2,2,16,8,1280]{4,3,2,1,0:T(8,128)(2,1)}, u32[]{:S(2)}, u32[]{:S(2)}) collective-permute-start(bf16[2,2,16,8,1280]{4,3,2,1,0:T(8,128)(2,1)S(1)} %pad_maximum_fusion.1), channel_id=1, source_target_pairs={{0,128},{1,65},{2,130},{3,67},{64,192},{65,1},{66,194},{67,3},{128... | collective-permute-start | bytes 3932168 | tf_op jit(solution)/shard_map/ppermute | solution.py:43
  70.6 0.0 copy-done.1
  70.6 0.0 copy-start
  70.6 0.2 masks.1
  70.9 1.0 fusion.1
  71.9 0.0 copy-start.2
  71.9 6.4 %collective-permute-start = (bf16[2,7,16,128]{3,2,1,0:T(8,128)(2,1)S(1)}, bf16[2,7,16,128]{3,2,1,0:T(8,128)(2,1)S(1)}, u32[]{:S(2)}, u32[]{:S(2)}) collective-permute-start(bf16[2,7,16,128]{3,2,1,0:T(8,128)(2,1)S(1)} %pad_maximum_fusion.5), channel_id=1, source_target_pairs={{4,8},{8,4},{12,16},{16,12},{20,24},{24,20},{28,32},{32,28},{36,40... | collective-permute-start | bytes 172040 | tf_op jit(solution)/shard_map/ppermute | solution.py:345
  78.4 13.8 %collective-permute-start.10 = (bf16[2,2,16,8,1280]{4,3,2,1,0:T(8,128)(2,1)S(1)}, bf16[2,2,16,8,1280]{4,3,2,1,0:T(8,128)(2,1)S(1)}, u32[]{:S(2)}, u32[]{:S(2)}) collective-permute-start(bf16[2,2,16,8,1280]{4,3,2,1,0:T(8,128)(2,1)S(1)} %pad_maximum_fusion), channel_id=1, source_target_pairs={{0,1},{1,0},{2,3},{3,2},{4,5},{5,4},{6,7},{7,6},{8,9},{9,8},{10,11... | collective-permute-start | bytes 3932168 | tf_op jit(solution)/shard_map/ppermute | solution.py:51
  92.2 1.9 %collective-permute-start.12 = (bf16[2,2,16,8,1280]{4,3,2,1,0:T(8,128)(2,1)S(1)}, bf16[2,2,16,8,1280]{4,3,2,1,0:T(8,128)(2,1)S(1)}, u32[]{:S(2)}, u32[]{:S(2)}) collective-permute-start(bf16[2,2,16,8,1280]{4,3,2,1,0:T(8,128)(2,1)S(1)} %pad_maximum_fusion.1), channel_id=1, source_target_pairs={{0,1},{1,0},{2,3},{3,2},{4,5},{5,4},{6,7},{7,6},{8,9},{9,8},{10,11... | collective-permute-start | bytes 3932168 | tf_op jit(solution)/shard_map/ppermute | solution.py:51
  94.1 0.0 collective-permute-done.6
  94.1 7.1 %collective-permute-start.11 = (bf16[2,2,16,8,1280]{4,3,2,1,0:T(8,128)(2,1)}, bf16[2,2,16,8,1280]{4,3,2,1,0:T(8,128)(2,1)S(1)}, u32[]{:S(2)}, u32[]{:S(2)}) collective-permute-start(bf16[2,2,16,8,1280]{4,3,2,1,0:T(8,128)(2,1)} %collective-permute-done.6), channel_id=1, source_target_pairs={{0,1},{1,0},{2,3},{3,2},{4,5},{5,4},{6,7},{7,6},{8,9},{9,8},{10,11... | collective-permute-start | bytes 3932168 | tf_op jit(solution)/shard_map/ppermute | solution.py:51
  101.2 0.0 collective-permute-done.9
  101.2 5.0 %collective-permute-start.13 = (bf16[2,2,16,8,1280]{4,3,2,1,0:T(8,128)(2,1)}, bf16[2,2,16,8,1280]{4,3,2,1,0:T(8,128)(2,1)S(1)}, u32[]{:S(2)}, u32[]{:S(2)}) collective-permute-start(bf16[2,2,16,8,1280]{4,3,2,1,0:T(8,128)(2,1)} %collective-permute-done.9), channel_id=1, source_target_pairs={{0,1},{1,0},{2,3},{3,2},{4,5},{5,4},{6,7},{7,6},{8,9},{9,8},{10,11... | collective-permute-start | bytes 3932168 | tf_op jit(solution)/shard_map/ppermute | solution.py:51
  106.2 1.3 fusion.7
  107.5 0.0 collective-permute-done
  107.5 1.9 %collective-permute-start.1 = (bf16[2,7,16,128]{3,2,1,0:T(8,128)(2,1)S(1)}, bf16[2,7,16,128]{3,2,1,0:T(8,128)(2,1)S(1)}, u32[]{:S(2)}, u32[]{:S(2)}) collective-permute-start(bf16[2,7,16,128]{3,2,1,0:T(8,128)(2,1)S(1)} %pad_maximum_fusion.6), channel_id=1, source_target_pairs={{0,4},{4,0},{8,12},{12,8},{16,20},{20,16},{24,28},{28,24},{32,36},... | collective-permute-start | bytes 172040 | tf_op jit(solution)/shard_map/ppermute | solution.py:345
  109.5 3.4 %collective-permute-done.1 = bf16[2,7,16,128]{3,2,1,0:T(8,128)(2,1)S(1)} collective-permute-done((bf16[2,7,16,128]{3,2,1,0:T(8,128)(2,1)S(1)}, bf16[2,7,16,128]{3,2,1,0:T(8,128)(2,1)S(1)}, u32[]{:S(2)}, u32[]{:S(2)}) %collective-permute-start.1) | collective-permute-done | bytes 57376 | tf_op jit(solution)/shard_map/ppermute | solution.py:345
  112.9 0.1 pad_maximum_fusion.3
  113.0 4.2 %collective-permute-start.2 = (bf16[22,7,2,128]{3,2,1,0:T(2,128)(2,1)S(1)}, bf16[22,7,2,128]{3,2,1,0:T(2,128)(2,1)S(1)}, u32[]{:S(2)}, u32[]{:S(2)}) collective-permute-start(bf16[22,7,2,128]{3,2,1,0:T(2,128)(2,1)S(1)} %pad_maximum_fusion.3), channel_id=1, source_target_pairs={{0,1},{1,2},{2,3},{4,5},{5,6},{6,7},{8,9},{9,10},{10,11},{12,13},{... | collective-permute-start | bytes 236552 | tf_op jit(solution)/shard_map/ppermute | solution.py:355
  117.3 0.1 pad_maximum_fusion.4
  117.4 1.3 collective-permute-done.2.lat_s
  118.7 1.9 %collective-permute-start.3 = (bf16[22,7,2,128]{3,2,1,0:T(2,128)(2,1)S(1)}, bf16[22,7,2,128]{3,2,1,0:T(2,128)(2,1)S(1)}, u32[]{:S(2)}, u32[]{:S(2)}) collective-permute-start(bf16[22,7,2,128]{3,2,1,0:T(2,128)(2,1)S(1)} %pad_maximum_fusion.4), channel_id=1, source_target_pairs={{1,0},{2,1},{3,2},{5,4},{6,5},{7,6},{9,8},{10,9},{11,10},{13,12},{... | collective-permute-start | bytes 236552 | tf_op jit(solution)/shard_map/ppermute | solution.py:356
  120.6 5.9 %collective-permute-done.3.lat_n = bf16[22,7,2,128]{3,2,1,0:T(2,128)(2,1)S(1)} collective-permute-done((bf16[22,7,2,128]{3,2,1,0:T(2,128)(2,1)S(1)}, bf16[22,7,2,128]{3,2,1,0:T(2,128)(2,1)S(1)}, u32[]{:S(2)}, u32[]{:S(2)}) %collective-permute-start.3) | collective-permute-done | bytes 78880 | tf_op jit(solution)/shard_map/ppermute | solution.py:356
  126.6 0.0 copy-done
  126.6 3.2 %prepare.1 = (f32[400,768]{1,0:T(8,128)S(1)}, bf16[400,768]{1,0:T(8,128)(2,1)S(1)}, f32[400,128]{1,0:T(8,128)S(1)}) custom-call(f32[20,6,16,128]{3,2,1,0:T(8,128)S(1)} %bitcast.34, f32[20,16,128]{2,1,0:T(8,128)S(1)} %get-tuple-element.10.mask, bf16[2,7,16,128]{3,2,1,0:T(8,128)(2,1)S(1)} %get-tuple-element.24.lon_w, ...), custom_call_target="tpu_custom_call" | custom-call | tf_op jit(solution)/shard_map/prepare/pallas_call | solution.py:374
  129.8 0.0 collective-permute-done.10
  129.8 0.0 collective-permute-done.12
  129.8 0.0 collective-permute-done.11
  129.8 0.0 collective-permute-done.13
  129.8 0.0 copy-done.2
  129.9 14.5 %steps.1 = f32[20,6,16,128]{3,2,1,0:T(8,128)} custom-call(s32[1024]{0:T(1024)S(1)} %copy-done.2, bf16[400,768]{1,0:T(8,128)(2,1)S(1)} %get-tuple-element.11.x1, f32[400,768]{1,0:T(8,128)S(1)} %get-tuple-element.12.moved1_any, f32[400,128]{1,0:T(8,128)S(1)} %get-tuple-element.13.mask0, f32[20,16,128]{2,1,0:T(8,128)S(1)} %get-tuple-element.14.mask1, ...), custom_call_target="tpu_custom_call" | custom-call | tf_op jit(solution)/shard_map/steps/pallas_call | solution.py:376
  (7 shorter events, 0.1 us)
Async XLA Ops:
  31.5 7.8 %collective-permute-start.4 = (bf16[16,8,1280]{2,1,0:T(8,128)(2,1)S(1)}, bf16[16,8,1280]{2,1,0:T(8,128)(2,1)S(1)}, u32[]{:S(2)}, u32[]{:S(2)}) collective-permute-start(bf16[16,8,1280]{2,1,0:T(8,128)(2,1)S(1)} %all_gather.3), channel_id=1, source_target_pairs={{0,64},{1,129},{2,66},{3,131},{64,0},{65,193},{66,2},{67,195},{128... | collective-permute-start | bytes 983048 | tf_op jit(solution)/shard_map/ppermute | solution.py:43
  39.4 12.6 %collective-permute-start.7 = (bf16[2,16,8,1280]{3,2,1,0:T(8,128)(2,1)S(1)}, bf16[2,16,8,1280]{3,2,1,0:T(8,128)(2,1)S(1)}, u32[]{:S(2)}, u32[]{:S(2)}) collective-permute-start(bf16[2,16,8,1280]{3,2,1,0:T(8,128)(2,1)S(1)} %get-tuple-element.20), channel_id=1, source_target_pairs={{0,66},{1,385},{2,64},{3,387},{64,2},{65,449},{66,0},{67,451},{128... | collective-permute-start | bytes 1966088 | tf_op jit(solution)/shard_map/ppermute | solution.py:43
  44.1 12.4 %collective-permute-start.5 = (bf16[2,16,8,1280]{3,2,1,0:T(8,128)(2,1)S(1)}, bf16[2,16,8,1280]{3,2,1,0:T(8,128)(2,1)S(1)}, u32[]{:S(2)}, u32[]{:S(2)}) collective-permute-start(bf16[2,16,8,1280]{3,2,1,0:T(8,128)(2,1)S(1)} %get-tuple-element.20), channel_id=1, source_target_pairs={{0,128},{1,65},{2,130},{3,67},{64,192},{65,1},{66,194},{67,3},{128... | collective-permute-start | bytes 1966088 | tf_op jit(solution)/shard_map/ppermute | solution.py:43
  52.0 16.5 %collective-permute-start.8 = (bf16[2,16,8,1280]{3,2,1,0:T(8,128)(2,1)S(1)}, bf16[2,16,8,1280]{3,2,1,0:T(8,128)(2,1)S(1)}, u32[]{:S(2)}, u32[]{:S(2)}) collective-permute-start(bf16[2,16,8,1280]{3,2,1,0:T(8,128)(2,1)S(1)} %collective-permute-done.7), channel_id=1, source_target_pairs={{0,384},{1,67},{2,386},{3,65},{64,448},{65,3},{66,450},{67,1},{128... | collective-permute-start | bytes 1966088 | tf_op jit(solution)/shard_map/ppermute | solution.py:43
  56.6 37.5 %collective-permute-start.6 = (bf16[2,2,16,8,1280]{4,3,2,1,0:T(8,128)(2,1)S(1)}, bf16[2,2,16,8,1280]{4,3,2,1,0:T(8,128)(2,1)}, u32[]{:S(2)}, u32[]{:S(2)}) collective-permute-start(bf16[2,2,16,8,1280]{4,3,2,1,0:T(8,128)(2,1)S(1)} %pad_maximum_fusion), channel_id=1, source_target_pairs={{0,384},{1,67},{2,386},{3,65},{64,448},{65,3},{66,450},{67,1},{128... | collective-permute-start | bytes 3932168 | tf_op jit(solution)/shard_map/ppermute | solution.py:43
  68.5 2.1 %copy-start.1 = (s32[2,16,20]{2,1,0:T(8,128)S(1)}, s32[2,16,20]{2,1,0:T(8,128)}, u32[]{:S(2)}) copy-start(s32[2,16,20]{2,1,0:T(8,128)} %days.1) | copy-start | bytes 7684
  68.7 32.6 %collective-permute-start.9 = (bf16[2,2,16,8,1280]{4,3,2,1,0:T(8,128)(2,1)S(1)}, bf16[2,2,16,8,1280]{4,3,2,1,0:T(8,128)(2,1)}, u32[]{:S(2)}, u32[]{:S(2)}) collective-permute-start(bf16[2,2,16,8,1280]{4,3,2,1,0:T(8,128)(2,1)S(1)} %pad_maximum_fusion.1), channel_id=1, source_target_pairs={{0,128},{1,65},{2,130},{3,67},{64,192},{65,1},{66,194},{67,3},{128... | collective-permute-start | bytes 3932168 | tf_op jit(solution)/shard_map/ppermute | solution.py:43
  70.6 55.9 %copy-start = (f32[16,20,6,128]{3,0,2,1:T(8,128)S(1)}, f32[16,20,6,128]{3,0,2,1:T(8,128)}, u32[]{:S(2)}) copy-start(f32[16,20,6,128]{3,0,2,1:T(8,128)} %param.6) | copy-start | bytes 2949124
  71.9 57.9 %copy-start.2 = (s32[1024]{0:T(1024)S(1)}, s32[1024]{0:T(1024)}, u32[]{:S(2)}) copy-start(s32[1024]{0:T(1024)} %constant.37.clone.positions) | copy-start | bytes 12292
  71.9 35.6 %collective-permute-start = (bf16[2,7,16,128]{3,2,1,0:T(8,128)(2,1)S(1)}, bf16[2,7,16,128]{3,2,1,0:T(8,128)(2,1)S(1)}, u32[]{:S(2)}, u32[]{:S(2)}) collective-permute-start(bf16[2,7,16,128]{3,2,1,0:T(8,128)(2,1)S(1)} %pad_maximum_fusion.5), channel_id=1, source_target_pairs={{4,8},{8,4},{12,16},{16,12},{20,24},{24,20},{28,32},{32,28},{36,40... | collective-permute-start | bytes 172040 | tf_op jit(solution)/shard_map/ppermute | solution.py:345
  78.4 51.4 %collective-permute-start.10 = (bf16[2,2,16,8,1280]{4,3,2,1,0:T(8,128)(2,1)S(1)}, bf16[2,2,16,8,1280]{4,3,2,1,0:T(8,128)(2,1)S(1)}, u32[]{:S(2)}, u32[]{:S(2)}) collective-permute-start(bf16[2,2,16,8,1280]{4,3,2,1,0:T(8,128)(2,1)S(1)} %pad_maximum_fusion), channel_id=1, source_target_pairs={{0,1},{1,0},{2,3},{3,2},{4,5},{5,4},{6,7},{7,6},{8,9},{9,8},{10,11... | collective-permute-start | bytes 3932168 | tf_op jit(solution)/shard_map/ppermute | solution.py:51
  92.2 37.7 %collective-permute-start.12 = (bf16[2,2,16,8,1280]{4,3,2,1,0:T(8,128)(2,1)S(1)}, bf16[2,2,16,8,1280]{4,3,2,1,0:T(8,128)(2,1)S(1)}, u32[]{:S(2)}, u32[]{:S(2)}) collective-permute-start(bf16[2,2,16,8,1280]{4,3,2,1,0:T(8,128)(2,1)S(1)} %pad_maximum_fusion.1), channel_id=1, source_target_pairs={{0,1},{1,0},{2,3},{3,2},{4,5},{5,4},{6,7},{7,6},{8,9},{9,8},{10,11... | collective-permute-start | bytes 3932168 | tf_op jit(solution)/shard_map/ppermute | solution.py:51
  94.1 35.7 %collective-permute-start.11 = (bf16[2,2,16,8,1280]{4,3,2,1,0:T(8,128)(2,1)}, bf16[2,2,16,8,1280]{4,3,2,1,0:T(8,128)(2,1)S(1)}, u32[]{:S(2)}, u32[]{:S(2)}) collective-permute-start(bf16[2,2,16,8,1280]{4,3,2,1,0:T(8,128)(2,1)} %collective-permute-done.6), channel_id=1, source_target_pairs={{0,1},{1,0},{2,3},{3,2},{4,5},{5,4},{6,7},{7,6},{8,9},{9,8},{10,11... | collective-permute-start | bytes 3932168 | tf_op jit(solution)/shard_map/ppermute | solution.py:51
  101.2 28.6 %collective-permute-start.13 = (bf16[2,2,16,8,1280]{4,3,2,1,0:T(8,128)(2,1)}, bf16[2,2,16,8,1280]{4,3,2,1,0:T(8,128)(2,1)S(1)}, u32[]{:S(2)}, u32[]{:S(2)}) collective-permute-start(bf16[2,2,16,8,1280]{4,3,2,1,0:T(8,128)(2,1)} %collective-permute-done.9), channel_id=1, source_target_pairs={{0,1},{1,0},{2,3},{3,2},{4,5},{5,4},{6,7},{7,6},{8,9},{9,8},{10,11... | collective-permute-start | bytes 3932168 | tf_op jit(solution)/shard_map/ppermute | solution.py:51
  107.5 5.4 %collective-permute-start.1 = (bf16[2,7,16,128]{3,2,1,0:T(8,128)(2,1)S(1)}, bf16[2,7,16,128]{3,2,1,0:T(8,128)(2,1)S(1)}, u32[]{:S(2)}, u32[]{:S(2)}) collective-permute-start(bf16[2,7,16,128]{3,2,1,0:T(8,128)(2,1)S(1)} %pad_maximum_fusion.6), channel_id=1, source_target_pairs={{0,4},{4,0},{8,12},{12,8},{16,20},{20,16},{24,28},{28,24},{32,36},... | collective-permute-start | bytes 172040 | tf_op jit(solution)/shard_map/ppermute | solution.py:345
  113.0 5.7 %collective-permute-start.2 = (bf16[22,7,2,128]{3,2,1,0:T(2,128)(2,1)S(1)}, bf16[22,7,2,128]{3,2,1,0:T(2,128)(2,1)S(1)}, u32[]{:S(2)}, u32[]{:S(2)}) collective-permute-start(bf16[22,7,2,128]{3,2,1,0:T(2,128)(2,1)S(1)} %pad_maximum_fusion.3), channel_id=1, source_target_pairs={{0,1},{1,2},{2,3},{4,5},{5,6},{6,7},{8,9},{9,10},{10,11},{12,13},{... | collective-permute-start | bytes 236552 | tf_op jit(solution)/shard_map/ppermute | solution.py:355
  118.7 7.9 %collective-permute-start.3 = (bf16[22,7,2,128]{3,2,1,0:T(2,128)(2,1)S(1)}, bf16[22,7,2,128]{3,2,1,0:T(2,128)(2,1)S(1)}, u32[]{:S(2)}, u32[]{:S(2)}) collective-permute-start(bf16[22,7,2,128]{3,2,1,0:T(2,128)(2,1)S(1)} %pad_maximum_fusion.4), channel_id=1, source_target_pairs={{1,0},{2,1},{3,2},{5,4},{6,5},{7,6},{9,8},{10,9},{11,10},{13,12},{... | collective-permute-start | bytes 236552 | tf_op jit(solution)/shard_map/ppermute | solution.py:356

commit v8 on v7

--- a/solution.py
+++ b/solution.py
@@ -167,60 +167,67 @@
     return (half + half * jnp.tanh(half)).astype(jnp.bfloat16)
 
 
-def networks(core, x, mask_ref, weights, h1, h2, out, rows, arrive):
-    def net(n, initial):
-        if arrive:
-            arrive(n, 0)
-        want = (1 - n).astype(jnp.float32)
-        for t in range(HID // TILE):
-            w = weights[n, t * TILE : (t + 1) * TILE, 0:IN]
-            d = lax.dot_general(x[...], w, (((1,), (1,)), ((), ())), preferred_element_type=jnp.float32)
-            h1[0:rows, t * TILE : (t + 1) * TILE] = silu(d)
-        if arrive:
-            arrive(n, 1)
-        for t in range(HID // TILE):
-            w = weights[n, :, IN + t * TILE : IN + (t + 1) * TILE]
-            d = jnp.dot(h1[0:rows, :], w, preferred_element_type=jnp.float32)
-            h2[0:rows, t * TILE : (t + 1) * TILE] = silu(d)
-        pick = mask_ref[...].reshape(rows, L) == want
-        pick = jnp.concatenate([pick, pick], axis=1)
-        for t in range(IN // TILE):
-            cols = slice(t * TILE, (t + 1) * TILE)
-            w = weights[n, :, IN + HID + t * TILE : IN + HID + (t + 1) * TILE]
-            d = jnp.dot(h2[0:rows, :], w, preferred_element_type=jnp.float32)
-            out[0:rows, cols] = jnp.where(pick, d, 0.0 if initial else out[0:rows, cols])
-
-    net(core, True)
-    net(1 - core, False)
-
-
-def step_kernel(positions, x1, moved1_any, mask0, mask1, *rest):
-    pieces = rest[:8]
-    result = rest[8]
-    weights, h1, h2, out, ext, x2, moved2, moved1, sems, moved_sem = rest[9:]
-    at = lax.axis_index("y") * 8 + lax.axis_index("xl") * 4 + lax.axis_index("xh") * 2 + lax.axis_index("core")
-    core = lax.axis_index("core")
-    base = at * 32
-    lat = lax.axis_index("xh") * 2 + lax.axis_index("core")
-    for k in range(8):
+def network(n, x, mask_ref, weights, h1, h2, out, before, rows, arrive):
+    want = (1 - n).astype(jnp.float32)
+    arrive(0)
+    for t in range(HID // TILE):
+        w = weights[t * TILE : (t + 1) * TILE, 0:IN]
+        d = lax.dot_general(x[...], w, (((1,), (1,)), ((), ())), preferred_element_type=jnp.float32)
+        h1[0:rows, t * TILE : (t + 1) * TILE] = silu(d)
+    arrive(1)
+    for t in range(HID // TILE):
+        w = weights[:, IN + t * TILE : IN + (t + 1) * TILE]
+        d = jnp.dot(h1[0:rows, :], w, preferred_element_type=jnp.float32)
+        h2[0:rows, t * TILE : (t + 1) * TILE] = silu(d)
+    pick = mask_ref[...].reshape(rows, L) == want
+    pick = jnp.concatenate([pick, pick], axis=1)
+    for t in range(IN // TILE):
+        cols = slice(t * TILE, (t + 1) * TILE)
+        w = weights[:, IN + HID + t * TILE : IN + HID + (t + 1) * TILE]
+        d = jnp.dot(h2[0:rows, :], w, preferred_element_type=jnp.float32)
+        out[0:rows, cols] = jnp.where(pick, d, 0.0 if before is None else before[0:rows, cols])
+
+
+def here():
+    xl, xh, core = (lax.axis_index(a) for a in ("xl", "xh", "core"))
+    return (lax.axis_index("y") * 8 + xl * 4 + xh * 2 + core) * 32, core, xh * 2 + core
+
+
+def place(positions, base, pieces, weights, sems):
+    for k in range(4):
         for slot in range(4):
-            code = positions[base + k * 4 + slot]
+            code = positions[base + k * 4 + slot] % 16
             row = pl.multiple_of((code % 8) * BLOCK, BLOCK)
-            col = pl.multiple_of(((code // 8) % 2) * HALF, 128)
+            col = pl.multiple_of((code // 8) * HALF, 128)
             src = pieces[k].at[pl.ds(slot * BLOCK, BLOCK), :]
-            dst = weights.at[code // 16, pl.ds(row, BLOCK), pl.ds(col, HALF)]
+            dst = weights.at[pl.ds(row, BLOCK), pl.ds(col, HALF)]
             pltpu.make_async_copy(src, dst, sems.at[code]).start()
 
+    def arrive(half):
+        for k in range(8):
+            src = pieces[0].at[pl.ds(0, BLOCK), :]
+            dst = weights.at[pl.ds(k * BLOCK, BLOCK), pl.ds(half * HALF, HALF)]
+            pltpu.make_async_copy(src, dst, sems.at[half * 8 + k]).wait()
+
+    return arrive
+
+
+def own_kernel(positions, x1, mask0, a6, a7, b6, b7, out, own, h1, h2, sems):
+    base, core, _ = here()
+    arrive = place(positions, base, (a6, a7, b6, b7), own, sems)
+    network(core, x1, mask0, own, h1, h2, out, None, ROWS, arrive)
+
+
+def step_kernel(positions, x1, moved1_any, mask0, mask1, out1, own, *rest):
+    pieces = rest[:4]
+    result = rest[4]
+    other, h1, h2, out, ext, x2, moved2, moved1, sems, moved_sem = rest[5:]
+    base, core, lat = here()
+    arrive = place(positions, base + 16, pieces, other, sems)
     arrived = pltpu.make_async_copy(moved1_any, moved1, moved_sem)
     arrived.start()
 
-    def arrive(net, half):
-        for k in range(8):
-            src = pieces[0].at[pl.ds(0, BLOCK), :]
-            dst = weights.at[net, pl.ds(k * BLOCK, BLOCK), pl.ds(half * HALF, HALF)]
-            pltpu.make_async_copy(src, dst, sems.at[(net * 2 + half) * 8 + k]).wait()
-
-    networks(core, x1, mask0, weights, h1, h2, out, ROWS, arrive)
+    network(1 - core, x1, mask0, other, h1, h2, out, out1, ROWS, arrive)
     arrived.wait()
 
     def spread(c, carry):
@@ -249,7 +256,9 @@
         return carry
 
     lax.fori_loop(0, C, second, 0, unroll=5)
-    networks(core, x2, mask1, weights, h1, h2, out, C * R, None)
+    ready = lambda half: None
+    network(core, x2, mask1, own, h1, h2, out, None, C * R, ready)
+    network(1 - core, x2, mask1, other, h1, h2, out, out, C * R, ready)
 
     def finish(c, carry):
         row = pl.multiple_of(c * R, R)
@@ -285,18 +294,37 @@
     return [pl.BlockSpec(memory_space=pltpu.VMEM)] * n
 
 
+SMEM_SPEC = [pl.BlockSpec(memory_space=pltpu.SMEM)]
+ANY_SPEC = [pl.BlockSpec(memory_space=pl.ANY)]
+
+
+def own_call():
+    return pl.pallas_call(
+        own_kernel,
+        out_shape=(
+            jax.ShapeDtypeStruct((ROWS, IN), jnp.float32),
+            jax.ShapeDtypeStruct((HID, 2 * HALF), jnp.bfloat16),
+        ),
+        in_specs=SMEM_SPEC + vmem(2) + ANY_SPEC * 4,
+        out_specs=vmem(2),
+        scratch_shapes=[
+            pltpu.VMEM((ROWS, HID), jnp.bfloat16),
+            pltpu.VMEM((ROWS, HID), jnp.bfloat16),
+            pltpu.SemaphoreType.DMA((16,)),
+        ],
+        compiler_params=pltpu.CompilerParams(vmem_limit_bytes=14 << 20),
+        name="own",
+    )
+
+
 def steps_call():
     return pl.pallas_call(
         step_kernel,
         out_shape=jax.ShapeDtypeStruct((C, F, R, L), jnp.float32),
-        in_specs=[pl.BlockSpec(memory_space=pltpu.SMEM)]
-        + vmem(1)
-        + [pl.BlockSpec(memory_space=pl.ANY)]
-        + vmem(2)
-        + [pl.BlockSpec(memory_space=pl.ANY)] * 8,
+        in_specs=SMEM_SPEC + vmem(1) + ANY_SPEC + vmem(4) + ANY_SPEC * 4,
         out_specs=pl.BlockSpec(memory_space=pltpu.VMEM),
         scratch_shapes=[
-            pltpu.VMEM((2, HID, 2 * HALF), jnp.bfloat16),
+            pltpu.VMEM((HID, 2 * HALF), jnp.bfloat16),
             pltpu.VMEM((ROWS, HID), jnp.bfloat16),
             pltpu.VMEM((ROWS, HID), jnp.bfloat16),
             pltpu.VMEM((ROWS, IN), jnp.float32),
@@ -304,7 +332,7 @@
             pltpu.VMEM((C * R, IN), jnp.bfloat16),
             pltpu.VMEM((C * R, IN), jnp.float32),
             pltpu.VMEM((ROWS, IN), jnp.float32),
-            pltpu.SemaphoreType.DMA((32,)),
+            pltpu.SemaphoreType.DMA((16,)),
             pltpu.SemaphoreType.DMA,
         ],
         compiler_params=pltpu.CompilerParams(vmem_limit_bytes=26 << 20),
@@ -373,7 +401,9 @@
     )
     moved1, x1, mask0 = prepare(ft, masks[0], lon_w, lon_e, lat_s, lat_n)
 
-    result = steps_call()(position_table().reshape(-1), x1, moved1, mask0, masks[1], *pieces)
+    positions = position_table().reshape(-1)
+    out1, own = own_call()(positions, x1, mask0, *pieces[:4])
+    result = steps_call()(positions, x1, moved1, mask0, masks[1], out1, own, *pieces[4:])
     return result.transpose(2, 0, 1, 3)
 
 

time: 145 us -> 150 us (1.034)
  waiting for transfers between devices: 28.4 us -> 32.5 us
  Pallas kernels: 18 us -> 19.5 us
    ppermute x2, starting transfers between devices: 8.36 us -> 3.84 us  [lon_swap(): return lax.ppermute(cols, LON, pairs)]
    ppermute x2, waiting for transfers between devices: 3.4 us -> 7.62 us  [lon_swap(): return lax.ppermute(cols, LON, pairs)]
    ppermute x4, starting transfers between devices: 27.8 us -> 31.7 us  [core_swap(): return lax.ppermute(a, 'core', [(0, 1), (1, 0)])]
    pallas_call x1 -> x2, Pallas kernels: 14.5 us -> 16.1 us  [the longest x1 10.5 us: shards(): steps_call()(positions, x1, moved1, mask0, masks[1], out1, own, *pieces[4:])]
  transfers between devices with their start and end apart: 14 -> 14, of which waited for: 6 -> 6; matrix products, arithmetic and copies ran while one was open for 2% -> 2% of each run, Pallas kernels for 2% -> 6%
where the time goes in v8:
time: 150 us
  starting transfers between devices  62.7 us (42%)
  waiting for transfers between devices  32.5 us (22%)
  blocking collectives  30.8 us (21%)
  Pallas kernels  19.5 us (13%)
  local copies, waits for them, and re-layouts  2.37 us (2%)
    ppermute x4, starting transfers between devices, core_swap(): return lax.ppermute(a, 'core', [(0, 1), (1, 0)])  31.7 us
    all_gather x1, blocking collectives, gather_weights(): z = lax.all_gather(block, 'z', axis=0)  30.8 us
    ppermute x6, starting transfers between devices, exchange(): return lax.ppermute(a, ('y', 'xl', 'xh', 'core'), pairs)  20.9 us
    ppermute x6, waiting for transfers between devices, exchange(): return lax.ppermute(a, ('y', 'xl', 'xh', 'core'), pairs)  17.8 us
    pallas_call x1, Pallas kernels, shards(): steps_call()(positions, x1, moved1, mask0, masks[1], out1, own, *pieces[4:])  10.5 us
    ppermute x2, waiting for transfers between devices, lon_swap(): return lax.ppermute(cols, LON, pairs)  7.62 us
    ppermute x1, waiting for transfers between devices, shards(): lat_n = lax.ppermute(wide(slice(0, 2)), LAT, [(i + 1, i) for i in ends])  5.77 us
    pallas_call x1, Pallas kernels, shards(): out1, own = own_call()(positions, x1, mask0, *pieces[:4])  5.56 us
  transfers between devices with their start and end apart: 14, of which 6 were waited for; matrix products, arithmetic and copies ran while one was open for 2% of the time, Pallas kernels for 6%

profile of v8, /device:TPU:1, one launch (start us, length us, event | category | flops | bytes accessed | tf_op | source)
XLA Modules:
  0.0 149.7 jit_solution(2523264220771683144)
XLA Ops:
  0.0 0.7 fusion.3
  0.7 30.8 %all_gather.3 = bf16[16,8,1280]{2,1,0:T(8,128)(2,1)S(1)} all-gather(bf16[1,8,1280]{2,1,0:T(8,128)(2,1)S(1)} %fusion.3), channel_id=1, replica_groups=mesh['y'=4,'xl'=2,'z'=16,'xh'=2,'core'=2] {'z'}, dimensions={0}, use_global_device_ids=true | all-gather | bytes 348160 | tf_op jit(solution)/shard_map/all_gather | solution.py:55
  31.5 3.2 %collective-permute-start.4 = (bf16[16,8,1280]{2,1,0:T(8,128)(2,1)S(1)}, bf16[16,8,1280]{2,1,0:T(8,128)(2,1)S(1)}, u32[]{:S(2)}, u32[]{:S(2)}) collective-permute-start(bf16[16,8,1280]{2,1,0:T(8,128)(2,1)S(1)} %all_gather.3), channel_id=1, source_target_pairs={{0,64},{1,129},{2,66},{3,131},{64,0},{65,193},{66,2},{67,195},{128... | collective-permute-start | bytes 983048 | tf_op jit(solution)/shard_map/ppermute | solution.py:43
  34.7 4.6 %collective-permute-done.4 = bf16[16,8,1280]{2,1,0:T(8,128)(2,1)S(1)} collective-permute-done((bf16[16,8,1280]{2,1,0:T(8,128)(2,1)S(1)}, bf16[16,8,1280]{2,1,0:T(8,128)(2,1)S(1)}, u32[]{:S(2)}, u32[]{:S(2)}) %collective-permute-start.4) | collective-permute-done | bytes 327712 | tf_op jit(solution)/shard_map/ppermute | solution.py:43
  39.3 0.1 fusion.6
  39.4 4.6 %collective-permute-start.7 = (bf16[2,16,8,1280]{3,2,1,0:T(8,128)(2,1)S(1)}, bf16[2,16,8,1280]{3,2,1,0:T(8,128)(2,1)S(1)}, u32[]{:S(2)}, u32[]{:S(2)}) collective-permute-start(bf16[2,16,8,1280]{3,2,1,0:T(8,128)(2,1)S(1)} %get-tuple-element.24), channel_id=1, source_target_pairs={{0,66},{1,385},{2,64},{3,387},{64,2},{65,449},{66,0},{67,451},{128... | collective-permute-start | bytes 1966088 | tf_op jit(solution)/shard_map/ppermute | solution.py:43
  44.1 3.1 %collective-permute-start.5 = (bf16[2,16,8,1280]{3,2,1,0:T(8,128)(2,1)S(1)}, bf16[2,16,8,1280]{3,2,1,0:T(8,128)(2,1)S(1)}, u32[]{:S(2)}, u32[]{:S(2)}) collective-permute-start(bf16[2,16,8,1280]{3,2,1,0:T(8,128)(2,1)S(1)} %get-tuple-element.24), channel_id=1, source_target_pairs={{0,128},{1,65},{2,130},{3,67},{64,192},{65,1},{66,194},{67,3},{128... | collective-permute-start | bytes 1966088 | tf_op jit(solution)/shard_map/ppermute | solution.py:43
  47.2 4.8 %collective-permute-done.7 = bf16[2,16,8,1280]{3,2,1,0:T(8,128)(2,1)S(1)} collective-permute-done((bf16[2,16,8,1280]{3,2,1,0:T(8,128)(2,1)S(1)}, bf16[2,16,8,1280]{3,2,1,0:T(8,128)(2,1)S(1)}, u32[]{:S(2)}, u32[]{:S(2)}) %collective-permute-start.7) | collective-permute-done | bytes 655392 | tf_op jit(solution)/shard_map/ppermute | solution.py:43
  52.0 4.4 %collective-permute-start.8 = (bf16[2,16,8,1280]{3,2,1,0:T(8,128)(2,1)S(1)}, bf16[2,16,8,1280]{3,2,1,0:T(8,128)(2,1)S(1)}, u32[]{:S(2)}, u32[]{:S(2)}) collective-permute-start(bf16[2,16,8,1280]{3,2,1,0:T(8,128)(2,1)S(1)} %collective-permute-done.7), channel_id=1, source_target_pairs={{0,384},{1,67},{2,386},{3,65},{64,448},{65,3},{66,450},{67,1},{128... | collective-permute-start | bytes 1966088 | tf_op jit(solution)/shard_map/ppermute | solution.py:43
  56.4 0.0 collective-permute-done.5
  56.4 0.1 pad_maximum_fusion
  56.6 3.7 %collective-permute-start.6 = (bf16[2,2,16,8,1280]{4,3,2,1,0:T(8,128)(2,1)S(1)}, bf16[2,2,16,8,1280]{4,3,2,1,0:T(8,128)(2,1)}, u32[]{:S(2)}, u32[]{:S(2)}) collective-permute-start(bf16[2,2,16,8,1280]{4,3,2,1,0:T(8,128)(2,1)S(1)} %pad_maximum_fusion), channel_id=1, source_target_pairs={{0,384},{1,67},{2,386},{3,65},{64,448},{65,3},{66,450},{67,1},{128... | collective-permute-start | bytes 3932168 | tf_op jit(solution)/shard_map/ppermute | solution.py:43
  60.2 8.3 %collective-permute-done.8 = bf16[2,16,8,1280]{3,2,1,0:T(8,128)(2,1)S(1)} collective-permute-done((bf16[2,16,8,1280]{3,2,1,0:T(8,128)(2,1)S(1)}, bf16[2,16,8,1280]{3,2,1,0:T(8,128)(2,1)S(1)}, u32[]{:S(2)}, u32[]{:S(2)}) %collective-permute-start.8) | collective-permute-done | bytes 655392 | tf_op jit(solution)/shard_map/ppermute | solution.py:43
  68.5 0.0 copy-start.1
  68.6 0.1 pad_maximum_fusion.1
  68.7 1.9 %collective-permute-start.9 = (bf16[2,2,16,8,1280]{4,3,2,1,0:T(8,128)(2,1)S(1)}, bf16[2,2,16,8,1280]{4,3,2,1,0:T(8,128)(2,1)}, u32[]{:S(2)}, u32[]{:S(2)}) collective-permute-start(bf16[2,2,16,8,1280]{4,3,2,1,0:T(8,128)(2,1)S(1)} %pad_maximum_fusion.1), channel_id=1, source_target_pairs={{0,128},{1,65},{2,130},{3,67},{64,192},{65,1},{66,194},{67,3},{128... | collective-permute-start | bytes 3932168 | tf_op jit(solution)/shard_map/ppermute | solution.py:43
  70.6 0.0 copy-done.1
  70.6 0.0 copy-start
  70.6 0.2 masks.1
  70.9 1.0 fusion.1
  71.9 0.0 copy-start.2
  71.9 1.9 %collective-permute-start.1 = (bf16[2,7,16,128]{3,2,1,0:T(8,128)(2,1)S(1)}, bf16[2,7,16,128]{3,2,1,0:T(8,128)(2,1)S(1)}, u32[]{:S(2)}, u32[]{:S(2)}) collective-permute-start(bf16[2,7,16,128]{3,2,1,0:T(8,128)(2,1)S(1)} %pad_maximum_fusion.6), channel_id=1, source_target_pairs={{0,4},{4,0},{8,12},{12,8},{16,20},{20,16},{24,28},{28,24},{32,36},... | collective-permute-start | bytes 172040 | tf_op jit(solution)/shard_map/ppermute | solution.py:373
  73.9 18.1 %collective-permute-start.10 = (bf16[2,2,16,8,1280]{4,3,2,1,0:T(8,128)(2,1)S(1)}, bf16[2,2,16,8,1280]{4,3,2,1,0:T(8,128)(2,1)S(1)}, u32[]{:S(2)}, u32[]{:S(2)}) collective-permute-start(bf16[2,2,16,8,1280]{4,3,2,1,0:T(8,128)(2,1)S(1)} %pad_maximum_fusion), channel_id=1, source_target_pairs={{0,1},{1,0},{2,3},{3,2},{4,5},{5,4},{6,7},{7,6},{8,9},{9,8},{10,11... | collective-permute-start | bytes 3932168 | tf_op jit(solution)/shard_map/ppermute | solution.py:51
  92.0 1.9 %collective-permute-start.12 = (bf16[2,2,16,8,1280]{4,3,2,1,0:T(8,128)(2,1)S(1)}, bf16[2,2,16,8,1280]{4,3,2,1,0:T(8,128)(2,1)S(1)}, u32[]{:S(2)}, u32[]{:S(2)}) collective-permute-start(bf16[2,2,16,8,1280]{4,3,2,1,0:T(8,128)(2,1)S(1)} %pad_maximum_fusion.1), channel_id=1, source_target_pairs={{0,1},{1,0},{2,3},{3,2},{4,5},{5,4},{6,7},{7,6},{8,9},{9,8},{10,11... | collective-permute-start | bytes 3932168 | tf_op jit(solution)/shard_map/ppermute | solution.py:51
  93.9 0.0 collective-permute-done.6
  93.9 6.1 %collective-permute-start.11 = (bf16[2,2,16,8,1280]{4,3,2,1,0:T(8,128)(2,1)}, bf16[2,2,16,8,1280]{4,3,2,1,0:T(8,128)(2,1)S(1)}, u32[]{:S(2)}, u32[]{:S(2)}) collective-permute-start(bf16[2,2,16,8,1280]{4,3,2,1,0:T(8,128)(2,1)} %collective-permute-done.6), channel_id=1, source_target_pairs={{0,1},{1,0},{2,3},{3,2},{4,5},{5,4},{6,7},{7,6},{8,9},{9,8},{10,11... | collective-permute-start | bytes 3932168 | tf_op jit(solution)/shard_map/ppermute | solution.py:51
  100.0 0.0 collective-permute-done.9
  100.0 5.6 %collective-permute-start.13 = (bf16[2,2,16,8,1280]{4,3,2,1,0:T(8,128)(2,1)}, bf16[2,2,16,8,1280]{4,3,2,1,0:T(8,128)(2,1)S(1)}, u32[]{:S(2)}, u32[]{:S(2)}) collective-permute-start(bf16[2,2,16,8,1280]{4,3,2,1,0:T(8,128)(2,1)} %collective-permute-done.9), channel_id=1, source_target_pairs={{0,1},{1,0},{2,3},{3,2},{4,5},{5,4},{6,7},{7,6},{8,9},{9,8},{10,11... | collective-permute-start | bytes 3932168 | tf_op jit(solution)/shard_map/ppermute | solution.py:51
  105.6 1.3 fusion.7
  106.9 0.0 collective-permute-done.1
  106.9 1.9 %collective-permute-start = (bf16[2,7,16,128]{3,2,1,0:T(8,128)(2,1)S(1)}, bf16[2,7,16,128]{3,2,1,0:T(8,128)(2,1)S(1)}, u32[]{:S(2)}, u32[]{:S(2)}) collective-permute-start(bf16[2,7,16,128]{3,2,1,0:T(8,128)(2,1)S(1)} %pad_maximum_fusion.5), channel_id=1, source_target_pairs={{4,8},{8,4},{12,16},{16,12},{20,24},{24,20},{28,32},{32,28},{36,40... | collective-permute-start | bytes 172040 | tf_op jit(solution)/shard_map/ppermute | solution.py:373
  108.8 7.6 %collective-permute-done = bf16[2,7,16,128]{3,2,1,0:T(8,128)(2,1)S(1)} collective-permute-done((bf16[2,7,16,128]{3,2,1,0:T(8,128)(2,1)S(1)}, bf16[2,7,16,128]{3,2,1,0:T(8,128)(2,1)S(1)}, u32[]{:S(2)}, u32[]{:S(2)}) %collective-permute-start) | collective-permute-done | bytes 57376 | tf_op jit(solution)/shard_map/ppermute | solution.py:373
  116.5 0.1 pad_maximum_fusion.3
  116.6 4.2 %collective-permute-start.2 = (bf16[22,7,2,128]{3,2,1,0:T(2,128)(2,1)S(1)}, bf16[22,7,2,128]{3,2,1,0:T(2,128)(2,1)S(1)}, u32[]{:S(2)}, u32[]{:S(2)}) collective-permute-start(bf16[22,7,2,128]{3,2,1,0:T(2,128)(2,1)S(1)} %pad_maximum_fusion.3), channel_id=1, source_target_pairs={{0,1},{1,2},{2,3},{4,5},{5,6},{6,7},{8,9},{9,10},{10,11},{12,13},{... | collective-permute-start | bytes 236552 | tf_op jit(solution)/shard_map/ppermute | solution.py:383
  120.9 0.1 pad_maximum_fusion.4
  121.0 1.3 collective-permute-done.2.lat_s
  122.3 2.1 %collective-permute-start.3 = (bf16[22,7,2,128]{3,2,1,0:T(2,128)(2,1)S(1)}, bf16[22,7,2,128]{3,2,1,0:T(2,128)(2,1)S(1)}, u32[]{:S(2)}, u32[]{:S(2)}) collective-permute-start(bf16[22,7,2,128]{3,2,1,0:T(2,128)(2,1)S(1)} %pad_maximum_fusion.4), channel_id=1, source_target_pairs={{1,0},{2,1},{3,2},{5,4},{6,5},{7,6},{9,8},{10,9},{11,10},{13,12},{... | collective-permute-start | bytes 236552 | tf_op jit(solution)/shard_map/ppermute | solution.py:384
  124.4 5.8 %collective-permute-done.3.lat_n = bf16[22,7,2,128]{3,2,1,0:T(2,128)(2,1)S(1)} collective-permute-done((bf16[22,7,2,128]{3,2,1,0:T(2,128)(2,1)S(1)}, bf16[22,7,2,128]{3,2,1,0:T(2,128)(2,1)S(1)}, u32[]{:S(2)}, u32[]{:S(2)}) %collective-permute-start.3) | collective-permute-done | bytes 78880 | tf_op jit(solution)/shard_map/ppermute | solution.py:384
  130.2 0.0 copy-done
  130.2 3.2 %prepare.1 = (f32[400,768]{1,0:T(8,128)S(1)}, bf16[400,768]{1,0:T(8,128)(2,1)S(1)}, f32[400,128]{1,0:T(8,128)S(1)}) custom-call(f32[20,6,16,128]{3,2,1,0:T(8,128)S(1)} %bitcast.34, f32[20,16,128]{2,1,0:T(8,128)S(1)} %get-tuple-element.12.mask, bf16[2,7,16,128]{3,2,1,0:T(8,128)(2,1)S(1)} %get-tuple-element.28.lon_w, ...), custom_call_target="tpu_custom_call" | custom-call | tf_op jit(solution)/shard_map/prepare/pallas_call | solution.py:402
  133.4 0.0 copy-done.2
  133.4 5.6 %own.1 = (f32[400,768]{1,0:T(8,128)S(1)}, bf16[1024,2560]{1,0:T(8,128)(2,1)S(1)}) custom-call(s32[1024]{0:T(1024)S(1)} %copy-done.2, bf16[400,768]{1,0:T(8,128)(2,1)S(1)} %get-tuple-element.13.x1, f32[400,128]{1,0:T(8,128)S(1)} %get-tuple-element.15.mask0, bf16[512,1280]{1,0:T(8,128)(2,1)S(1)} %bitcast.31, bf16[512,1280]{1,0:T(8,128)(2,1)} %bitcast.13.a7, ...), custom_call_target="tpu_custom_call" | custom-call | tf_op jit(solution)/shard_map/own/pallas_call | solution.py:405
  139.0 0.0 collective-permute-done.10
  139.0 0.0 collective-permute-done.12
  139.0 0.0 collective-permute-done.11
  139.0 0.0 collective-permute-done.13
  139.0 10.5 %steps.1 = f32[20,6,16,128]{3,2,1,0:T(8,128)} custom-call(s32[1024]{0:T(1024)S(1)} %copy-done.2, bf16[400,768]{1,0:T(8,128)(2,1)S(1)} %get-tuple-element.13.x1, f32[400,768]{1,0:T(8,128)S(1)} %get-tuple-element.14.moved1_any, f32[400,128]{1,0:T(8,128)S(1)} %get-tuple-element.15.mask0, f32[20,16,128]{2,1,0:T(8,128)S(1)} %get-tuple-element.16.mask1, ...), custom_call_target="tpu_custom_call" | custom-call | tf_op jit(solution)/shard_map/steps/pallas_call | solution.py:406
  (7 shorter events, 0.1 us)
Async XLA Ops:
  31.5 7.8 %collective-permute-start.4 = (bf16[16,8,1280]{2,1,0:T(8,128)(2,1)S(1)}, bf16[16,8,1280]{2,1,0:T(8,128)(2,1)S(1)}, u32[]{:S(2)}, u32[]{:S(2)}) collective-permute-start(bf16[16,8,1280]{2,1,0:T(8,128)(2,1)S(1)} %all_gather.3), channel_id=1, source_target_pairs={{0,64},{1,129},{2,66},{3,131},{64,0},{65,193},{66,2},{67,195},{128... | collective-permute-start | bytes 983048 | tf_op jit(solution)/shard_map/ppermute | solution.py:43
  39.4 12.6 %collective-permute-start.7 = (bf16[2,16,8,1280]{3,2,1,0:T(8,128)(2,1)S(1)}, bf16[2,16,8,1280]{3,2,1,0:T(8,128)(2,1)S(1)}, u32[]{:S(2)}, u32[]{:S(2)}) collective-permute-start(bf16[2,16,8,1280]{3,2,1,0:T(8,128)(2,1)S(1)} %get-tuple-element.24), channel_id=1, source_target_pairs={{0,66},{1,385},{2,64},{3,387},{64,2},{65,449},{66,0},{67,451},{128... | collective-permute-start | bytes 1966088 | tf_op jit(solution)/shard_map/ppermute | solution.py:43
  44.1 12.4 %collective-permute-start.5 = (bf16[2,16,8,1280]{3,2,1,0:T(8,128)(2,1)S(1)}, bf16[2,16,8,1280]{3,2,1,0:T(8,128)(2,1)S(1)}, u32[]{:S(2)}, u32[]{:S(2)}) collective-permute-start(bf16[2,16,8,1280]{3,2,1,0:T(8,128)(2,1)S(1)} %get-tuple-element.24), channel_id=1, source_target_pairs={{0,128},{1,65},{2,130},{3,67},{64,192},{65,1},{66,194},{67,3},{128... | collective-permute-start | bytes 1966088 | tf_op jit(solution)/shard_map/ppermute | solution.py:43
  52.0 16.5 %collective-permute-start.8 = (bf16[2,16,8,1280]{3,2,1,0:T(8,128)(2,1)S(1)}, bf16[2,16,8,1280]{3,2,1,0:T(8,128)(2,1)S(1)}, u32[]{:S(2)}, u32[]{:S(2)}) collective-permute-start(bf16[2,16,8,1280]{3,2,1,0:T(8,128)(2,1)S(1)} %collective-permute-done.7), channel_id=1, source_target_pairs={{0,384},{1,67},{2,386},{3,65},{64,448},{65,3},{66,450},{67,1},{128... | collective-permute-start | bytes 1966088 | tf_op jit(solution)/shard_map/ppermute | solution.py:43
  56.6 37.4 %collective-permute-start.6 = (bf16[2,2,16,8,1280]{4,3,2,1,0:T(8,128)(2,1)S(1)}, bf16[2,2,16,8,1280]{4,3,2,1,0:T(8,128)(2,1)}, u32[]{:S(2)}, u32[]{:S(2)}) collective-permute-start(bf16[2,2,16,8,1280]{4,3,2,1,0:T(8,128)(2,1)S(1)} %pad_maximum_fusion), channel_id=1, source_target_pairs={{0,384},{1,67},{2,386},{3,65},{64,448},{65,3},{66,450},{67,1},{128... | collective-permute-start | bytes 3932168 | tf_op jit(solution)/shard_map/ppermute | solution.py:43
  68.5 2.1 %copy-start.1 = (s32[2,16,20]{2,1,0:T(8,128)S(1)}, s32[2,16,20]{2,1,0:T(8,128)}, u32[]{:S(2)}) copy-start(s32[2,16,20]{2,1,0:T(8,128)} %days.1) | copy-start | bytes 7684
  68.7 31.3 %collective-permute-start.9 = (bf16[2,2,16,8,1280]{4,3,2,1,0:T(8,128)(2,1)S(1)}, bf16[2,2,16,8,1280]{4,3,2,1,0:T(8,128)(2,1)}, u32[]{:S(2)}, u32[]{:S(2)}) collective-permute-start(bf16[2,2,16,8,1280]{4,3,2,1,0:T(8,128)(2,1)S(1)} %pad_maximum_fusion.1), channel_id=1, source_target_pairs={{0,128},{1,65},{2,130},{3,67},{64,192},{65,1},{66,194},{67,3},{128... | collective-permute-start | bytes 3932168 | tf_op jit(solution)/shard_map/ppermute | solution.py:43
  70.6 59.5 %copy-start = (f32[16,20,6,128]{3,0,2,1:T(8,128)S(1)}, f32[16,20,6,128]{3,0,2,1:T(8,128)}, u32[]{:S(2)}) copy-start(f32[16,20,6,128]{3,0,2,1:T(8,128)} %param.6) | copy-start | bytes 2949124
  71.9 61.5 %copy-start.2 = (s32[1024]{0:T(1024)S(1)}, s32[1024]{0:T(1024)}, u32[]{:S(2)}) copy-start(s32[1024]{0:T(1024)} %constant.37.clone.positions) | copy-start | bytes 12292
  71.9 35.0 %collective-permute-start.1 = (bf16[2,7,16,128]{3,2,1,0:T(8,128)(2,1)S(1)}, bf16[2,7,16,128]{3,2,1,0:T(8,128)(2,1)S(1)}, u32[]{:S(2)}, u32[]{:S(2)}) collective-permute-start(bf16[2,7,16,128]{3,2,1,0:T(8,128)(2,1)S(1)} %pad_maximum_fusion.6), channel_id=1, source_target_pairs={{0,4},{4,0},{8,12},{12,8},{16,20},{20,16},{24,28},{28,24},{32,36},... | collective-permute-start | bytes 172040 | tf_op jit(solution)/shard_map/ppermute | solution.py:373
  73.9 65.1 %collective-permute-start.10 = (bf16[2,2,16,8,1280]{4,3,2,1,0:T(8,128)(2,1)S(1)}, bf16[2,2,16,8,1280]{4,3,2,1,0:T(8,128)(2,1)S(1)}, u32[]{:S(2)}, u32[]{:S(2)}) collective-permute-start(bf16[2,2,16,8,1280]{4,3,2,1,0:T(8,128)(2,1)S(1)} %pad_maximum_fusion), channel_id=1, source_target_pairs={{0,1},{1,0},{2,3},{3,2},{4,5},{5,4},{6,7},{7,6},{8,9},{9,8},{10,11... | collective-permute-start | bytes 3932168 | tf_op jit(solution)/shard_map/ppermute | solution.py:51
  92.0 47.0 %collective-permute-start.12 = (bf16[2,2,16,8,1280]{4,3,2,1,0:T(8,128)(2,1)S(1)}, bf16[2,2,16,8,1280]{4,3,2,1,0:T(8,128)(2,1)S(1)}, u32[]{:S(2)}, u32[]{:S(2)}) collective-permute-start(bf16[2,2,16,8,1280]{4,3,2,1,0:T(8,128)(2,1)S(1)} %pad_maximum_fusion.1), channel_id=1, source_target_pairs={{0,1},{1,0},{2,3},{3,2},{4,5},{5,4},{6,7},{7,6},{8,9},{9,8},{10,11... | collective-permute-start | bytes 3932168 | tf_op jit(solution)/shard_map/ppermute | solution.py:51
  93.9 45.1 %collective-permute-start.11 = (bf16[2,2,16,8,1280]{4,3,2,1,0:T(8,128)(2,1)}, bf16[2,2,16,8,1280]{4,3,2,1,0:T(8,128)(2,1)S(1)}, u32[]{:S(2)}, u32[]{:S(2)}) collective-permute-start(bf16[2,2,16,8,1280]{4,3,2,1,0:T(8,128)(2,1)} %collective-permute-done.6), channel_id=1, source_target_pairs={{0,1},{1,0},{2,3},{3,2},{4,5},{5,4},{6,7},{7,6},{8,9},{9,8},{10,11... | collective-permute-start | bytes 3932168 | tf_op jit(solution)/shard_map/ppermute | solution.py:51
  100.0 39.0 %collective-permute-start.13 = (bf16[2,2,16,8,1280]{4,3,2,1,0:T(8,128)(2,1)}, bf16[2,2,16,8,1280]{4,3,2,1,0:T(8,128)(2,1)S(1)}, u32[]{:S(2)}, u32[]{:S(2)}) collective-permute-start(bf16[2,2,16,8,1280]{4,3,2,1,0:T(8,128)(2,1)} %collective-permute-done.9), channel_id=1, source_target_pairs={{0,1},{1,0},{2,3},{3,2},{4,5},{5,4},{6,7},{7,6},{8,9},{9,8},{10,11... | collective-permute-start | bytes 3932168 | tf_op jit(solution)/shard_map/ppermute | solution.py:51
  106.9 9.6 %collective-permute-start = (bf16[2,7,16,128]{3,2,1,0:T(8,128)(2,1)S(1)}, bf16[2,7,16,128]{3,2,1,0:T(8,128)(2,1)S(1)}, u32[]{:S(2)}, u32[]{:S(2)}) collective-permute-start(bf16[2,7,16,128]{3,2,1,0:T(8,128)(2,1)S(1)} %pad_maximum_fusion.5), channel_id=1, source_target_pairs={{4,8},{8,4},{12,16},{16,12},{20,24},{24,20},{28,32},{32,28},{36,40... | collective-permute-start | bytes 172040 | tf_op jit(solution)/shard_map/ppermute | solution.py:373
  116.6 5.7 %collective-permute-start.2 = (bf16[22,7,2,128]{3,2,1,0:T(2,128)(2,1)S(1)}, bf16[22,7,2,128]{3,2,1,0:T(2,128)(2,1)S(1)}, u32[]{:S(2)}, u32[]{:S(2)}) collective-permute-start(bf16[22,7,2,128]{3,2,1,0:T(2,128)(2,1)S(1)} %pad_maximum_fusion.3), channel_id=1, source_target_pairs={{0,1},{1,2},{2,3},{4,5},{5,6},{6,7},{8,9},{9,10},{10,11},{12,13},{... | collective-permute-start | bytes 236552 | tf_op jit(solution)/shard_map/ppermute | solution.py:383
  122.3 7.9 %collective-permute-start.3 = (bf16[22,7,2,128]{3,2,1,0:T(2,128)(2,1)S(1)}, bf16[22,7,2,128]{3,2,1,0:T(2,128)(2,1)S(1)}, u32[]{:S(2)}, u32[]{:S(2)}) collective-permute-start(bf16[22,7,2,128]{3,2,1,0:T(2,128)(2,1)S(1)} %pad_maximum_fusion.4), channel_id=1, source_target_pairs={{1,0},{2,1},{3,2},{5,4},{6,5},{7,6},{9,8},{10,9},{11,10},{13,12},{... | collective-permute-start | bytes 236552 | tf_op jit(solution)/shard_map/ppermute | solution.py:384
